TPU v7x, 256 devices: a whole 4x4x8 slice. The times are simulated.
256 devices in a mesh: lev: 4 (over z_hi), gx: 16 (over x, y), gy: 4 (over z_lo, core).
Axes of the slice: x: 4, y: 4, z: 8 (z_hi: 4, z_lo: 2; z = z_hi * 2 + z_lo), core: 2. Of those that a mesh axis runs over, the one named last changes fastest.
Arguments:
- increment: float32 [2, 64, 1024, 512], P(None, 'lev', 'gx', 'gy'), may hold values from -6 to 6
- norm_gain: float32 [2, 64, 1024, 512], P(None, 'lev', 'gx', 'gy'), may hold values from 0.5 to 2
- diffusion_i: float32 [64, 1024, 512], P('lev', 'gx', 'gy'), may hold values from 0.1 to 0.24
- diffusion_j: float32 [64, 1024, 512], P('lev', 'gx', 'gy'), may hold values from 0.1 to 0.24
- sea_mask: int32 [64, 1024, 512], P('lev', 'gx', 'gy'), may hold values from 0 to 1, as said below
- coupling: float32 [128, 128], replicated, may hold values from -0.5 to 0.5
Outputs:
- correlated: float32 [2, 64, 1024, 512], P(None, 'lev', 'gx', 'gy')
Inputs may be any that keep to these rules, and one draw needn't show every extreme that they name: `sea_mask`: in every column the sea cells are the levels from the top down to some depth, which may be zero.
All inputs are finite; a program needn't handle non-finite values.
Results may differ from a plain program's by a relative error of at most 0.00009.
Values sent between devices are 32-bit elements; how exact they have to be, the bound alone decides.
A program may use at most 64 MiB of HBM per device.

v0:
```python
import functools

import jax
import jax.numpy as jnp
from jax import lax
from jax.experimental import pallas as pl
from jax.experimental.pallas import tpu as pltpu
from jax.sharding import PartitionSpec as P

ITERS = 2


def circular(x, width):
    fields, levels, rows, cols = x.shape
    gap_rows = 16 - 2 * width
    up = [(i, (i + 1) % lax.axis_size("gx")) for i in range(lax.axis_size("gx"))]
    down = [(j, i) for i, j in up]
    north = lax.ppermute(x[:, :, rows - width:], "gx", up)
    south = lax.ppermute(x[:, :, :width], "gx", down)
    gap = jnp.zeros((fields, levels, gap_rows, cols), x.dtype)
    tall = jnp.concatenate([x, south, gap, north], 2)
    right = [(i, i + 1) for i in range(lax.axis_size("gy") - 1)]
    left = [(j, i) for i, j in right]
    east = lax.ppermute(tall[..., :width], "gy", left)
    west = lax.ppermute(tall[..., cols - width:], "gy", right)
    middle = jnp.zeros((fields, levels, rows + 16, 128 - 2 * width), x.dtype)
    return jnp.concatenate([tall, east, middle, west], 3)


def diffusion_kernel(steps, rows, cols, v_ref, c_ref, o_ref):
    height, span = v_ref.shape[2], v_ref.shape[3]
    along_i = c_ref[0, 0]
    along_j = c_ref[1, 0]
    sea = c_ref[2, 0]
    weight_i = along_i * sea * pltpu.roll(sea, height - 1, 0)
    weight_j = along_j * sea * pltpu.roll(sea, span - 1, 1)
    for f in range(v_ref.shape[0]):
        values = v_ref[f, 0]
        for s in range(steps):
            flux_i = weight_i * (pltpu.roll(values, height - 1, 0) - values)
            flux_j = weight_j * (pltpu.roll(values, span - 1, 1) - values)
            values = values + flux_i - pltpu.roll(flux_i, 1, 0) + flux_j - pltpu.roll(flux_j, 1, 1)
        o_ref[f, 0] = values[:rows, :cols]


def diffusion(values, coefs, steps):
    fields, levels, rows, cols = values.shape
    ext = circular(values, steps)
    height, span = ext.shape[2], ext.shape[3]
    return pl.pallas_call(
        functools.partial(diffusion_kernel, steps, rows, cols),
        out_shape=jax.ShapeDtypeStruct(values.shape, values.dtype),
        grid=(levels,),
        in_specs=[
            pl.BlockSpec((fields, 1, height, span), lambda l: (0, l, 0, 0)),
            pl.BlockSpec((3, 1, height, span), lambda l: (0, l, 0, 0)),
        ],
        out_specs=pl.BlockSpec((fields, 1, rows, cols), lambda l: (0, l, 0, 0)),
    )(ext, coefs)


def to_columns(x):
    return lax.all_to_all(x, "lev", 2, 1, tiled=True)


def to_levels(x):
    return lax.all_to_all(x, "lev", 1, 2, tiled=True)


def level_mix(fields, matrix):
    columns = to_columns(fields)
    mixed = jnp.einsum("abcd,cdij->abij", matrix, columns, precision=lax.Precision.HIGHEST)
    return to_levels(mixed)


def shards(increment, norm_gain, diffusion_i, diffusion_j, sea_mask, coupling):
    steps = 2 * ITERS
    ocean = sea_mask.astype(jnp.float32)
    scaled = ocean[None] * norm_gain * increment
    order_count = coupling.shape[0]
    level_count = order_count // 2
    balance = jnp.eye(order_count, dtype=jnp.float32) + coupling
    forward = balance.reshape(2, level_count, 2, level_count)
    adjoint = jnp.transpose(forward, (2, 3, 0, 1))
    coefs = circular(jnp.stack([diffusion_i, diffusion_j, ocean]), steps)
    adjoint_mixed = level_mix(scaled, adjoint) * ocean[None]
    spread = diffusion(adjoint_mixed, coefs, steps)
    forward_mixed = level_mix(spread, forward)
    return ocean[None] * norm_gain * forward_mixed


def solution(mesh):
    return jax.shard_map(
        shards,
        mesh=mesh,
        in_specs=(
            P(None, "lev", "gx", "gy"),
            P(None, "lev", "gx", "gy"),
            P("lev", "gx", "gy"),
            P("lev", "gx", "gy"),
            P("lev", "gx", "gy"),
            P(),
        ),
        out_specs=P(None, "lev", "gx", "gy"),
        check_vma=False,
    )
```

profile of v0, /device:TPU:1, one launch (start us, length us, event | category | flops | bytes accessed | tf_op | source)
XLA Modules:
  0.0 200.0 jit_solution(10935158225565733551)
XLA Ops:
  0.0 1.2 convert_bitcast_fusion
  1.3 0.1 copy-done.6
  1.4 1.5 multiply_multiply_fusion
  2.9 1.6 copy.14
  4.5 9.0 %all-to-all-start = ((f32[2,16,64,128]{3,1,0,2:T(8,128)}), f32[2,16,64,128]{3,1,0,2:T(8,128)S(1)}, u32[]{:S(2)}, u32[]{:S(2)}) async-start(f32[2,16,64,128]{3,1,0,2:T(8,128)} %copy.14), calls=%async_computation | async-start | bytes 2097152 | tf_op jit(solution)/shard_map/all_to_all | solution.py:63
  13.6 0.1 reshape.4
  13.8 23.4 %all-to-all-done = f32[2,16,64,128]{3,1,0,2:T(8,128)S(1)} async-done(((f32[2,16,64,128]{3,1,0,2:T(8,128)}), f32[2,16,64,128]{3,1,0,2:T(8,128)S(1)}, u32[]{:S(2)}, u32[]{:S(2)}) %all-to-all-start) | async-done | bytes 1048608 | tf_op jit(solution)/shard_map/all_to_all | solution.py:63
  37.2 0.1 copy.15
  37.3 1.1 convolution_bitcast_fusion.1
  38.4 1.6 copy.16
  40.0 5.4 %all-to-all-start.1 = ((f32[2,64,16,128]{3,2,0,1:T(8,128)}), f32[2,64,16,128]{3,2,0,1:T(8,128)}, u32[]{:S(2)}, u32[]{:S(2)}) async-start(f32[2,64,16,128]{3,2,0,1:T(8,128)} %copy.16), calls=%async_computation.1 | async-start | bytes 2097152 | tf_op jit(solution)/shard_map/all_to_all | solution.py:67
  45.5 5.0 %collective-permute-start.4 = (f32[3,16,4,128]{3,2,1,0:T(4,128)S(1)}, f32[3,16,4,128]{3,2,1,0:T(4,128)S(1)}, u32[]{:S(2)}, u32[]{:S(2)}) collective-permute-start(f32[3,16,4,128]{3,2,1,0:T(4,128)S(1)} %get-tuple-element.7), channel_id=1, source_target_pairs={{4,0},{8,4},{12,8},{16,12},{20,16},{24,20},{28,24},{32,28},{36,32}... | collective-permute-start | bytes 294920 | tf_op jit(solution)/shard_map/ppermute | solution.py:19
  50.5 1.6 collective-permute-done.4
  52.2 5.1 %collective-permute-done.5 = f32[3,16,4,128]{3,2,1,0:T(4,128)S(1)} collective-permute-done((f32[3,16,4,128]{3,2,1,0:T(4,128)S(1)}, f32[3,16,4,128]{3,2,1,0:T(4,128)S(1)}, u32[]{:S(2)}, u32[]{:S(2)}) %collective-permute-start.5) | collective-permute-done | bytes 98336 | tf_op jit(solution)/shard_map/ppermute | solution.py:18
  57.4 0.6 copy-done.12
  58.0 0.7 copy-done.8
  58.7 0.2 pad_maximum_fusion.2
  58.9 1.7 all-to-all-done.1
  60.6 1.4 copy.17
  62.0 0.1 bitcast_multiply_fusion.1
  62.1 0.7 fusion.4
  62.8 4.9 %collective-permute-start = (f32[2,16,4,128]{3,2,1,0:T(4,128)}, f32[2,16,4,128]{3,2,1,0:T(4,128)}, u32[]{:S(2)}, u32[]{:S(2)}) collective-permute-start(f32[2,16,4,128]{3,2,1,0:T(4,128)} %get-tuple-element.11), channel_id=1, source_target_pairs={{4,0},{8,4},{12,8},{16,12},{20,16},{24,20},{28,24},{32,28},{36,32}... | collective-permute-start | bytes 196616 | tf_op jit(solution)/shard_map/ppermute | solution.py:19
  67.7 2.5 %fusion.2 = (f32[3,16,80,4]{3,2,1,0:T(8,128)}, f32[3,16,80,4]{3,2,1,0:T(8,128)}) fusion(f32[3,16,80,128]{3,2,1,0:T(8,128)S(1)} %pad_maximum_fusion.2), kind=kLoop, calls=%fused_computation.17 | loop fusion | bytes 245760 | tf_op jit(solution)/shard_map/slice | solution.py:24
  70.2 2.9 %copy.22 = f32[3,16,80,4]{2,1,3,0:T(8,128)} copy(f32[3,16,80,4]{3,2,1,0:T(8,128)} %get-tuple-element.5) | data formatting | bytes 122880 | tf_op jit(solution)/shard_map/slice | solution.py:24
  73.2 9.1 %collective-permute-start.6 = (f32[3,16,80,4]{2,1,3,0:T(8,128)}, f32[3,16,80,4]{2,1,3,0:T(8,128)}, u32[]{:S(2)}, u32[]{:S(2)}) collective-permute-start(f32[3,16,80,4]{2,1,3,0:T(8,128)} %copy.22), channel_id=1, source_target_pairs={{1,0},{2,1},{3,2},{5,4},{6,5},{7,6},{9,8},{10,9},{11,10},{13,12},{... | collective-permute-start | bytes 184328 | tf_op jit(solution)/shard_map/ppermute | solution.py:24
  82.2 1.3 copy.23
  83.5 9.9 %collective-permute-start.7 = (f32[3,16,80,4]{2,1,3,0:T(8,128)}, f32[3,16,80,4]{2,1,3,0:T(8,128)S(1)}, u32[]{:S(2)}, u32[]{:S(2)}) collective-permute-start(f32[3,16,80,4]{2,1,3,0:T(8,128)} %copy.23), channel_id=1, source_target_pairs={{0,1},{1,2},{2,3},{4,5},{5,6},{6,7},{8,9},{9,10},{10,11},{12,13},{... | collective-permute-start | bytes 184328 | tf_op jit(solution)/shard_map/ppermute | solution.py:25
  93.5 2.8 %copy.24 = f32[3,16,80,4]{3,2,1,0:T(8,128)} copy(f32[3,16,80,4]{2,1,3,0:T(8,128)} %collective-permute-done.6) | data formatting | bytes 122880 | tf_op jit(solution)/shard_map/ppermute | solution.py:24
  96.3 2.0 copy.25
  98.2 1.0 pad_maximum_fusion.3
  99.2 1.5 fusion.3
  100.7 2.4 %copy.18 = f32[2,16,80,4]{2,1,3,0:T(8,128)} copy(f32[2,16,80,4]{3,2,1,0:T(8,128)} %get-tuple-element.9) | data formatting | bytes 81920 | tf_op jit(solution)/shard_map/slice | solution.py:24
  103.2 1.1 copy.19
  104.2 3.2 %collective-permute-start.3 = (f32[2,16,80,4]{2,1,3,0:T(8,128)}, f32[2,16,80,4]{2,1,3,0:T(8,128)S(1)}, u32[]{:S(2)}, u32[]{:S(2)}) collective-permute-start(f32[2,16,80,4]{2,1,3,0:T(8,128)} %copy.19), channel_id=1, source_target_pairs={{0,1},{1,2},{2,3},{4,5},{5,6},{6,7},{8,9},{9,10},{10,11},{12,13},{... | collective-permute-start | bytes 122888 | tf_op jit(solution)/shard_map/ppermute | solution.py:25
  107.5 2.1 %collective-permute-start.2 = (f32[2,16,80,4]{2,1,3,0:T(8,128)}, f32[2,16,80,4]{2,1,3,0:T(8,128)S(1)}, u32[]{:S(2)}, u32[]{:S(2)}) collective-permute-start(f32[2,16,80,4]{2,1,3,0:T(8,128)} %copy.18), channel_id=1, source_target_pairs={{1,0},{2,1},{3,2},{5,4},{6,5},{7,6},{9,8},{10,9},{11,10},{13,12},{... | collective-permute-start | bytes 122888 | tf_op jit(solution)/shard_map/ppermute | solution.py:24
  109.6 4.4 %pad_maximum_fusion.c_ref = f32[3,16,80,256]{3,2,1,0:T(8,128)} fusion(f32[3,16,80,4]{3,2,1,0:T(8,128)} %copy.25, f32[3,16,80,4]{3,2,1,0:T(8,128)} %copy.24, f32[3,16,4,128]{3,2,1,0:T(4,128)} %copy-done.12, f32[3,16,8,128]{3,2,1,0:T(8,128)} %copy-done.8, f32[3,16,4,128]{3,2,1,0:T(4,128)} %copy-done.11, f32[1,16,64,128]{3,2,1,0:T(8,128)S(1)} %copy-done.1, ...), kind=kLoop, calls=%fused_computation | loop fusion | flops 7864320 | bytes 6022144 | tf_op jit(solution)/shard_map/concatenate | solution.py:27
  114.0 0.5 copy.20
  114.5 1.5 copy.21
  116.0 3.4 %pad_maximum_fusion.1.v_ref = f32[2,16,80,256]{3,2,1,0:T(8,128)} fusion(f32[2,16,80,4]{3,2,1,0:T(8,128)} %copy.21, f32[2,16,80,4]{3,2,1,0:T(8,128)S(1)} %copy.20, f32[2,16,4,128]{3,2,1,0:T(4,128)} %collective-permute-done.1, f32[2,16,8,128]{3,2,1,0:T(8,128)S(1)} %broadcast_in_dim.17, f32[2,16,4,128]{3,2,1,0:T(4,128)} %collective-permute-done, ...), kind=kLoop, calls=%fused_computation.1 | loop fusion | flops 3932160 | bytes 4015104 | tf_op jit(solution)/shard_map/concatenate | solution.py:27
  119.4 16.0 %shard_map.64 = f32[2,16,64,128]{3,2,1,0:T(8,128)} custom-call(f32[2,16,80,256]{3,2,1,0:T(8,128)} %pad_maximum_fusion.1.v_ref, f32[3,16,80,256]{3,2,1,0:T(8,128)} %pad_maximum_fusion.c_ref), custom_call_target="tpu_custom_call" | custom-call | tf_op jit(solution)/shard_map/pallas_call | solution.py:50
  135.4 1.8 copy.26
  137.3 30.5 %all_to_all.72 = f32[2,16,64,128]{3,1,0,2:T(8,128)S(1)} all-to-all(f32[2,16,64,128]{3,1,0,2:T(8,128)S(1)} %copy.26), channel_id=1, replica_groups=mesh['lev'=4,'gx'=16,'gy'=4] {'lev'}, dimensions={2} | all-to-all | bytes 2097152 | tf_op jit(solution)/shard_map/all_to_all | solution.py:63
  167.8 0.1 copy.27
  168.0 1.1 convolution_bitcast_fusion
  169.0 0.6 copy.29
  169.7 29.0 %all_to_all.73 = f32[2,64,16,128]{3,2,0,1:T(8,128)S(1)} all-to-all(f32[2,64,16,128]{3,2,0,1:T(8,128)S(1)} %copy.29), channel_id=1, replica_groups=mesh['lev'=4,'gx'=16,'gy'=4] {'lev'}, dimensions={1} | all-to-all | bytes 2097152 | tf_op jit(solution)/shard_map/all_to_all | solution.py:67
  198.6 0.1 copy.30
  198.8 1.2 bitcast_multiply_fusion
  (40 shorter events, 0.3 us)
Async XLA Ops:
  0.0 1.4 copy-start.6
  1.3 56.1 %copy-start = (f32[1,16,64,128]{3,2,1,0:T(8,128)}, f32[1,16,64,128]{3,2,1,0:T(8,128)S(1)}, u32[]{:S(2)}) copy-start(f32[1,16,64,128]{3,2,1,0:T(8,128)S(1)} %get-tuple-element.13) | copy-start | bytes 1572868
  2.9 10.6 %copy-start.13 = (f32[128,128]{1,0:T(8,128)S(1)}, f32[128,128]{1,0:T(8,128)}, u32[]{:S(2)}) copy-start(f32[128,128]{1,0:T(8,128)} %param.11) | copy-start | bytes 196612
  4.5 32.7 %all-to-all-start = ((f32[2,16,64,128]{3,1,0,2:T(8,128)}), f32[2,16,64,128]{3,1,0,2:T(8,128)S(1)}, u32[]{:S(2)}, u32[]{:S(2)}) async-start(f32[2,16,64,128]{3,1,0,2:T(8,128)} %copy.14), calls=%async_computation | async-start | bytes 2097152 | tf_op jit(solution)/shard_map/all_to_all | solution.py:63
  13.7 24.7 %copy-start.9 = (f32[2,64,2,64]{3,2,1,0:T(2,128)}, f32[2,64,2,64]{3,2,1,0:T(2,128)S(1)}, u32[]{:S(2)}) copy-start(f32[2,64,2,64]{3,2,1,0:T(2,128)S(1)} %reshape.4) | copy-start | bytes 196612
  38.4 7.1 %copy-start.3 = (f32[16,64,128]{2,1,0:T(8,128)S(1)}, f32[16,64,128]{2,1,0:T(8,128)}, u32[]{:S(2)}) copy-start(f32[16,64,128]{2,1,0:T(8,128)} %param.9) | copy-start | bytes 1572868
  38.4 7.1 %copy-start.4 = (f32[16,64,128]{2,1,0:T(8,128)S(1)}, f32[16,64,128]{2,1,0:T(8,128)}, u32[]{:S(2)}) copy-start(f32[16,64,128]{2,1,0:T(8,128)} %param.8) | copy-start | bytes 1572868
  40.0 20.6 %all-to-all-start.1 = ((f32[2,64,16,128]{3,2,0,1:T(8,128)}), f32[2,64,16,128]{3,2,0,1:T(8,128)}, u32[]{:S(2)}, u32[]{:S(2)}) async-start(f32[2,64,16,128]{3,2,0,1:T(8,128)} %copy.16), calls=%async_computation.1 | async-start | bytes 2097152 | tf_op jit(solution)/shard_map/all_to_all | solution.py:67
  45.5 13.2 %copy-start.5 = (f32[16,64,128]{2,1,0:T(8,128)S(1)}, f32[16,64,128]{2,1,0:T(8,128)}, u32[]{:S(2)}) copy-start(f32[16,64,128]{2,1,0:T(8,128)} %param.8) | copy-start | bytes 1572868
  45.5 6.6 %collective-permute-start.4 = (f32[3,16,4,128]{3,2,1,0:T(4,128)S(1)}, f32[3,16,4,128]{3,2,1,0:T(4,128)S(1)}, u32[]{:S(2)}, u32[]{:S(2)}) collective-permute-start(f32[3,16,4,128]{3,2,1,0:T(4,128)S(1)} %get-tuple-element.7), channel_id=1, source_target_pairs={{4,0},{8,4},{12,8},{16,12},{20,16},{24,20},{28,24},{32,28},{36,32}... | collective-permute-start | bytes 294920 | tf_op jit(solution)/shard_map/ppermute | solution.py:19
  50.5 6.8 %collective-permute-start.5 = (f32[3,16,4,128]{3,2,1,0:T(4,128)S(1)}, f32[3,16,4,128]{3,2,1,0:T(4,128)S(1)}, u32[]{:S(2)}, u32[]{:S(2)}) collective-permute-start(f32[3,16,4,128]{3,2,1,0:T(4,128)S(1)} %get-tuple-element.8), channel_id=1, source_target_pairs={{0,4},{4,8},{8,12},{12,16},{16,20},{20,24},{24,28},{28,32},{32,36}... | collective-permute-start | bytes 294920 | tf_op jit(solution)/shard_map/ppermute | solution.py:18
  52.2 5.2 %copy-start.11 = (f32[3,16,4,128]{3,2,1,0:T(4,128)}, f32[3,16,4,128]{3,2,1,0:T(4,128)S(1)}, u32[]{:S(2)}) copy-start(f32[3,16,4,128]{3,2,1,0:T(4,128)S(1)} %collective-permute-done.4) | copy-start | bytes 294916
  57.3 0.7 copy-start.12
  58.0 0.7 copy-start.8
  62.8 35.4 %collective-permute-start = (f32[2,16,4,128]{3,2,1,0:T(4,128)}, f32[2,16,4,128]{3,2,1,0:T(4,128)}, u32[]{:S(2)}, u32[]{:S(2)}) collective-permute-start(f32[2,16,4,128]{3,2,1,0:T(4,128)} %get-tuple-element.11), channel_id=1, source_target_pairs={{4,0},{8,4},{12,8},{16,12},{20,16},{24,20},{28,24},{32,28},{36,32}... | collective-permute-start | bytes 196616 | tf_op jit(solution)/shard_map/ppermute | solution.py:19
  67.7 30.5 %collective-permute-start.1 = (f32[2,16,4,128]{3,2,1,0:T(4,128)}, f32[2,16,4,128]{3,2,1,0:T(4,128)}, u32[]{:S(2)}, u32[]{:S(2)}) collective-permute-start(f32[2,16,4,128]{3,2,1,0:T(4,128)} %get-tuple-element.12), channel_id=1, source_target_pairs={{0,4},{4,8},{8,12},{12,16},{16,20},{20,24},{24,28},{28,32},{32,36}... | collective-permute-start | bytes 196616 | tf_op jit(solution)/shard_map/ppermute | solution.py:18
  70.2 12.0 %copy-start.2 = (f32[3,16,80,4]{3,2,1,0:T(8,128)S(1)}, f32[3,16,80,4]{3,2,1,0:T(8,128)}, u32[]{:S(2)}) copy-start(f32[3,16,80,4]{3,2,1,0:T(8,128)} %get-tuple-element.6) | copy-start | bytes 184324
  73.2 20.3 %collective-permute-start.6 = (f32[3,16,80,4]{2,1,3,0:T(8,128)}, f32[3,16,80,4]{2,1,3,0:T(8,128)}, u32[]{:S(2)}, u32[]{:S(2)}) collective-permute-start(f32[3,16,80,4]{2,1,3,0:T(8,128)} %copy.22), channel_id=1, source_target_pairs={{1,0},{2,1},{3,2},{5,4},{6,5},{7,6},{9,8},{10,9},{11,10},{13,12},{... | collective-permute-start | bytes 184328 | tf_op jit(solution)/shard_map/ppermute | solution.py:24
  83.5 12.8 %collective-permute-start.7 = (f32[3,16,80,4]{2,1,3,0:T(8,128)}, f32[3,16,80,4]{2,1,3,0:T(8,128)S(1)}, u32[]{:S(2)}, u32[]{:S(2)}) collective-permute-start(f32[3,16,80,4]{2,1,3,0:T(8,128)} %copy.23), channel_id=1, source_target_pairs={{0,1},{1,2},{2,3},{4,5},{5,6},{6,7},{8,9},{9,10},{10,11},{12,13},{... | collective-permute-start | bytes 184328 | tf_op jit(solution)/shard_map/ppermute | solution.py:25
  100.7 8.8 %copy-start.1 = (f32[1,16,64,128]{3,2,1,0:T(8,128)S(1)}, f32[1,16,64,128]{3,2,1,0:T(8,128)}, u32[]{:S(2)}) copy-start(f32[1,16,64,128]{3,2,1,0:T(8,128)} %copy-done) | copy-start | bytes 1572868
  104.2 10.2 %collective-permute-start.3 = (f32[2,16,80,4]{2,1,3,0:T(8,128)}, f32[2,16,80,4]{2,1,3,0:T(8,128)S(1)}, u32[]{:S(2)}, u32[]{:S(2)}) collective-permute-start(f32[2,16,80,4]{2,1,3,0:T(8,128)} %copy.19), channel_id=1, source_target_pairs={{0,1},{1,2},{2,3},{4,5},{5,6},{6,7},{8,9},{9,10},{10,11},{12,13},{... | collective-permute-start | bytes 122888 | tf_op jit(solution)/shard_map/ppermute | solution.py:25
  107.5 6.5 %collective-permute-start.2 = (f32[2,16,80,4]{2,1,3,0:T(8,128)}, f32[2,16,80,4]{2,1,3,0:T(8,128)S(1)}, u32[]{:S(2)}, u32[]{:S(2)}) collective-permute-start(f32[2,16,80,4]{2,1,3,0:T(8,128)} %copy.18), channel_id=1, source_target_pairs={{1,0},{2,1},{3,2},{5,4},{6,5},{7,6},{9,8},{10,9},{11,10},{13,12},{... | collective-permute-start | bytes 122888 | tf_op jit(solution)/shard_map/ppermute | solution.py:24
  137.3 30.7 %copy-start.10 = (f32[2,64,2,64]{3,2,1,0:T(2,128)S(1)}, f32[2,64,2,64]{3,2,1,0:T(2,128)}, u32[]{:S(2)}) copy-start(f32[2,64,2,64]{3,2,1,0:T(2,128)} %copy-done.9) | copy-start | bytes 196612
  169.7 29.1 %copy-start.7 = (f32[2,16,64,128]{3,2,1,0:T(8,128)S(1)}, f32[2,16,64,128]{3,2,1,0:T(8,128)}, u32[]{:S(2)}) copy-start(f32[2,16,64,128]{3,2,1,0:T(8,128)} %param.7) | copy-start | bytes 3145732
where the time goes:
time: 201 us; the launch traced here: 200 us
  blocking collectives  59.5 us (30%)
  starting transfers between devices  48.7 us (24%)
  waiting for transfers between devices  31.9 us (16%)
  local copies, waits for them, and re-layouts  28.2 us (14%)
  Pallas kernels  16 us (8%)
  other arithmetic  13.2 us (7%)
  matrix products  2.11 us (1%)
    all_to_all x1, blocking collectives, to_columns(): return lax.all_to_all(x, 'lev', 2, 1, tiled=True)  30.5 us
    all_to_all x1, blocking collectives, to_levels(): return lax.all_to_all(x, 'lev', 1, 2, tiled=True)  29 us
    all_to_all x1, waiting for transfers between devices, to_columns(): return lax.all_to_all(x, 'lev', 2, 1, tiled=True)  23.4 us
    pallas_call x1, Pallas kernels, diffusion(): pl.pallas_call(functools.partial(diffusion_kernel, steps, rows, cols), ou...  16 us
    ppermute x2, starting transfers between devices, circular(): west = lax.ppermute(tall[..., cols - width:], 'gy', right)  13.1 us
    ppermute x2, starting transfers between devices, circular(): east = lax.ppermute(tall[..., :width], 'gy', left)  11.2 us
    ppermute x2, starting transfers between devices, circular(): south = lax.ppermute(x[:, :, :width], 'gx', down)  9.94 us
    slice x4, local copies, waits for them, and re-layouts, circular(): east = lax.ppermute(tall[..., :width], 'gy', left)  9.37 us
  transfers between devices with their start and end apart: 10, of which 4 were waited for; matrix products, arithmetic and copies ran while one was open for 8% of the time, Pallas kernels for 0%

commit v1 on v0

--- a/solution.py
+++ b/solution.py
@@ -10,19 +10,35 @@
 ITERS = 2
 
 
+def neighbour(piece, dx, dy):
+    nx = lax.axis_size("gx")
+    ny = lax.axis_size("gy")
+    pairs = [
+        (i * ny + j, ((i + dx) % nx) * ny + j + dy)
+        for i in range(nx)
+        for j in range(ny)
+        if 0 <= j + dy < ny
+    ]
+    return lax.ppermute(piece, ("gx", "gy"), pairs)
+
+
 def circular(x, width):
     fields, levels, rows, cols = x.shape
-    gap_rows = 16 - 2 * width
-    up = [(i, (i + 1) % lax.axis_size("gx")) for i in range(lax.axis_size("gx"))]
-    down = [(j, i) for i, j in up]
-    north = lax.ppermute(x[:, :, rows - width:], "gx", up)
-    south = lax.ppermute(x[:, :, :width], "gx", down)
-    gap = jnp.zeros((fields, levels, gap_rows, cols), x.dtype)
+    top, bottom = slice(rows - width, rows), slice(0, width)
+    first, last = slice(0, width), slice(cols - width, cols)
+    north = neighbour(x[:, :, top], 1, 0)
+    south = neighbour(x[:, :, bottom], -1, 0)
+    east = neighbour(x[:, :, :, first], 0, -1)
+    west = neighbour(x[:, :, :, last], 0, 1)
+    north_east = neighbour(x[:, :, top, first], 1, -1)
+    south_east = neighbour(x[:, :, bottom, first], -1, -1)
+    north_west = neighbour(x[:, :, top, last], 1, 1)
+    south_west = neighbour(x[:, :, bottom, last], -1, 1)
+    gap = jnp.zeros((fields, levels, 16 - 2 * width, cols), x.dtype)
     tall = jnp.concatenate([x, south, gap, north], 2)
-    right = [(i, i + 1) for i in range(lax.axis_size("gy") - 1)]
-    left = [(j, i) for i, j in right]
-    east = lax.ppermute(tall[..., :width], "gy", left)
-    west = lax.ppermute(tall[..., cols - width:], "gy", right)
+    gap = jnp.zeros((fields, levels, 16 - 2 * width, width), x.dtype)
+    east = jnp.concatenate([east, south_east, gap, north_east], 2)
+    west = jnp.concatenate([west, south_west, gap, north_west], 2)
     middle = jnp.zeros((fields, levels, rows + 16, 128 - 2 * width), x.dtype)
     return jnp.concatenate([tall, east, middle, west], 3)
 
@@ -83,7 +99,10 @@
     forward = balance.reshape(2, level_count, 2, level_count)
     adjoint = jnp.transpose(forward, (2, 3, 0, 1))
     coefs = circular(jnp.stack([diffusion_i, diffusion_j, ocean]), steps)
-    adjoint_mixed = level_mix(scaled, adjoint) * ocean[None]
+    columns = to_columns(scaled)
+    mixed = jnp.einsum("abcd,cdij->abij", adjoint, columns, precision=lax.Precision.HIGHEST)
+    coefs, mixed = lax.optimization_barrier((coefs, mixed))
+    adjoint_mixed = to_levels(mixed) * ocean[None]
     spread = diffusion(adjoint_mixed, coefs, steps)
     forward_mixed = level_mix(spread, forward)
     return ocean[None] * norm_gain * forward_mixed

time: 201 us -> 220 us (1.095)
  blocking collectives: 59.5 us -> 86.6 us
  waiting for transfers between devices: 31.9 us -> 8.64 us
  starting transfers between devices: 48.7 us -> 62.7 us
  other arithmetic: 13.2 us -> 15.6 us
    all_to_all x1 -> x2, blocking collectives: 29 us -> 59.5 us  [to_levels(): return lax.all_to_all(x, 'lev', 1, 2, tiled=True)]
    all_to_all x1, waiting for transfers between devices: 23.4 us -> 0.01 us  [to_columns(): return lax.all_to_all(x, 'lev', 2, 1, tiled=True)]
    ppermute x8 -> x16, starting transfers between devices: 34.2 us -> 54.5 us  [neighbour(): return lax.ppermute(piece, ('gx', 'gy'), pairs)]
    all_to_all x1 -> x0, starting transfers between devices: 5.45 us -> none  [to_levels(): return lax.all_to_all(x, 'lev', 1, 2, tiled=True)]
    all_to_all x1, blocking collectives: 30.5 us -> 27.1 us  [to_columns(): return lax.all_to_all(x, 'lev', 2, 1, tiled=True)]
    slice x1 -> x2, other arithmetic: 0.04 us -> 2.67 us  [the longest x1 1.94 us: circular(): south_east = neighbour(x[:, :, bottom, first], -1, -1)]
    ppermute x8 -> x16, waiting for transfers between devices: 6.8 us -> 8.64 us  [neighbour(): return lax.ppermute(piece, ('gx', 'gy'), pairs)]
    slice x7 -> x8, local copies, waits for them, and re-layouts: 12.4 us -> 11.8 us  [the longest x4 7.43 us: circular(): east = neighbour(x[:, :, :, first], 0, -1)]
  transfers between devices with their start and end apart: 10 -> 17, of which waited for: 4 -> 3; matrix products, arithmetic and copies ran while one was open for 8% -> 12% of each run, Pallas kernels for 0% -> 0%
where the time goes in v1:
time: 220 us; the launch traced here: 219 us
  blocking collectives  86.6 us (39%)
  starting transfers between devices  62.7 us (28%)
  local copies, waits for them, and re-layouts  26.5 us (12%)
  Pallas kernels  16 us (7%)
  other arithmetic  15.6 us (7%)
  waiting for transfers between devices  8.64 us (4%)
    all_to_all x2, blocking collectives, to_levels(): return lax.all_to_all(x, 'lev', 1, 2, tiled=True)  59.5 us
    ppermute x16, starting transfers between devices, neighbour(): return lax.ppermute(piece, ('gx', 'gy'), pairs)  54.5 us
    all_to_all x1, blocking collectives, to_columns(): return lax.all_to_all(x, 'lev', 2, 1, tiled=True)  27.1 us
    pallas_call x1, Pallas kernels, diffusion(): pl.pallas_call(functools.partial(diffusion_kernel, steps, rows, cols), ou...  16 us
    concatenate x2, other arithmetic, circular(): return jnp.concatenate([tall, east, middle, west], 3)  9.08 us
    ppermute x16, waiting for transfers between devices, neighbour(): return lax.ppermute(piece, ('gx', 'gy'), pairs)  8.64 us
    all_to_all x1, starting transfers between devices, to_columns(): return lax.all_to_all(x, 'lev', 2, 1, tiled=True)  8.18 us
    ppermute x4, local copies, waits for them, and re-layouts, neighbour(): return lax.ppermute(piece, ('gx', 'gy'), pairs)  7.98 us
  transfers between devices with their start and end apart: 17, of which 3 were waited for; matrix products, arithmetic and copies ran while one was open for 12% of the time, Pallas kernels for 0%

profile of v1, /device:TPU:1, one launch (start us, length us, event | category | flops | bytes accessed | tf_op | source)
XLA Modules:
  0.0 218.6 jit_solution(6772909194943909084)
XLA Ops:
  0.0 1.3 fusion.6
  1.3 1.9 pad_maximum_fusion.4
  3.2 8.2 %collective-permute-start.3 = (f32[3,16,4,4]{3,2,1,0:T(4,128)}, f32[3,16,4,4]{3,2,1,0:T(4,128)S(1)}, u32[]{:S(2)}, u32[]{:S(2)}) collective-permute-start(f32[3,16,4,4]{3,2,1,0:T(4,128)} %get-tuple-element.13), channel_id=1, source_target_pairs={{1,60},{2,61},{3,62},{5,0},{6,1},{7,2},{9,4},{10,5},{11,6},{13,8},... | collective-permute-start | bytes 9224 | tf_op jit(solution)/shard_map/ppermute | solution.py:22
  11.7 1.6 copy.44
  13.3 8.2 %all-to-all-start = ((f32[2,16,64,128]{3,1,0,2:T(8,128)}), f32[2,16,64,128]{3,1,0,2:T(8,128)}, u32[]{:S(2)}, u32[]{:S(2)}) async-start(f32[2,16,64,128]{3,1,0,2:T(8,128)} %copy.44), calls=%async_computation | async-start | bytes 2097152 | tf_op jit(solution)/shard_map/all_to_all | solution.py:79
  21.6 2.2 %fusion.2 = (f32[3,16,64,4]{3,2,1,0:T(8,128)}, f32[3,16,64,4]{3,2,1,0:T(8,128)}) fusion(f32[3,16,64,128]{3,2,1,0:T(8,128)S(1)} %pad_maximum_fusion), kind=kLoop, calls=%fused_computation.19 | loop fusion | bytes 196608 | tf_op jit(solution)/shard_map/slice | solution.py:31
  23.8 1.9 copy.41
  25.8 3.1 %collective-permute-start.5 = (f32[3,16,64,4]{2,1,3,0:T(8,128)S(1)}, f32[3,16,64,4]{2,1,3,0:T(8,128)S(1)}, u32[]{:S(2)}, u32[]{:S(2)}) collective-permute-start(f32[3,16,64,4]{2,1,3,0:T(8,128)S(1)} %copy.41), channel_id=1, source_target_pairs={{0,1},{1,2},{2,3},{4,5},{5,6},{6,7},{8,9},{9,10},{10,11},{12,13},{... | collective-permute-start | bytes 147464 | tf_op jit(solution)/shard_map/ppermute | solution.py:22
  28.9 1.9 copy.39
  30.8 1.9 collective-permute-start.2
  32.7 0.7 pad_maximum_fusion.6
  33.5 0.5 collective-permute-start
  33.9 1.0 collective-permute-start.1
  34.9 3.6 %collective-permute-start.7 = (f32[3,16,4,4]{3,2,1,0:T(4,128)}, f32[3,16,4,4]{3,2,1,0:T(4,128)}, u32[]{:S(2)}, u32[]{:S(2)}) collective-permute-start(f32[3,16,4,4]{3,2,1,0:T(4,128)} %get-tuple-element.14), channel_id=1, source_target_pairs={{0,5},{1,6},{2,7},{4,9},{5,10},{6,11},{8,13},{9,14},{10,15},{12,17... | collective-permute-start | bytes 9224 | tf_op jit(solution)/shard_map/ppermute | solution.py:22
  38.6 6.0 %collective-permute-start.6 = (f32[3,16,4,4]{3,2,1,0:T(4,128)}, f32[3,16,4,4]{3,2,1,0:T(4,128)}, u32[]{:S(2)}, u32[]{:S(2)}) collective-permute-start(f32[3,16,4,4]{3,2,1,0:T(4,128)} %get-tuple-element.15), channel_id=1, source_target_pairs={{0,61},{1,62},{2,63},{4,1},{5,2},{6,3},{8,5},{9,6},{10,7},{12,9},{... | collective-permute-start | bytes 9224 | tf_op jit(solution)/shard_map/ppermute | solution.py:22
  44.6 1.9 collective-permute-start.4
  46.6 0.9 convert_add_fusion
  47.8 2.6 %copy.40 = f32[3,16,64,4]{3,2,1,0:T(8,128)} copy(f32[3,16,64,4]{2,1,3,0:T(8,128)} %copy-done.6) | data formatting | bytes 98304 | tf_op jit(solution)/shard_map/ppermute | solution.py:22
  50.4 2.6 %copy.42 = f32[3,16,64,4]{3,2,1,0:T(8,128)} copy(f32[3,16,64,4]{2,1,3,0:T(8,128)} %copy-done.5) | data formatting | bytes 98304 | tf_op jit(solution)/shard_map/ppermute | solution.py:22
  53.0 2.2 collective-permute-done.4
  55.2 5.2 %maximum_maximum_fusion.c_ref = f32[3,16,80,256]{3,2,1,0:T(8,128)} fusion(f32[3,16,4,4]{3,2,1,0:T(4,128)} %collective-permute-done.7, f32[3,16,8,4]{3,2,1,0:T(8,128)S(1)} %broadcast_in_dim.25, f32[3,16,4,4]{3,2,1,0:T(4,128)} %collective-permute-done.6, f32[3,16,64,4]{3,2,1,0:T(8,128)} %copy.42, f32[3,16,4,4]{3,2,1,0:T(4,128)} %collective-permute-done.4, ...), kind=kLoop, calls=%fused_computation | loop fusion | flops 13762560 | bytes 5901312 | tf_op jit(solution)/shard_map/concatenate | solution.py:43
  60.3 1.4 copy.45
  61.7 1.1 convolution_bitcast_fusion.1
  62.8 0.6 copy.46
  63.4 34.5 %all_to_all.72 = f32[2,64,16,128]{3,2,0,1:T(8,128)S(1)} all-to-all(f32[2,64,16,128]{3,2,0,1:T(8,128)S(1)} %copy.46), channel_id=1, replica_groups=mesh['lev'=4,'gx'=16,'gy'=4] {'lev'}, dimensions={1} | all-to-all | bytes 2097152 | tf_op jit(solution)/shard_map/all_to_all | solution.py:83
  98.2 1.7 fusion.4
  99.9 3.3 %collective-permute-start.8 = (f32[2,16,4,128]{3,2,1,0:T(4,128)S(1)}, f32[2,16,4,128]{3,2,1,0:T(4,128)S(1)}, u32[]{:S(2)}, u32[]{:S(2)}) collective-permute-start(f32[2,16,4,128]{3,2,1,0:T(4,128)S(1)} %get-tuple-element.17), channel_id=1, source_target_pairs={{0,60},{1,61},{2,62},{3,63},{4,0},{5,1},{6,2},{7,3},{8,4},{9,5},{1... | collective-permute-start | bytes 196616 | tf_op jit(solution)/shard_map/ppermute | solution.py:22
  103.2 1.6 copy.48
  104.7 1.6 copy.50
  106.4 3.1 %collective-permute-start.13 = (f32[2,16,64,4]{2,1,3,0:T(8,128)S(1)}, f32[2,16,64,4]{2,1,3,0:T(8,128)S(1)}, u32[]{:S(2)}, u32[]{:S(2)}) collective-permute-start(f32[2,16,64,4]{2,1,3,0:T(8,128)S(1)} %copy.50), channel_id=1, source_target_pairs={{0,1},{1,2},{2,3},{4,5},{5,6},{6,7},{8,9},{9,10},{10,11},{12,13},{... | collective-permute-start | bytes 98312 | tf_op jit(solution)/shard_map/ppermute | solution.py:22
  109.4 1.9 collective-permute-start.10
  111.3 0.8 fusion.5
  112.1 5.3 %collective-permute-start.11 = (f32[2,16,4,4]{3,2,1,0:T(4,128)S(1)}, f32[2,16,4,4]{3,2,1,0:T(4,128)S(1)}, u32[]{:S(2)}, u32[]{:S(2)}) collective-permute-start(f32[2,16,4,4]{3,2,1,0:T(4,128)S(1)} %get-tuple-element.21), channel_id=1, source_target_pairs={{1,60},{2,61},{3,62},{5,0},{6,1},{7,2},{9,4},{10,5},{11,6},{13,8},... | collective-permute-start | bytes 6152 | tf_op jit(solution)/shard_map/ppermute | solution.py:22
  117.5 1.3 collective-permute-done.11
  118.8 1.9 collective-permute-start.15
  120.7 10.7 %collective-permute-start.14 = (f32[2,16,4,4]{3,2,1,0:T(4,128)}, f32[2,16,4,4]{3,2,1,0:T(4,128)S(1)}, u32[]{:S(2)}, u32[]{:S(2)}) collective-permute-start(f32[2,16,4,4]{3,2,1,0:T(4,128)} %get-tuple-element.23), channel_id=1, source_target_pairs={{0,61},{1,62},{2,63},{4,1},{5,2},{6,3},{8,5},{9,6},{10,7},{12,9},{... | collective-permute-start | bytes 6152 | tf_op jit(solution)/shard_map/ppermute | solution.py:22
  131.4 2.1 collective-permute-start.12
  133.5 1.4 copy.49
  134.9 1.4 copy.51
  136.3 5.1 %collective-permute-done.12 = f32[2,16,4,4]{3,2,1,0:T(4,128)S(1)} collective-permute-done((f32[2,16,4,4]{3,2,1,0:T(4,128)}, f32[2,16,4,4]{3,2,1,0:T(4,128)S(1)}, u32[]{:S(2)}, u32[]{:S(2)}) %collective-permute-start.12) | collective-permute-done | bytes 2080 | tf_op jit(solution)/shard_map/ppermute | solution.py:22
  141.4 3.9 %maximum_maximum_fusion.1.v_ref = f32[2,16,80,256]{3,2,1,0:T(8,128)} fusion(f32[2,16,4,4]{3,2,1,0:T(4,128)S(1)} %collective-permute-done.15, f32[2,16,8,4]{3,2,1,0:T(8,128)S(1)} %broadcast_in_dim.28, f32[2,16,4,4]{3,2,1,0:T(4,128)S(1)} %collective-permute-done.14, f32[2,16,64,4]{3,2,1,0:T(8,128)} %copy.51, f32[2,16,4,4]{3,2,1,0:T(4,128)S(1)} %collective-permute-done.12, ...), kind=kLoop, calls=%fused_computation.1 | loop fusion | flops 7864320 | bytes 3961856 | tf_op jit(solution)/shard_map/concatenate | solution.py:43
  145.4 16.0 %shard_map.64 = f32[2,16,64,128]{3,2,1,0:T(8,128)} custom-call(f32[2,16,80,256]{3,2,1,0:T(8,128)} %maximum_maximum_fusion.1.v_ref, f32[3,16,80,256]{3,2,1,0:T(8,128)} %maximum_maximum_fusion.c_ref), custom_call_target="tpu_custom_call" | custom-call | tf_op jit(solution)/shard_map/pallas_call | solution.py:66
  161.4 1.8 copy.52
  163.2 27.1 %all_to_all.73 = f32[2,16,64,128]{3,1,0,2:T(8,128)S(1)} all-to-all(f32[2,16,64,128]{3,1,0,2:T(8,128)S(1)} %copy.52), channel_id=1, replica_groups=mesh['lev'=4,'gx'=16,'gy'=4] {'lev'}, dimensions={2} | all-to-all | bytes 2097152 | tf_op jit(solution)/shard_map/all_to_all | solution.py:79
  190.5 1.1 convolution_bitcast_fusion
  191.6 0.6 copy.55
  192.2 25.0 %all_to_all.74 = f32[2,64,16,128]{3,2,0,1:T(8,128)S(1)} all-to-all(f32[2,64,16,128]{3,2,0,1:T(8,128)S(1)} %copy.55), channel_id=1, replica_groups=mesh['lev'=4,'gx'=16,'gy'=4] {'lev'}, dimensions={1} | all-to-all | bytes 2097152 | tf_op jit(solution)/shard_map/all_to_all | solution.py:83
  217.3 1.2 bitcast_multiply_fusion
  (46 shorter events, 1.3 us)
Async XLA Ops:
  0.0 11.5 %copy-start.2 = (f32[2,16,64,128]{3,2,1,0:T(8,128)S(1)}, f32[2,16,64,128]{3,2,1,0:T(8,128)}, u32[]{:S(2)}) copy-start(f32[2,16,64,128]{3,2,1,0:T(8,128)} %param.7) | copy-start | bytes 3145732
  0.0 11.5 %copy-start.3 = (f32[2,16,64,128]{3,2,1,0:T(8,128)S(1)}, f32[2,16,64,128]{3,2,1,0:T(8,128)}, u32[]{:S(2)}) copy-start(f32[2,16,64,128]{3,2,1,0:T(8,128)} %param.6) | copy-start | bytes 3145732
  3.2 31.7 %collective-permute-start.3 = (f32[3,16,4,4]{3,2,1,0:T(4,128)}, f32[3,16,4,4]{3,2,1,0:T(4,128)S(1)}, u32[]{:S(2)}, u32[]{:S(2)}) collective-permute-start(f32[3,16,4,4]{3,2,1,0:T(4,128)} %get-tuple-element.13), channel_id=1, source_target_pairs={{1,60},{2,61},{3,62},{5,0},{6,1},{7,2},{9,4},{10,5},{11,6},{13,8},... | collective-permute-start | bytes 9224 | tf_op jit(solution)/shard_map/ppermute | solution.py:22
  11.7 9.8 %copy-start = (f32[16,64,128]{2,1,0:T(8,128)S(1)}, f32[16,64,128]{2,1,0:T(8,128)}, u32[]{:S(2)}) copy-start(f32[16,64,128]{2,1,0:T(8,128)} %param.9) | copy-start | bytes 1572868
  11.7 9.8 %copy-start.1 = (f32[16,64,128]{2,1,0:T(8,128)S(1)}, f32[16,64,128]{2,1,0:T(8,128)}, u32[]{:S(2)}) copy-start(f32[16,64,128]{2,1,0:T(8,128)} %param.8) | copy-start | bytes 1572868
  13.3 47.0 %all-to-all-start = ((f32[2,16,64,128]{3,1,0,2:T(8,128)}), f32[2,16,64,128]{3,1,0,2:T(8,128)}, u32[]{:S(2)}, u32[]{:S(2)}) async-start(f32[2,16,64,128]{3,1,0,2:T(8,128)} %copy.44), calls=%async_computation | async-start | bytes 2097152 | tf_op jit(solution)/shard_map/all_to_all | solution.py:79
  25.8 12.8 %collective-permute-start.5 = (f32[3,16,64,4]{2,1,3,0:T(8,128)S(1)}, f32[3,16,64,4]{2,1,3,0:T(8,128)S(1)}, u32[]{:S(2)}, u32[]{:S(2)}) collective-permute-start(f32[3,16,64,4]{2,1,3,0:T(8,128)S(1)} %copy.41), channel_id=1, source_target_pairs={{0,1},{1,2},{2,3},{4,5},{5,6},{6,7},{8,9},{9,10},{10,11},{12,13},{... | collective-permute-start | bytes 147464 | tf_op jit(solution)/shard_map/ppermute | solution.py:22
  30.8 13.8 %collective-permute-start.2 = (f32[3,16,64,4]{2,1,3,0:T(8,128)S(1)}, f32[3,16,64,4]{2,1,3,0:T(8,128)S(1)}, u32[]{:S(2)}, u32[]{:S(2)}) collective-permute-start(f32[3,16,64,4]{2,1,3,0:T(8,128)S(1)} %copy.39), channel_id=1, source_target_pairs={{1,0},{2,1},{3,2},{5,4},{6,5},{7,6},{9,8},{10,9},{11,10},{13,12},{... | collective-permute-start | bytes 147464 | tf_op jit(solution)/shard_map/ppermute | solution.py:22
  33.5 21.7 %collective-permute-start = (f32[3,16,4,128]{3,2,1,0:T(4,128)}, f32[3,16,4,128]{3,2,1,0:T(4,128)}, u32[]{:S(2)}, u32[]{:S(2)}) collective-permute-start(f32[3,16,4,128]{3,2,1,0:T(4,128)} %get-tuple-element.9), channel_id=1, source_target_pairs={{0,60},{1,61},{2,62},{3,63},{4,0},{5,1},{6,2},{7,3},{8,4},{9,5},{1... | collective-permute-start | bytes 294920 | tf_op jit(solution)/shard_map/ppermute | solution.py:22
  33.9 21.2 %collective-permute-start.1 = (f32[3,16,4,128]{3,2,1,0:T(4,128)}, f32[3,16,4,128]{3,2,1,0:T(4,128)}, u32[]{:S(2)}, u32[]{:S(2)}) collective-permute-start(f32[3,16,4,128]{3,2,1,0:T(4,128)} %get-tuple-element.10), channel_id=1, source_target_pairs={{0,4},{1,5},{2,6},{3,7},{4,8},{5,9},{6,10},{7,11},{8,12},{9,13},{1... | collective-permute-start | bytes 294920 | tf_op jit(solution)/shard_map/ppermute | solution.py:22
  34.9 11.6 %copy-start.4 = (f32[3,16,4,4]{3,2,1,0:T(4,128)}, f32[3,16,4,4]{3,2,1,0:T(4,128)S(1)}, u32[]{:S(2)}) copy-start(f32[3,16,4,4]{3,2,1,0:T(4,128)S(1)} %collective-permute-done.3) | copy-start | bytes 9220
  34.9 18.1 %collective-permute-start.7 = (f32[3,16,4,4]{3,2,1,0:T(4,128)}, f32[3,16,4,4]{3,2,1,0:T(4,128)}, u32[]{:S(2)}, u32[]{:S(2)}) collective-permute-start(f32[3,16,4,4]{3,2,1,0:T(4,128)} %get-tuple-element.14), channel_id=1, source_target_pairs={{0,5},{1,6},{2,7},{4,9},{5,10},{6,11},{8,13},{9,14},{10,15},{12,17... | collective-permute-start | bytes 9224 | tf_op jit(solution)/shard_map/ppermute | solution.py:22
  38.6 6.0 %copy-start.5 = (f32[3,16,64,4]{2,1,3,0:T(8,128)}, f32[3,16,64,4]{2,1,3,0:T(8,128)S(1)}, u32[]{:S(2)}) copy-start(f32[3,16,64,4]{2,1,3,0:T(8,128)S(1)} %collective-permute-done.5) | copy-start | bytes 147460
  38.6 14.4 %collective-permute-start.6 = (f32[3,16,4,4]{3,2,1,0:T(4,128)}, f32[3,16,4,4]{3,2,1,0:T(4,128)}, u32[]{:S(2)}, u32[]{:S(2)}) collective-permute-start(f32[3,16,4,4]{3,2,1,0:T(4,128)} %get-tuple-element.15), channel_id=1, source_target_pairs={{0,61},{1,62},{2,63},{4,1},{5,2},{6,3},{8,5},{9,6},{10,7},{12,9},{... | collective-permute-start | bytes 9224 | tf_op jit(solution)/shard_map/ppermute | solution.py:22
  44.6 2.0 copy-start.6
  44.6 10.5 %collective-permute-start.4 = (f32[3,16,4,4]{3,2,1,0:T(4,128)}, f32[3,16,4,4]{3,2,1,0:T(4,128)}, u32[]{:S(2)}, u32[]{:S(2)}) collective-permute-start(f32[3,16,4,4]{3,2,1,0:T(4,128)} %get-tuple-element.16), channel_id=1, source_target_pairs={{1,4},{2,5},{3,6},{5,8},{6,9},{7,10},{9,12},{10,13},{11,14},{13,16... | collective-permute-start | bytes 9224 | tf_op jit(solution)/shard_map/ppermute | solution.py:22
  47.6 12.7 %copy-start.7 = (f32[256]{0:T(256)}, f32[256]{0:T(256)S(1)}, u32[]{:S(2)}) copy-start(f32[256]{0:T(256)S(1)} %pad.23.clone) | copy-start | bytes 3076
  99.9 41.6 %collective-permute-start.8 = (f32[2,16,4,128]{3,2,1,0:T(4,128)S(1)}, f32[2,16,4,128]{3,2,1,0:T(4,128)S(1)}, u32[]{:S(2)}, u32[]{:S(2)}) collective-permute-start(f32[2,16,4,128]{3,2,1,0:T(4,128)S(1)} %get-tuple-element.17), channel_id=1, source_target_pairs={{0,60},{1,61},{2,62},{3,63},{4,0},{5,1},{6,2},{7,3},{8,4},{9,5},{1... | collective-permute-start | bytes 196616 | tf_op jit(solution)/shard_map/ppermute | solution.py:22
  103.1 38.3 %collective-permute-start.9 = (f32[2,16,4,128]{3,2,1,0:T(4,128)S(1)}, f32[2,16,4,128]{3,2,1,0:T(4,128)S(1)}, u32[]{:S(2)}, u32[]{:S(2)}) collective-permute-start(f32[2,16,4,128]{3,2,1,0:T(4,128)S(1)} %get-tuple-element.18), channel_id=1, source_target_pairs={{0,4},{1,5},{2,6},{3,7},{4,8},{5,9},{6,10},{7,11},{8,12},{9,13},{1... | collective-permute-start | bytes 196616 | tf_op jit(solution)/shard_map/ppermute | solution.py:22
  106.4 14.3 %collective-permute-start.13 = (f32[2,16,64,4]{2,1,3,0:T(8,128)S(1)}, f32[2,16,64,4]{2,1,3,0:T(8,128)S(1)}, u32[]{:S(2)}, u32[]{:S(2)}) collective-permute-start(f32[2,16,64,4]{2,1,3,0:T(8,128)S(1)} %copy.50), channel_id=1, source_target_pairs={{0,1},{1,2},{2,3},{4,5},{5,6},{6,7},{8,9},{9,10},{10,11},{12,13},{... | collective-permute-start | bytes 98312 | tf_op jit(solution)/shard_map/ppermute | solution.py:22
  109.4 22.0 %collective-permute-start.10 = (f32[2,16,64,4]{2,1,3,0:T(8,128)S(1)}, f32[2,16,64,4]{2,1,3,0:T(8,128)S(1)}, u32[]{:S(2)}, u32[]{:S(2)}) collective-permute-start(f32[2,16,64,4]{2,1,3,0:T(8,128)S(1)} %copy.48), channel_id=1, source_target_pairs={{1,0},{2,1},{3,2},{5,4},{6,5},{7,6},{9,8},{10,9},{11,10},{13,12},{... | collective-permute-start | bytes 98312 | tf_op jit(solution)/shard_map/ppermute | solution.py:22
  112.1 6.6 %collective-permute-start.11 = (f32[2,16,4,4]{3,2,1,0:T(4,128)S(1)}, f32[2,16,4,4]{3,2,1,0:T(4,128)S(1)}, u32[]{:S(2)}, u32[]{:S(2)}) collective-permute-start(f32[2,16,4,4]{3,2,1,0:T(4,128)S(1)} %get-tuple-element.21), channel_id=1, source_target_pairs={{1,60},{2,61},{3,62},{5,0},{6,1},{7,2},{9,4},{10,5},{11,6},{13,8},... | collective-permute-start | bytes 6152 | tf_op jit(solution)/shard_map/ppermute | solution.py:22
  118.8 17.5 %collective-permute-start.15 = (f32[2,16,4,4]{3,2,1,0:T(4,128)}, f32[2,16,4,4]{3,2,1,0:T(4,128)S(1)}, u32[]{:S(2)}, u32[]{:S(2)}) collective-permute-start(f32[2,16,4,4]{3,2,1,0:T(4,128)} %get-tuple-element.22), channel_id=1, source_target_pairs={{0,5},{1,6},{2,7},{4,9},{5,10},{6,11},{8,13},{9,14},{10,15},{12,17... | collective-permute-start | bytes 6152 | tf_op jit(solution)/shard_map/ppermute | solution.py:22
  120.7 15.6 %collective-permute-start.14 = (f32[2,16,4,4]{3,2,1,0:T(4,128)}, f32[2,16,4,4]{3,2,1,0:T(4,128)S(1)}, u32[]{:S(2)}, u32[]{:S(2)}) collective-permute-start(f32[2,16,4,4]{3,2,1,0:T(4,128)} %get-tuple-element.23), channel_id=1, source_target_pairs={{0,61},{1,62},{2,63},{4,1},{5,2},{6,3},{8,5},{9,6},{10,7},{12,9},{... | collective-permute-start | bytes 6152 | tf_op jit(solution)/shard_map/ppermute | solution.py:22
  131.4 10.0 %collective-permute-start.12 = (f32[2,16,4,4]{3,2,1,0:T(4,128)}, f32[2,16,4,4]{3,2,1,0:T(4,128)S(1)}, u32[]{:S(2)}, u32[]{:S(2)}) collective-permute-start(f32[2,16,4,4]{3,2,1,0:T(4,128)} %get-tuple-element.24), channel_id=1, source_target_pairs={{1,4},{2,5},{3,6},{5,8},{6,9},{7,10},{9,12},{10,13},{11,14},{13,16... | collective-permute-start | bytes 6152 | tf_op jit(solution)/shard_map/ppermute | solution.py:22

commit v2 on v0

--- a/solution.py
+++ b/solution.py
@@ -27,14 +27,15 @@
     return jnp.concatenate([tall, east, middle, west], 3)
 
 
-def diffusion_kernel(steps, rows, cols, v_ref, c_ref, o_ref):
+def diffusion_kernel(steps, rows, cols, v_ref, o_ref):
     height, span = v_ref.shape[2], v_ref.shape[3]
-    along_i = c_ref[0, 0]
-    along_j = c_ref[1, 0]
-    sea = c_ref[2, 0]
+    fields = o_ref.shape[0]
+    along_i = v_ref[fields, 0]
+    along_j = v_ref[fields + 1, 0]
+    sea = v_ref[fields + 2, 0]
     weight_i = along_i * sea * pltpu.roll(sea, height - 1, 0)
     weight_j = along_j * sea * pltpu.roll(sea, span - 1, 1)
-    for f in range(v_ref.shape[0]):
+    for f in range(fields):
         values = v_ref[f, 0]
         for s in range(steps):
             flux_i = weight_i * (pltpu.roll(values, height - 1, 0) - values)
@@ -45,18 +46,15 @@
 
 def diffusion(values, coefs, steps):
     fields, levels, rows, cols = values.shape
-    ext = circular(values, steps)
+    ext = circular(jnp.concatenate([values, coefs]), steps)
     height, span = ext.shape[2], ext.shape[3]
     return pl.pallas_call(
         functools.partial(diffusion_kernel, steps, rows, cols),
         out_shape=jax.ShapeDtypeStruct(values.shape, values.dtype),
         grid=(levels,),
-        in_specs=[
-            pl.BlockSpec((fields, 1, height, span), lambda l: (0, l, 0, 0)),
-            pl.BlockSpec((3, 1, height, span), lambda l: (0, l, 0, 0)),
-        ],
+        in_specs=[pl.BlockSpec((ext.shape[0], 1, height, span), lambda l: (0, l, 0, 0))],
         out_specs=pl.BlockSpec((fields, 1, rows, cols), lambda l: (0, l, 0, 0)),
-    )(ext, coefs)
+    )(ext)
 
 
 def to_columns(x):
@@ -82,7 +80,7 @@
     balance = jnp.eye(order_count, dtype=jnp.float32) + coupling
     forward = balance.reshape(2, level_count, 2, level_count)
     adjoint = jnp.transpose(forward, (2, 3, 0, 1))
-    coefs = circular(jnp.stack([diffusion_i, diffusion_j, ocean]), steps)
+    coefs = jnp.stack([diffusion_i, diffusion_j, ocean])
     adjoint_mixed = level_mix(scaled, adjoint) * ocean[None]
     spread = diffusion(adjoint_mixed, coefs, steps)
     forward_mixed = level_mix(spread, forward)

time: 201 us -> 192 us (0.955)
  starting transfers between devices: 48.7 us -> 21.6 us
  blocking collectives: 59.5 us -> 85.6 us
  local copies, waits for them, and re-layouts: 28.2 us -> 22.7 us
  other arithmetic: 13.2 us -> 10.2 us
    all_to_all x1 -> x2, blocking collectives: 29 us -> 56.8 us  [to_levels(): return lax.all_to_all(x, 'lev', 1, 2, tiled=True)]
    ppermute x2 -> x1, starting transfers between devices: 13.1 us -> 1.91 us  [circular(): west = lax.ppermute(tall[..., cols - width:], 'gy', right)]
    ppermute x2 -> x1, starting transfers between devices: 11.2 us -> 5.63 us  [circular(): east = lax.ppermute(tall[..., :width], 'gy', left)]
    all_to_all x1 -> x0, starting transfers between devices: 5.45 us -> none  [to_levels(): return lax.all_to_all(x, 'lev', 1, 2, tiled=True)]
    ppermute x2 -> x1, starting transfers between devices: 9.94 us -> 5.01 us  [circular(): south = lax.ppermute(x[:, :, :width], 'gx', down)]
    slice x4 -> x2, local copies, waits for them, and re-layouts: 9.37 us -> 6.96 us  [circular(): east = lax.ppermute(tall[..., :width], 'gy', left)]
    concatenate x2 -> x1, other arithmetic: 7.8 us -> 5.49 us  [circular(): return jnp.concatenate([tall, east, middle, west], 3)]
    ppermute x2 -> x1, waiting for transfers between devices: 5.15 us -> 5.22 us  [circular(): north = lax.ppermute(x[:, :, rows - width:], 'gx', up)]
  transfers between devices with their start and end apart: 10 -> 5, of which waited for: 4 -> 3; matrix products, arithmetic and copies ran while one was open for 8% -> 4% of each run, Pallas kernels for 0% -> 0%
where the time goes in v2:
time: 192 us; the launch traced here: 189 us
  blocking collectives  85.6 us (45%)
  waiting for transfers between devices  30.9 us (16%)
  local copies, waits for them, and re-layouts  22.7 us (12%)
  starting transfers between devices  21.6 us (11%)
  Pallas kernels  15.8 us (8%)
  other arithmetic  10.2 us (5%)
  matrix products  2.11 us (1%)
    all_to_all x2, blocking collectives, to_levels(): return lax.all_to_all(x, 'lev', 1, 2, tiled=True)  56.8 us
    all_to_all x1, blocking collectives, to_columns(): return lax.all_to_all(x, 'lev', 2, 1, tiled=True)  28.8 us
    all_to_all x1, waiting for transfers between devices, to_columns(): return lax.all_to_all(x, 'lev', 2, 1, tiled=True)  23.4 us
    pallas_call x1, Pallas kernels, diffusion(): pl.pallas_call(functools.partial(diffusion_kernel, steps, rows, cols), ou...  15.8 us
    all_to_all x1, starting transfers between devices, to_columns(): return lax.all_to_all(x, 'lev', 2, 1, tiled=True)  9.01 us
    slice x2, local copies, waits for them, and re-layouts, circular(): east = lax.ppermute(tall[..., :width], 'gy', left)  6.96 us
    ppermute x1, starting transfers between devices, circular(): east = lax.ppermute(tall[..., :width], 'gy', left)  5.63 us
    concatenate x1, other arithmetic, circular(): return jnp.concatenate([tall, east, middle, west], 3)  5.49 us
  transfers between devices with their start and end apart: 5, of which 3 were waited for; matrix products, arithmetic and copies ran while one was open for 4% of the time, Pallas kernels for 0%

profile of v2, /device:TPU:1, one launch (start us, length us, event | category | flops | bytes accessed | tf_op | source)
XLA Modules:
  0.0 189.1 jit_solution(14083723639778528003)
XLA Ops:
  0.0 1.2 fusion.3
  1.2 0.0 copy-start.7
  1.2 1.8 multiply_multiply_fusion
  3.0 1.6 copy.14
  4.5 9.0 %all-to-all-start = ((f32[2,16,64,128]{3,1,0,2:T(8,128)}), f32[2,16,64,128]{3,1,0,2:T(8,128)S(1)}, u32[]{:S(2)}, u32[]{:S(2)}) async-start(f32[2,16,64,128]{3,1,0,2:T(8,128)} %copy.14), calls=%async_computation | async-start | bytes 2097152 | tf_op jit(solution)/shard_map/all_to_all | solution.py:61
  13.6 0.0 copy-done.7
  13.6 0.1 reshape.4
  13.7 0.0 copy-start.3
  13.7 0.1 copy.13
  13.8 23.4 %all-to-all-done = f32[2,16,64,128]{3,1,0,2:T(8,128)S(1)} async-done(((f32[2,16,64,128]{3,1,0,2:T(8,128)}), f32[2,16,64,128]{3,1,0,2:T(8,128)S(1)}, u32[]{:S(2)}, u32[]{:S(2)}) %all-to-all-start) | async-done | bytes 1048608 | tf_op jit(solution)/shard_map/all_to_all | solution.py:61
  37.2 0.1 copy.15
  37.4 1.1 convolution_bitcast_fusion.1
  38.4 0.0 copy-done.3
  38.4 0.6 copy.16
  39.1 0.0 copy-start
  39.1 0.0 copy-start.1
  39.1 31.4 %all_to_all.72 = f32[2,64,16,128]{3,2,0,1:T(8,128)S(1)} all-to-all(f32[2,64,16,128]{3,2,0,1:T(8,128)S(1)} %copy.16), channel_id=1, replica_groups=mesh['lev'=4,'gx'=16,'gy'=4] {'lev'}, dimensions={1} | all-to-all | bytes 2097152 | tf_op jit(solution)/shard_map/all_to_all | solution.py:65
  70.5 0.1 copy.17
  70.6 0.1 bitcast_multiply_fusion.1
  70.7 0.0 copy-done
  70.8 0.1 pad_maximum_fusion.5
  70.8 5.0 %collective-permute-start = (f32[5,16,4,128]{3,2,1,0:T(4,128)S(1)}, f32[5,16,4,128]{3,2,1,0:T(4,128)S(1)}, u32[]{:S(2)}, u32[]{:S(2)}) collective-permute-start(f32[5,16,4,128]{3,2,1,0:T(4,128)S(1)} %get-tuple-element.7), channel_id=1, source_target_pairs={{4,0},{8,4},{12,8},{16,12},{20,16},{24,20},{28,24},{32,28},{36,32}... | collective-permute-start | bytes 491528 | tf_op jit(solution)/shard_map/ppermute | solution.py:19
  75.8 0.0 collective-permute-start.1
  75.8 2.3 %collective-permute-done = f32[5,16,4,128]{3,2,1,0:T(4,128)S(1)} collective-permute-done((f32[5,16,4,128]{3,2,1,0:T(4,128)S(1)}, f32[5,16,4,128]{3,2,1,0:T(4,128)S(1)}, u32[]{:S(2)}, u32[]{:S(2)}) %collective-permute-start) | collective-permute-done | bytes 163872 | tf_op jit(solution)/shard_map/ppermute | solution.py:19
  78.1 5.2 %collective-permute-done.1 = f32[5,16,4,128]{3,2,1,0:T(4,128)S(1)} collective-permute-done((f32[5,16,4,128]{3,2,1,0:T(4,128)S(1)}, f32[5,16,4,128]{3,2,1,0:T(4,128)S(1)}, u32[]{:S(2)}, u32[]{:S(2)}) %collective-permute-start.1) | collective-permute-done | bytes 163872 | tf_op jit(solution)/shard_map/ppermute | solution.py:18
  83.4 0.6 copy-done.6
  84.0 0.3 pad_maximum_fusion.1
  84.3 3.8 %fusion.2 = (f32[5,16,80,4]{3,2,1,0:T(8,128)}, f32[5,16,80,4]{3,2,1,0:T(8,128)}) fusion(f32[5,16,80,128]{3,2,1,0:T(8,128)S(1)} %pad_maximum_fusion.1), kind=kLoop, calls=%fused_computation.16 | loop fusion | bytes 409600 | tf_op jit(solution)/shard_map/slice | solution.py:24
  88.2 3.1 %copy.18 = f32[5,16,80,4]{2,1,3,0:T(8,128)} copy(f32[5,16,80,4]{3,2,1,0:T(8,128)} %get-tuple-element.5) | data formatting | bytes 204800 | tf_op jit(solution)/shard_map/slice | solution.py:24
  91.3 5.6 %collective-permute-start.2 = (f32[5,16,80,4]{2,1,3,0:T(8,128)}, f32[5,16,80,4]{2,1,3,0:T(8,128)}, u32[]{:S(2)}, u32[]{:S(2)}) collective-permute-start(f32[5,16,80,4]{2,1,3,0:T(8,128)} %copy.18), channel_id=1, source_target_pairs={{1,0},{2,1},{3,2},{5,4},{6,5},{7,6},{9,8},{10,9},{11,10},{13,12},{... | collective-permute-start | bytes 307208 | tf_op jit(solution)/shard_map/ppermute | solution.py:24
  96.9 3.1 %copy.19 = f32[5,16,80,4]{2,1,3,0:T(8,128)} copy(f32[5,16,80,4]{3,2,1,0:T(8,128)} %get-tuple-element.6) | data formatting | bytes 204800 | tf_op jit(solution)/shard_map/slice | solution.py:25
  100.1 1.9 %collective-permute-start.3 = (f32[5,16,80,4]{2,1,3,0:T(8,128)}, f32[5,16,80,4]{2,1,3,0:T(8,128)}, u32[]{:S(2)}, u32[]{:S(2)}) collective-permute-start(f32[5,16,80,4]{2,1,3,0:T(8,128)} %copy.19), channel_id=1, source_target_pairs={{0,1},{1,2},{2,3},{4,5},{5,6},{6,7},{8,9},{9,10},{10,11},{12,13},{... | collective-permute-start | bytes 307208 | tf_op jit(solution)/shard_map/ppermute | solution.py:25
  102.0 0.1 pad.8.clone
  102.1 0.0 collective-permute-done.2
  102.1 3.2 %copy.20 = f32[5,16,80,4]{3,2,1,0:T(8,128)} copy(f32[5,16,80,4]{2,1,3,0:T(8,128)} %collective-permute-done.2) | data formatting | bytes 204800 | tf_op jit(solution)/shard_map/ppermute | solution.py:24
  105.3 0.0 collective-permute-done.3
  105.3 3.2 %copy.21 = f32[5,16,80,4]{3,2,1,0:T(8,128)} copy(f32[5,16,80,4]{2,1,3,0:T(8,128)} %collective-permute-done.3) | data formatting | bytes 204800 | tf_op jit(solution)/shard_map/ppermute | solution.py:25
  108.5 5.5 %pad_maximum_fusion.v_ref = f32[5,16,80,256]{3,2,1,0:T(8,128)} fusion(f32[5,16,80,4]{3,2,1,0:T(8,128)} %copy.21, f32[5,16,80,4]{3,2,1,0:T(8,128)} %copy.20, f32[5,16,4,128]{3,2,1,0:T(4,128)} %copy-done.6, f32[5,16,8,128]{3,2,1,0:T(8,128)S(1)} %broadcast_in_dim.12, f32[5,16,4,128]{3,2,1,0:T(4,128)} %copy-done.5, f32[1,16,64,128]{3,2,1,0:T(8,128)S(1)} %get-tuple-element.10, ...), kind=kLoop, calls=%fused_computation | loop fusion | flops 14745600 | bytes 10036224 | tf_op jit(solution)/shard_map/concatenate | solution.py:27
  114.0 15.8 %shard_map.64 = f32[2,16,64,128]{3,2,1,0:T(8,128)} custom-call(f32[5,16,80,256]{3,2,1,0:T(8,128)} %pad_maximum_fusion.v_ref), custom_call_target="tpu_custom_call" | custom-call | tf_op jit(solution)/shard_map/pallas_call | solution.py:51
  129.8 1.9 copy.22
  131.7 28.8 %all_to_all.73 = f32[2,16,64,128]{3,1,0,2:T(8,128)S(1)} all-to-all(f32[2,16,64,128]{3,1,0,2:T(8,128)S(1)} %copy.22), channel_id=1, replica_groups=mesh['lev'=4,'gx'=16,'gy'=4] {'lev'}, dimensions={2} | all-to-all | bytes 2097152 | tf_op jit(solution)/shard_map/all_to_all | solution.py:61
  160.4 0.1 copy.23
  160.6 1.1 convolution_bitcast_fusion
  161.6 0.0 copy-start.2
  161.7 0.6 copy.25
  162.3 25.4 %all_to_all.74 = f32[2,64,16,128]{3,2,0,1:T(8,128)S(1)} all-to-all(f32[2,64,16,128]{3,2,0,1:T(8,128)S(1)} %copy.25), channel_id=1, replica_groups=mesh['lev'=4,'gx'=16,'gy'=4] {'lev'}, dimensions={1} | all-to-all | bytes 2097152 | tf_op jit(solution)/shard_map/all_to_all | solution.py:65
  187.7 0.1 copy.26
  187.8 1.2 bitcast_multiply_fusion
  (10 shorter events, 0.1 us)
Async XLA Ops:
  1.2 12.4 %copy-start.7 = (f32[128,128]{1,0:T(8,128)S(1)}, f32[128,128]{1,0:T(8,128)}, u32[]{:S(2)}) copy-start(f32[128,128]{1,0:T(8,128)} %param.11) | copy-start | bytes 196612
  4.5 32.7 %all-to-all-start = ((f32[2,16,64,128]{3,1,0,2:T(8,128)}), f32[2,16,64,128]{3,1,0,2:T(8,128)S(1)}, u32[]{:S(2)}, u32[]{:S(2)}) async-start(f32[2,16,64,128]{3,1,0,2:T(8,128)} %copy.14), calls=%async_computation | async-start | bytes 2097152 | tf_op jit(solution)/shard_map/all_to_all | solution.py:61
  13.7 24.7 %copy-start.3 = (f32[2,64,2,64]{3,2,1,0:T(2,128)}, f32[2,64,2,64]{3,2,1,0:T(2,128)S(1)}, u32[]{:S(2)}) copy-start(f32[2,64,2,64]{3,2,1,0:T(2,128)S(1)} %reshape.4) | copy-start | bytes 196612
  39.1 31.7 %copy-start = (f32[16,64,128]{2,1,0:T(8,128)S(1)}, f32[16,64,128]{2,1,0:T(8,128)}, u32[]{:S(2)}) copy-start(f32[16,64,128]{2,1,0:T(8,128)} %param.9) | copy-start | bytes 1572868
  39.1 31.7 %copy-start.1 = (f32[16,64,128]{2,1,0:T(8,128)S(1)}, f32[16,64,128]{2,1,0:T(8,128)}, u32[]{:S(2)}) copy-start(f32[16,64,128]{2,1,0:T(8,128)} %param.8) | copy-start | bytes 1572868
  70.8 7.3 %collective-permute-start = (f32[5,16,4,128]{3,2,1,0:T(4,128)S(1)}, f32[5,16,4,128]{3,2,1,0:T(4,128)S(1)}, u32[]{:S(2)}, u32[]{:S(2)}) collective-permute-start(f32[5,16,4,128]{3,2,1,0:T(4,128)S(1)} %get-tuple-element.7), channel_id=1, source_target_pairs={{4,0},{8,4},{12,8},{16,12},{20,16},{24,20},{28,24},{32,28},{36,32}... | collective-permute-start | bytes 491528 | tf_op jit(solution)/shard_map/ppermute | solution.py:19
  75.8 7.5 %collective-permute-start.1 = (f32[5,16,4,128]{3,2,1,0:T(4,128)S(1)}, f32[5,16,4,128]{3,2,1,0:T(4,128)S(1)}, u32[]{:S(2)}, u32[]{:S(2)}) collective-permute-start(f32[5,16,4,128]{3,2,1,0:T(4,128)S(1)} %get-tuple-element.8), channel_id=1, source_target_pairs={{0,4},{4,8},{8,12},{12,16},{16,20},{20,24},{24,28},{28,32},{32,36}... | collective-permute-start | bytes 491528 | tf_op jit(solution)/shard_map/ppermute | solution.py:18
  78.1 5.3 %copy-start.5 = (f32[5,16,4,128]{3,2,1,0:T(4,128)}, f32[5,16,4,128]{3,2,1,0:T(4,128)S(1)}, u32[]{:S(2)}) copy-start(f32[5,16,4,128]{3,2,1,0:T(4,128)S(1)} %collective-permute-done) | copy-start | bytes 491524
  83.3 0.7 copy-start.6
  91.3 10.8 %collective-permute-start.2 = (f32[5,16,80,4]{2,1,3,0:T(8,128)}, f32[5,16,80,4]{2,1,3,0:T(8,128)}, u32[]{:S(2)}, u32[]{:S(2)}) collective-permute-start(f32[5,16,80,4]{2,1,3,0:T(8,128)} %copy.18), channel_id=1, source_target_pairs={{1,0},{2,1},{3,2},{5,4},{6,5},{7,6},{9,8},{10,9},{11,10},{13,12},{... | collective-permute-start | bytes 307208 | tf_op jit(solution)/shard_map/ppermute | solution.py:24
  100.1 5.2 %collective-permute-start.3 = (f32[5,16,80,4]{2,1,3,0:T(8,128)}, f32[5,16,80,4]{2,1,3,0:T(8,128)}, u32[]{:S(2)}, u32[]{:S(2)}) collective-permute-start(f32[5,16,80,4]{2,1,3,0:T(8,128)} %copy.19), channel_id=1, source_target_pairs={{0,1},{1,2},{2,3},{4,5},{5,6},{6,7},{8,9},{9,10},{10,11},{12,13},{... | collective-permute-start | bytes 307208 | tf_op jit(solution)/shard_map/ppermute | solution.py:25
  129.8 30.8 %copy-start.4 = (f32[2,64,2,64]{3,2,1,0:T(2,128)S(1)}, f32[2,64,2,64]{3,2,1,0:T(2,128)}, u32[]{:S(2)}) copy-start(f32[2,64,2,64]{3,2,1,0:T(2,128)} %copy-done.3) | copy-start | bytes 196612
  161.6 26.2 %copy-start.2 = (f32[2,16,64,128]{3,2,1,0:T(8,128)S(1)}, f32[2,16,64,128]{3,2,1,0:T(8,128)}, u32[]{:S(2)}) copy-start(f32[2,16,64,128]{3,2,1,0:T(8,128)} %param.7) | copy-start | bytes 3145732

commit v3 on v2

--- a/solution.py
+++ b/solution.py
@@ -46,7 +46,7 @@
 
 def diffusion(values, coefs, steps):
     fields, levels, rows, cols = values.shape
-    ext = circular(jnp.concatenate([values, coefs]), steps)
+    ext = jnp.concatenate([circular(values, steps), coefs])
     height, span = ext.shape[2], ext.shape[3]
     return pl.pallas_call(
         functools.partial(diffusion_kernel, steps, rows, cols),
@@ -80,8 +80,11 @@
     balance = jnp.eye(order_count, dtype=jnp.float32) + coupling
     forward = balance.reshape(2, level_count, 2, level_count)
     adjoint = jnp.transpose(forward, (2, 3, 0, 1))
-    coefs = jnp.stack([diffusion_i, diffusion_j, ocean])
-    adjoint_mixed = level_mix(scaled, adjoint) * ocean[None]
+    coefs = circular(jnp.stack([diffusion_i, diffusion_j, ocean]), steps)
+    columns = to_columns(scaled)
+    mixed = jnp.einsum("abcd,cdij->abij", adjoint, columns, precision=lax.Precision.HIGHEST)
+    coefs, mixed = lax.optimization_barrier((coefs, mixed))
+    adjoint_mixed = to_levels(mixed) * ocean[None]
     spread = diffusion(adjoint_mixed, coefs, steps)
     forward_mixed = level_mix(spread, forward)
     return ocean[None] * norm_gain * forward_mixed

time: 192 us -> 190 us (0.990)
  waiting for transfers between devices: 30.9 us -> 14.9 us
  starting transfers between devices: 21.6 us -> 28.1 us
  other arithmetic: 10.2 us -> 14.1 us
  local copies, waits for them, and re-layouts: 22.7 us -> 24.9 us
    all_to_all x1, waiting for transfers between devices: 23.4 us -> 0.01 us  [to_columns(): return lax.all_to_all(x, 'lev', 2, 1, tiled=True)]
    ppermute x1 -> x2, starting transfers between devices: 1.91 us -> 8.74 us  [circular(): west = lax.ppermute(tall[..., cols - width:], 'gy', right)]
    concatenate x0 -> x1, other arithmetic: none -> 4.96 us  [diffusion(): ext = jnp.concatenate([circular(values, steps), coefs])]
    ppermute x1 -> x2, waiting for transfers between devices: 5.22 us -> 8.56 us  [circular(): north = lax.ppermute(x[:, :, rows - width:], 'gx', up)]
    ppermute x1 -> x2, waiting for transfers between devices: 0.01 us -> 2.46 us  [circular(): east = lax.ppermute(tall[..., :width], 'gy', left)]
    ppermute x1 -> x2, starting transfers between devices: 5.63 us -> 3.85 us  [circular(): east = lax.ppermute(tall[..., :width], 'gy', left)]
    ppermute x1 -> x2, local copies, waits for them, and re-layouts: 3.22 us -> 4.35 us  [circular(): west = lax.ppermute(tall[..., cols - width:], 'gy', right)]
    slice x2 -> x4, local copies, waits for them, and re-layouts: 6.96 us -> 7.96 us  [circular(): east = lax.ppermute(tall[..., :width], 'gy', left)]
  transfers between devices with their start and end apart: 5 -> 9, of which waited for: 3 -> 6; matrix products, arithmetic and copies ran while one was open for 4% -> 9% of each run, Pallas kernels for 0% -> 0%
where the time goes in v3:
time: 190 us; the launch traced here: 187 us
  blocking collectives  86.8 us (46%)
  starting transfers between devices  28.1 us (15%)
  local copies, waits for them, and re-layouts  24.9 us (13%)
  Pallas kernels  15.8 us (8%)
  waiting for transfers between devices  14.9 us (8%)
  other arithmetic  14.1 us (7%)
  matrix products  2.11 us (1%)
    all_to_all x2, blocking collectives, to_levels(): return lax.all_to_all(x, 'lev', 1, 2, tiled=True)  57.2 us
    all_to_all x1, blocking collectives, to_columns(): return lax.all_to_all(x, 'lev', 2, 1, tiled=True)  29.6 us
    pallas_call x1, Pallas kernels, diffusion(): pl.pallas_call(functools.partial(diffusion_kernel, steps, rows, cols), ou...  15.8 us
    all_to_all x1, starting transfers between devices, to_columns(): return lax.all_to_all(x, 'lev', 2, 1, tiled=True)  9.01 us
    ppermute x2, starting transfers between devices, circular(): west = lax.ppermute(tall[..., cols - width:], 'gy', right)  8.74 us
    ppermute x2, waiting for transfers between devices, circular(): north = lax.ppermute(x[:, :, rows - width:], 'gx', up)  8.56 us
    slice x4, local copies, waits for them, and re-layouts, circular(): east = lax.ppermute(tall[..., :width], 'gy', left)  7.96 us
    ppermute x2, starting transfers between devices, circular(): south = lax.ppermute(x[:, :, :width], 'gx', down)  5.09 us
  transfers between devices with their start and end apart: 9, of which 6 were waited for; matrix products, arithmetic and copies ran while one was open for 9% of the time, Pallas kernels for 0%

profile of v3, /device:TPU:1, one launch (start us, length us, event | category | flops | bytes accessed | tf_op | source)
XLA Modules:
  0.0 187.0 jit_solution(11855459950468774213)
XLA Ops:
  0.0 1.2 fusion.5
  1.3 0.1 copy-done.2
  1.4 1.5 multiply_multiply_fusion
  2.9 1.6 copy.18
  4.5 9.0 %all-to-all-start = ((f32[2,16,64,128]{3,1,0,2:T(8,128)}), f32[2,16,64,128]{3,1,0,2:T(8,128)}, u32[]{:S(2)}, u32[]{:S(2)}) async-start(f32[2,16,64,128]{3,1,0,2:T(8,128)} %copy.18), calls=%async_computation | async-start | bytes 2097152 | tf_op jit(solution)/shard_map/all_to_all | solution.py:61
  13.5 5.0 %collective-permute-start = (f32[3,16,4,128]{3,2,1,0:T(4,128)S(1)}, f32[3,16,4,128]{3,2,1,0:T(4,128)S(1)}, u32[]{:S(2)}, u32[]{:S(2)}) collective-permute-start(f32[3,16,4,128]{3,2,1,0:T(4,128)S(1)} %get-tuple-element.11), channel_id=1, source_target_pairs={{4,0},{8,4},{12,8},{16,12},{20,16},{24,20},{28,24},{32,28},{36,32}... | collective-permute-start | bytes 294920 | tf_op jit(solution)/shard_map/ppermute | solution.py:19
  18.5 1.6 collective-permute-done
  20.2 5.1 %collective-permute-done.1 = f32[3,16,4,128]{3,2,1,0:T(4,128)S(1)} collective-permute-done((f32[3,16,4,128]{3,2,1,0:T(4,128)S(1)}, f32[3,16,4,128]{3,2,1,0:T(4,128)S(1)}, u32[]{:S(2)}, u32[]{:S(2)}) %collective-permute-start.1) | collective-permute-done | bytes 98336 | tf_op jit(solution)/shard_map/ppermute | solution.py:18
  25.3 0.6 copy-done.9
  26.0 0.7 copy-done.4
  26.6 0.2 pad_maximum_fusion.2
  26.8 1.9 %fusion.2 = (f32[3,16,80,4]{3,2,1,0:T(8,128)}, f32[3,16,80,4]{3,2,1,0:T(8,128)S(1)}) fusion(f32[3,16,80,128]{3,2,1,0:T(8,128)S(1)} %pad_maximum_fusion.2), kind=kLoop, calls=%fused_computation.17 | loop fusion | bytes 245760 | tf_op jit(solution)/shard_map/slice | solution.py:24
  28.8 2.8 %copy.13 = f32[3,16,80,4]{2,1,3,0:T(8,128)} copy(f32[3,16,80,4]{3,2,1,0:T(8,128)} %get-tuple-element.9) | data formatting | bytes 122880 | tf_op jit(solution)/shard_map/slice | solution.py:24
  31.6 1.2 copy.14
  32.8 4.9 %collective-permute-start.3 = (f32[3,16,80,4]{2,1,3,0:T(8,128)}, f32[3,16,80,4]{2,1,3,0:T(8,128)}, u32[]{:S(2)}, u32[]{:S(2)}) collective-permute-start(f32[3,16,80,4]{2,1,3,0:T(8,128)} %copy.14), channel_id=1, source_target_pairs={{0,1},{1,2},{2,3},{4,5},{5,6},{6,7},{8,9},{9,10},{10,11},{12,13},{... | collective-permute-start | bytes 184328 | tf_op jit(solution)/shard_map/ppermute | solution.py:25
  37.7 1.9 %collective-permute-start.2 = (f32[3,16,80,4]{2,1,3,0:T(8,128)}, f32[3,16,80,4]{2,1,3,0:T(8,128)}, u32[]{:S(2)}, u32[]{:S(2)}) collective-permute-start(f32[3,16,80,4]{2,1,3,0:T(8,128)} %copy.13), channel_id=1, source_target_pairs={{1,0},{2,1},{3,2},{5,4},{6,5},{7,6},{9,8},{10,9},{11,10},{13,12},{... | collective-permute-start | bytes 184328 | tf_op jit(solution)/shard_map/ppermute | solution.py:24
  39.7 0.9 convert_add_fusion
  40.5 0.1 reshape.4
  40.7 0.8 copy.17
  41.5 2.5 %collective-permute-done.2 = f32[3,16,80,4]{2,1,3,0:T(8,128)} collective-permute-done((f32[3,16,80,4]{2,1,3,0:T(8,128)}, f32[3,16,80,4]{2,1,3,0:T(8,128)}, u32[]{:S(2)}, u32[]{:S(2)}) %collective-permute-start.2) | collective-permute-done | bytes 61472 | tf_op jit(solution)/shard_map/ppermute | solution.py:24
  44.0 1.5 copy.15
  45.5 2.8 %copy.16 = f32[3,16,80,4]{3,2,1,0:T(8,128)} copy(f32[3,16,80,4]{2,1,3,0:T(8,128)} %collective-permute-done.3) | data formatting | bytes 122880 | tf_op jit(solution)/shard_map/ppermute | solution.py:25
  48.3 3.8 %pad_maximum_fusion.1 = f32[3,16,80,256]{3,2,1,0:T(8,128)} fusion(f32[3,16,80,4]{3,2,1,0:T(8,128)} %copy.16, f32[3,16,80,4]{3,2,1,0:T(8,128)S(1)} %copy.15, f32[3,16,4,128]{3,2,1,0:T(4,128)} %copy-done.9, f32[3,16,8,128]{3,2,1,0:T(8,128)} %copy-done.4, f32[3,16,4,128]{3,2,1,0:T(4,128)} %copy-done.8, f32[1,16,64,128]{3,2,1,0:T(8,128)S(1)} %get-tuple-element.18, ...), kind=kLoop, calls=%fused_computation.1 | loop fusion | flops 7864320 | bytes 6022144 | tf_op jit(solution)/shard_map/concatenate | solution.py:27
  52.2 1.4 copy.19
  53.6 1.1 convolution_bitcast_fusion.1
  54.6 0.6 copy.20
  55.3 32.5 %all_to_all.72 = f32[2,64,16,128]{3,2,0,1:T(8,128)S(1)} all-to-all(f32[2,64,16,128]{3,2,0,1:T(8,128)S(1)} %copy.20), channel_id=1, replica_groups=mesh['lev'=4,'gx'=16,'gy'=4] {'lev'}, dimensions={1} | all-to-all | bytes 2097152 | tf_op jit(solution)/shard_map/all_to_all | solution.py:65
  87.9 0.1 bitcast_multiply_fusion.1
  88.2 1.5 collective-permute-start.5
  89.7 1.6 collective-permute-done.4
  91.3 3.4 %collective-permute-done.5 = f32[2,16,4,128]{3,2,1,0:T(4,128)S(1)} collective-permute-done((f32[2,16,4,128]{3,2,1,0:T(4,128)S(1)}, f32[2,16,4,128]{3,2,1,0:T(4,128)S(1)}, u32[]{:S(2)}, u32[]{:S(2)}) %collective-permute-start.5) | collective-permute-done | bytes 65568 | tf_op jit(solution)/shard_map/ppermute | solution.py:18
  94.8 1.5 fusion.3
  96.3 1.7 copy.22
  98.1 1.9 %collective-permute-start.6 = (f32[2,16,80,4]{2,1,3,0:T(8,128)S(1)}, f32[2,16,80,4]{2,1,3,0:T(8,128)S(1)}, u32[]{:S(2)}, u32[]{:S(2)}) collective-permute-start(f32[2,16,80,4]{2,1,3,0:T(8,128)S(1)} %copy.22), channel_id=1, source_target_pairs={{1,0},{2,1},{3,2},{5,4},{6,5},{7,6},{9,8},{10,9},{11,10},{13,12},{... | collective-permute-start | bytes 122888 | tf_op jit(solution)/shard_map/ppermute | solution.py:24
  100.0 0.4 copy.23
  100.4 3.8 %collective-permute-start.7 = (f32[2,16,80,4]{2,1,3,0:T(8,128)S(1)}, f32[2,16,80,4]{2,1,3,0:T(8,128)S(1)}, u32[]{:S(2)}, u32[]{:S(2)}) collective-permute-start(f32[2,16,80,4]{2,1,3,0:T(8,128)S(1)} %copy.23), channel_id=1, source_target_pairs={{0,1},{1,2},{2,3},{4,5},{5,6},{6,7},{8,9},{9,10},{10,11},{12,13},{... | collective-permute-start | bytes 122888 | tf_op jit(solution)/shard_map/ppermute | solution.py:25
  104.3 0.5 copy.24
  104.8 0.6 collective-permute-done.7
  105.4 1.5 copy.25
  106.9 5.0 %pad_maximum_fusion.v_ref = f32[5,16,80,256]{3,2,1,0:T(8,128)} fusion(f32[3,16,80,256]{3,2,1,0:T(8,128)} %pad_maximum_fusion.1, f32[2,16,80,4]{3,2,1,0:T(8,128)} %copy.25, f32[2,16,80,4]{3,2,1,0:T(8,128)S(1)} %copy.24, f32[2,16,4,128]{3,2,1,0:T(4,128)S(1)} %collective-permute-done.5, f32[2,16,8,128]{3,2,1,0:T(8,128)S(1)} %broadcast_in_dim.20, ...), kind=kLoop, calls=%fused_computation | loop fusion | flops 11468800 | bytes 11883520 | tf_op jit(solution)/shard_map/concatenate | solution.py:49
  111.9 15.8 %shard_map.64 = f32[2,16,64,128]{3,2,1,0:T(8,128)} custom-call(f32[5,16,80,256]{3,2,1,0:T(8,128)} %pad_maximum_fusion.v_ref), custom_call_target="tpu_custom_call" | custom-call | tf_op jit(solution)/shard_map/pallas_call | solution.py:51
  127.7 1.8 copy.26
  129.5 29.6 %all_to_all.73 = f32[2,16,64,128]{3,1,0,2:T(8,128)S(1)} all-to-all(f32[2,16,64,128]{3,1,0,2:T(8,128)S(1)} %copy.26), channel_id=1, replica_groups=mesh['lev'=4,'gx'=16,'gy'=4] {'lev'}, dimensions={2} | all-to-all | bytes 2097152 | tf_op jit(solution)/shard_map/all_to_all | solution.py:61
  159.1 0.1 copy.27
  159.3 1.1 convolution_bitcast_fusion
  160.3 0.6 copy.29
  160.9 24.7 %all_to_all.74 = f32[2,64,16,128]{3,2,0,1:T(8,128)S(1)} all-to-all(f32[2,64,16,128]{3,2,0,1:T(8,128)S(1)} %copy.29), channel_id=1, replica_groups=mesh['lev'=4,'gx'=16,'gy'=4] {'lev'}, dimensions={1} | all-to-all | bytes 2097152 | tf_op jit(solution)/shard_map/all_to_all | solution.py:65
  185.8 1.2 bitcast_multiply_fusion
  (33 shorter events, 0.7 us)
Async XLA Ops:
  0.0 1.4 copy-start.2
  2.9 10.6 %copy-start = (f32[16,64,128]{2,1,0:T(8,128)S(1)}, f32[16,64,128]{2,1,0:T(8,128)}, u32[]{:S(2)}) copy-start(f32[16,64,128]{2,1,0:T(8,128)} %param.9) | copy-start | bytes 1572868
  2.9 10.6 %copy-start.1 = (f32[16,64,128]{2,1,0:T(8,128)S(1)}, f32[16,64,128]{2,1,0:T(8,128)}, u32[]{:S(2)}) copy-start(f32[16,64,128]{2,1,0:T(8,128)} %param.8) | copy-start | bytes 1572868
  4.5 47.7 %all-to-all-start = ((f32[2,16,64,128]{3,1,0,2:T(8,128)}), f32[2,16,64,128]{3,1,0,2:T(8,128)}, u32[]{:S(2)}, u32[]{:S(2)}) async-start(f32[2,16,64,128]{3,1,0,2:T(8,128)} %copy.18), calls=%async_computation | async-start | bytes 2097152 | tf_op jit(solution)/shard_map/all_to_all | solution.py:61
  13.5 6.6 %collective-permute-start = (f32[3,16,4,128]{3,2,1,0:T(4,128)S(1)}, f32[3,16,4,128]{3,2,1,0:T(4,128)S(1)}, u32[]{:S(2)}, u32[]{:S(2)}) collective-permute-start(f32[3,16,4,128]{3,2,1,0:T(4,128)S(1)} %get-tuple-element.11), channel_id=1, source_target_pairs={{4,0},{8,4},{12,8},{16,12},{20,16},{24,20},{28,24},{32,28},{36,32}... | collective-permute-start | bytes 294920 | tf_op jit(solution)/shard_map/ppermute | solution.py:19
  18.5 6.8 %collective-permute-start.1 = (f32[3,16,4,128]{3,2,1,0:T(4,128)S(1)}, f32[3,16,4,128]{3,2,1,0:T(4,128)S(1)}, u32[]{:S(2)}, u32[]{:S(2)}) collective-permute-start(f32[3,16,4,128]{3,2,1,0:T(4,128)S(1)} %get-tuple-element.12), channel_id=1, source_target_pairs={{0,4},{4,8},{8,12},{12,16},{16,20},{20,24},{24,28},{28,32},{32,36}... | collective-permute-start | bytes 294920 | tf_op jit(solution)/shard_map/ppermute | solution.py:18
  20.2 5.2 %copy-start.8 = (f32[3,16,4,128]{3,2,1,0:T(4,128)}, f32[3,16,4,128]{3,2,1,0:T(4,128)S(1)}, u32[]{:S(2)}) copy-start(f32[3,16,4,128]{3,2,1,0:T(4,128)S(1)} %collective-permute-done) | copy-start | bytes 294916
  25.3 0.6 copy-start.9
  25.9 0.7 copy-start.4
  32.8 12.7 %collective-permute-start.3 = (f32[3,16,80,4]{2,1,3,0:T(8,128)}, f32[3,16,80,4]{2,1,3,0:T(8,128)}, u32[]{:S(2)}, u32[]{:S(2)}) collective-permute-start(f32[3,16,80,4]{2,1,3,0:T(8,128)} %copy.14), channel_id=1, source_target_pairs={{0,1},{1,2},{2,3},{4,5},{5,6},{6,7},{8,9},{9,10},{10,11},{12,13},{... | collective-permute-start | bytes 184328 | tf_op jit(solution)/shard_map/ppermute | solution.py:25
  37.7 6.3 %collective-permute-start.2 = (f32[3,16,80,4]{2,1,3,0:T(8,128)}, f32[3,16,80,4]{2,1,3,0:T(8,128)}, u32[]{:S(2)}, u32[]{:S(2)}) collective-permute-start(f32[3,16,80,4]{2,1,3,0:T(8,128)} %copy.13), channel_id=1, source_target_pairs={{1,0},{2,1},{3,2},{5,4},{6,5},{7,6},{9,8},{10,9},{11,10},{13,12},{... | collective-permute-start | bytes 184328 | tf_op jit(solution)/shard_map/ppermute | solution.py:24
  40.7 0.9 copy-start.5
  52.2 1.4 copy-start.7
  88.1 3.2 %collective-permute-start.4 = (f32[2,16,4,128]{3,2,1,0:T(4,128)S(1)}, f32[2,16,4,128]{3,2,1,0:T(4,128)S(1)}, u32[]{:S(2)}, u32[]{:S(2)}) collective-permute-start(f32[2,16,4,128]{3,2,1,0:T(4,128)S(1)} %get-tuple-element.15), channel_id=1, source_target_pairs={{4,0},{8,4},{12,8},{16,12},{20,16},{24,20},{28,24},{32,28},{36,32}... | collective-permute-start | bytes 196616 | tf_op jit(solution)/shard_map/ppermute | solution.py:19
  88.2 6.5 %collective-permute-start.5 = (f32[2,16,4,128]{3,2,1,0:T(4,128)S(1)}, f32[2,16,4,128]{3,2,1,0:T(4,128)S(1)}, u32[]{:S(2)}, u32[]{:S(2)}) collective-permute-start(f32[2,16,4,128]{3,2,1,0:T(4,128)S(1)} %get-tuple-element.16), channel_id=1, source_target_pairs={{0,4},{4,8},{8,12},{12,16},{16,20},{20,24},{24,28},{28,32},{32,36}... | collective-permute-start | bytes 196616 | tf_op jit(solution)/shard_map/ppermute | solution.py:18
  98.1 6.3 %collective-permute-start.6 = (f32[2,16,80,4]{2,1,3,0:T(8,128)S(1)}, f32[2,16,80,4]{2,1,3,0:T(8,128)S(1)}, u32[]{:S(2)}, u32[]{:S(2)}) collective-permute-start(f32[2,16,80,4]{2,1,3,0:T(8,128)S(1)} %copy.22), channel_id=1, source_target_pairs={{1,0},{2,1},{3,2},{5,4},{6,5},{7,6},{9,8},{10,9},{11,10},{13,12},{... | collective-permute-start | bytes 122888 | tf_op jit(solution)/shard_map/ppermute | solution.py:24
  100.4 5.0 %collective-permute-start.7 = (f32[2,16,80,4]{2,1,3,0:T(8,128)S(1)}, f32[2,16,80,4]{2,1,3,0:T(8,128)S(1)}, u32[]{:S(2)}, u32[]{:S(2)}) collective-permute-start(f32[2,16,80,4]{2,1,3,0:T(8,128)S(1)} %copy.23), channel_id=1, source_target_pairs={{0,1},{1,2},{2,3},{4,5},{5,6},{6,7},{8,9},{9,10},{10,11},{12,13},{... | collective-permute-start | bytes 122888 | tf_op jit(solution)/shard_map/ppermute | solution.py:25
  129.5 29.7 %copy-start.6 = (f32[2,64,2,64]{3,2,1,0:T(2,128)S(1)}, f32[2,64,2,64]{3,2,1,0:T(2,128)}, u32[]{:S(2)}) copy-start(f32[2,64,2,64]{3,2,1,0:T(2,128)} %copy-done.5) | copy-start | bytes 196612
  160.9 24.8 %copy-start.3 = (f32[2,16,64,128]{3,2,1,0:T(8,128)S(1)}, f32[2,16,64,128]{3,2,1,0:T(8,128)}, u32[]{:S(2)}) copy-start(f32[2,16,64,128]{3,2,1,0:T(8,128)} %param.7) | copy-start | bytes 3145732

commit v4 on v3

--- a/solution.py
+++ b/solution.py
@@ -8,6 +8,7 @@
 from jax.sharding import PartitionSpec as P
 
 ITERS = 2
+MESH = pl.DeviceIdType.MESH
 
 
 def circular(x, width):
@@ -57,11 +58,97 @@
     )(ext)
 
 
-def to_columns(x):
+def lev_exchange(x, src_axis, dst_axis, half_axis, collective):
+    n = lax.axis_size("lev")
+    assert half_axis == src_axis
+    out_shape = list(x.shape)
+    out_shape[src_axis] //= n
+    out_shape[dst_axis] *= n
+    src_size = out_shape[src_axis]
+    dst_size = x.shape[dst_axis]
+    half = src_size // 2
+    relay_shape = list(out_shape)
+    relay_shape[dst_axis] = dst_size
+    relay_shape[half_axis] = half
+
+    def window(axis, start, size, h=None):
+        index = [slice(None)] * x.ndim
+        index[axis] = pl.ds(start, size)
+        if h is not None:
+            if half_axis == axis:
+                index[axis] = pl.ds(start + h * half, half)
+            else:
+                index[half_axis] = pl.ds(h * half, half)
+        return tuple(index)
+
+    def kernel(x_ref, o_ref, relay, send_sem, recv_sem, local_sem):
+        me = lax.axis_index("lev")
+        gx = lax.axis_index("gx")
+        gy = lax.axis_index("gy")
+        right = (me + 1) % n
+        left = (me + n - 1) % n
+        opposite = (me + 2) % n
+        barrier = pltpu.get_barrier_semaphore()
+        for peer in (left, right):
+            pl.semaphore_signal(barrier, inc=1, device_id=(peer, gx, gy), device_id_type=MESH)
+        pl.semaphore_wait(barrier, 2)
+
+        def remote(src, dst, slot, peer):
+            return pltpu.make_async_remote_copy(
+                src_ref=src, dst_ref=dst, send_sem=send_sem.at[slot], recv_sem=recv_sem.at[slot],
+                device_id=(peer, gx, gy), device_id_type=MESH,
+            )
+
+        to_right = remote(x_ref.at[window(src_axis, right * src_size, src_size)],
+                          o_ref.at[window(dst_axis, me * dst_size, dst_size)], 0, right)
+        to_left = remote(x_ref.at[window(src_axis, left * src_size, src_size)],
+                         o_ref.at[window(dst_axis, me * dst_size, dst_size)], 1, left)
+        via_right = remote(x_ref.at[window(src_axis, opposite * src_size, src_size, 0)], relay.at[0], 2, right)
+        via_left = remote(x_ref.at[window(src_axis, opposite * src_size, src_size, 1)], relay.at[1], 3, left)
+        for copy in (via_right, via_left, to_right, to_left):
+            copy.start()
+        local = pltpu.make_async_copy(
+            x_ref.at[window(src_axis, me * src_size, src_size)],
+            o_ref.at[window(dst_axis, me * dst_size, dst_size)],
+            local_sem,
+        )
+        local.start()
+        via_right.wait_recv()
+        on_right = remote(relay.at[0], o_ref.at[window(dst_axis, left * dst_size, dst_size, 0)], 4, right)
+        on_right.start()
+        via_left.wait_recv()
+        on_left = remote(relay.at[1], o_ref.at[window(dst_axis, right * dst_size, dst_size, 1)], 5, left)
+        on_left.start()
+        local.wait()
+        via_right.wait_send()
+        via_left.wait_send()
+        for copy in (to_right, to_left, on_right, on_left):
+            copy.wait()
+
+    return pl.pallas_call(
+        kernel,
+        out_shape=jax.ShapeDtypeStruct(tuple(out_shape), x.dtype),
+        in_specs=[pl.BlockSpec(memory_space=pl.ANY)],
+        out_specs=pl.BlockSpec(memory_space=pl.ANY),
+        scratch_shapes=[
+            pltpu.VMEM((2,) + tuple(relay_shape), x.dtype),
+            pltpu.SemaphoreType.DMA((6,)),
+            pltpu.SemaphoreType.DMA((6,)),
+            pltpu.SemaphoreType.DMA,
+        ],
+        compiler_params=pltpu.CompilerParams(collective_id=collective, has_side_effects=True),
+    )(x)
+
+
+def to_columns(x, kernel=True):
+    if kernel:
+        return lev_exchange(x, 2, 1, 2, 0)
     return lax.all_to_all(x, "lev", 2, 1, tiled=True)
 
 
-def to_levels(x):
+def to_levels(x, kernel=True):
+    if kernel:
+        return lev_exchange(x, 1, 2, 1, 1)
     return lax.all_to_all(x, "lev", 1, 2, tiled=True)
 
 
@@ -81,7 +168,7 @@
     forward = balance.reshape(2, level_count, 2, level_count)
     adjoint = jnp.transpose(forward, (2, 3, 0, 1))
     coefs = circular(jnp.stack([diffusion_i, diffusion_j, ocean]), steps)
-    columns = to_columns(scaled)
+    columns = to_columns(scaled, False)
     mixed = jnp.einsum("abcd,cdij->abij", adjoint, columns, precision=lax.Precision.HIGHEST)
     coefs, mixed = lax.optimization_barrier((coefs, mixed))
     adjoint_mixed = to_levels(mixed) * ocean[None]

time: 190 us -> 177 us (0.932)
  the two profiles are of different devices: /device:TPU:1 before, /device:TPU:33 now
where the time goes in v4:
time: 177 us; the launch traced here: 176 us
  Pallas kernels  91.5 us (52%)
  starting transfers between devices  26.4 us (15%)
  local copies, waits for them, and re-layouts  24.7 us (14%)
  other arithmetic  16.4 us (9%)
  waiting for transfers between devices  13 us (7%)
  matrix products  3.56 us (2%)
    pallas_call x3, Pallas kernels, lev_exchange(): pl.pallas_call(kernel, out_shape=jax.ShapeDtypeStruct(tuple(out_shape), x...  75.7 us
    pallas_call x1, Pallas kernels, diffusion(): pl.pallas_call(functools.partial(diffusion_kernel, steps, rows, cols), ou...  15.8 us
    ppermute x2, starting transfers between devices, circular(): east = lax.ppermute(tall[..., :width], 'gy', left)  9.84 us
    ppermute x2, waiting for transfers between devices, circular(): north = lax.ppermute(x[:, :, rows - width:], 'gx', up)  8.56 us
    slice x4, local copies, waits for them, and re-layouts, circular(): east = lax.ppermute(tall[..., :width], 'gy', left)  7.96 us
    all_to_all x1, starting transfers between devices, to_columns(): return lax.all_to_all(x, 'lev', 2, 1, tiled=True)  7.28 us
    ppermute x2, starting transfers between devices, circular(): south = lax.ppermute(x[:, :, :width], 'gx', down)  5.09 us
    concatenate x1, other arithmetic, diffusion(): ext = jnp.concatenate([circular(values, steps), coefs])  4.96 us
  transfers between devices with their start and end apart: 9, of which 5 were waited for; matrix products, arithmetic and copies ran while one was open for 10% of the time, Pallas kernels for 0%

profile of v4, /device:TPU:33, one launch (start us, length us, event | category | flops | bytes accessed | tf_op | source)
XLA Modules:
  0.0 175.8 jit_solution(13513424189608357463)
XLA Ops:
  0.0 1.2 fusion.7
  1.3 0.1 copy-done.2
  1.4 1.5 multiply_multiply_fusion.1
  2.9 1.6 copy.18
  4.5 7.3 %all-to-all-start = ((f32[2,16,64,128]{3,1,0,2:T(8,128)}), f32[2,16,64,128]{3,1,0,2:T(8,128)}, u32[]{:S(2)}, u32[]{:S(2)}) async-start(f32[2,16,64,128]{3,1,0,2:T(8,128)} %copy.18), calls=%async_computation | async-start | bytes 2097152 | tf_op jit(solution)/shard_map/all_to_all | solution.py:146
  11.8 5.0 %collective-permute-start = (f32[3,16,4,128]{3,2,1,0:T(4,128)S(1)}, f32[3,16,4,128]{3,2,1,0:T(4,128)S(1)}, u32[]{:S(2)}, u32[]{:S(2)}) collective-permute-start(f32[3,16,4,128]{3,2,1,0:T(4,128)S(1)} %get-tuple-element.11), channel_id=1, source_target_pairs={{4,0},{8,4},{12,8},{16,12},{20,16},{24,20},{28,24},{32,28},{36,32}... | collective-permute-start | bytes 294920 | tf_op jit(solution)/shard_map/ppermute | solution.py:20
  16.8 1.6 collective-permute-done
  18.4 5.1 %collective-permute-done.1 = f32[3,16,4,128]{3,2,1,0:T(4,128)S(1)} collective-permute-done((f32[3,16,4,128]{3,2,1,0:T(4,128)S(1)}, f32[3,16,4,128]{3,2,1,0:T(4,128)S(1)}, u32[]{:S(2)}, u32[]{:S(2)}) %collective-permute-start.1) | collective-permute-done | bytes 98336 | tf_op jit(solution)/shard_map/ppermute | solution.py:19
  23.6 0.6 copy-done.9
  24.2 0.7 copy-done.4
  24.9 0.2 pad_maximum_fusion.2
  25.1 1.9 %fusion.4 = (f32[3,16,80,4]{3,2,1,0:T(8,128)}, f32[3,16,80,4]{3,2,1,0:T(8,128)S(1)}) fusion(f32[3,16,80,128]{3,2,1,0:T(8,128)S(1)} %pad_maximum_fusion.2), kind=kLoop, calls=%fused_computation.19 | loop fusion | bytes 245760 | tf_op jit(solution)/shard_map/slice | solution.py:25
  27.0 2.8 %copy.13 = f32[3,16,80,4]{2,1,3,0:T(8,128)} copy(f32[3,16,80,4]{3,2,1,0:T(8,128)} %get-tuple-element.9) | data formatting | bytes 122880 | tf_op jit(solution)/shard_map/slice | solution.py:25
  29.8 1.2 copy.14
  31.1 1.3 collective-permute-start.3
  32.4 5.6 %collective-permute-start.2 = (f32[3,16,80,4]{2,1,3,0:T(8,128)}, f32[3,16,80,4]{2,1,3,0:T(8,128)}, u32[]{:S(2)}, u32[]{:S(2)}) collective-permute-start(f32[3,16,80,4]{2,1,3,0:T(8,128)} %copy.13), channel_id=1, source_target_pairs={{1,0},{2,1},{3,2},{5,4},{6,5},{7,6},{9,8},{10,9},{11,10},{13,12},{... | collective-permute-start | bytes 184328 | tf_op jit(solution)/shard_map/ppermute | solution.py:25
  37.9 0.9 convert_add_fusion
  38.8 0.1 reshape.4
  38.9 0.8 copy.17
  39.7 0.1 pad.19.clone
  39.8 1.5 copy.15
  41.3 2.8 %copy.16 = f32[3,16,80,4]{3,2,1,0:T(8,128)} copy(f32[3,16,80,4]{2,1,3,0:T(8,128)} %collective-permute-done.3) | data formatting | bytes 122880 | tf_op jit(solution)/shard_map/ppermute | solution.py:26
  44.2 3.8 %pad_maximum_fusion.1 = f32[3,16,80,256]{3,2,1,0:T(8,128)} fusion(f32[3,16,80,4]{3,2,1,0:T(8,128)} %copy.16, f32[3,16,80,4]{3,2,1,0:T(8,128)S(1)} %copy.15, f32[3,16,4,128]{3,2,1,0:T(4,128)} %copy-done.9, f32[3,16,8,128]{3,2,1,0:T(8,128)} %copy-done.4, f32[3,16,4,128]{3,2,1,0:T(4,128)} %copy-done.8, f32[1,16,64,128]{3,2,1,0:T(8,128)S(1)} %get-tuple-element.18, ...), kind=kLoop, calls=%fused_computation.1 | loop fusion | flops 7864320 | bytes 6022144 | tf_op jit(solution)/shard_map/concatenate | solution.py:28
  48.0 1.4 copy.19
  49.4 1.1 convolution_bitcast_fusion.1
  50.5 1.6 copy.20.x_ref
  52.1 29.3 %shard_map.64 = f32[2,16,64,128]{3,2,1,0:T(8,128)} custom-call(f32[2,64,16,128]{3,2,1,0:T(8,128)} %copy.20.x_ref), custom_call_target="tpu_custom_call" | custom-call | tf_op jit(solution)/shard_map/pallas_call | solution.py:128
  81.3 1.3 broadcast_multiply_fusion
  82.7 0.1 collective-permute-start.4
  82.8 1.5 collective-permute-start.5
  84.2 1.6 collective-permute-done.4
  85.9 3.4 %collective-permute-done.5 = f32[2,16,4,128]{3,2,1,0:T(4,128)S(1)} collective-permute-done((f32[2,16,4,128]{3,2,1,0:T(4,128)S(1)}, f32[2,16,4,128]{3,2,1,0:T(4,128)S(1)}, u32[]{:S(2)}, u32[]{:S(2)}) %collective-permute-start.5) | collective-permute-done | bytes 65568 | tf_op jit(solution)/shard_map/ppermute | solution.py:19
  89.3 0.1 pad_maximum_fusion.3
  89.4 1.5 fusion.5
  90.9 1.7 copy.21
  92.6 4.3 %collective-permute-start.6 = (f32[2,16,80,4]{2,1,3,0:T(8,128)S(1)}, f32[2,16,80,4]{2,1,3,0:T(8,128)S(1)}, u32[]{:S(2)}, u32[]{:S(2)}) collective-permute-start(f32[2,16,80,4]{2,1,3,0:T(8,128)S(1)} %copy.21), channel_id=1, source_target_pairs={{1,0},{2,1},{3,2},{5,4},{6,5},{7,6},{9,8},{10,9},{11,10},{13,12},{... | collective-permute-start | bytes 122888 | tf_op jit(solution)/shard_map/ppermute | solution.py:25
  96.9 0.4 copy.22
  97.3 1.5 collective-permute-start.7
  98.9 0.5 copy.23
  99.4 1.1 collective-permute-done.7
  100.5 1.5 copy.24
  102.0 5.0 %pad_maximum_fusion.v_ref = f32[5,16,80,256]{3,2,1,0:T(8,128)} fusion(f32[3,16,80,256]{3,2,1,0:T(8,128)} %pad_maximum_fusion.1, f32[2,16,80,4]{3,2,1,0:T(8,128)} %copy.24, f32[2,16,80,4]{3,2,1,0:T(8,128)S(1)} %copy.23, f32[2,16,4,128]{3,2,1,0:T(4,128)S(1)} %collective-permute-done.5, f32[2,16,8,128]{3,2,1,0:T(8,128)S(1)} %broadcast_in_dim.20, ...), kind=kLoop, calls=%fused_computation | loop fusion | flops 11468800 | bytes 11883520 | tf_op jit(solution)/shard_map/concatenate | solution.py:50
  107.0 15.8 %shard_map.65.x_ref = f32[2,16,64,128]{3,2,1,0:T(8,128)} custom-call(f32[5,16,80,256]{3,2,1,0:T(8,128)} %pad_maximum_fusion.v_ref), custom_call_target="tpu_custom_call" | custom-call | tf_op jit(solution)/shard_map/pallas_call | solution.py:52
  122.8 27.3 %shard_map.66 = f32[2,64,16,128]{3,2,1,0:T(8,128)} custom-call(f32[2,16,64,128]{3,2,1,0:T(8,128)} %shard_map.65.x_ref), custom_call_target="tpu_custom_call" | custom-call | tf_op jit(solution)/shard_map/pallas_call | solution.py:128
  150.1 2.5 %convolution_bitcast_fusion = f32[2,64,16,128]{3,1,2,0:T(8,128)S(1)} fusion(f32[2,64,16,128]{3,2,1,0:T(8,128)} %shard_map.66, f32[2,64,2,64,1]{3,2,1,0,4:T(2,128)S(1)} %bitcast.35), kind=kOutput, calls=%fused_computation.3 | convolution fusion | flops 402653184 | bytes 2162688 | tf_op jit(solution)/shard_map/abcd,cdij->abij/dot_general | solution.py:157
  152.6 1.6 copy.27.x_ref
  154.2 19.2 %shard_map.67 = f32[2,16,64,128]{3,2,1,0:T(8,128)} custom-call(f32[2,64,16,128]{3,2,1,0:T(8,128)} %copy.27.x_ref), custom_call_target="tpu_custom_call" | custom-call | tf_op jit(solution)/shard_map/pallas_call | solution.py:128
  173.4 2.4 %multiply_multiply_fusion = f32[2,16,64,128]{3,2,1,0:T(8,128)} fusion(f32[2,16,64,128]{3,2,1,0:T(8,128)} %shard_map.67, f32[2,16,64,128]{3,2,1,0:T(8,128)S(1)} %copy-done.3, f32[16,64,128]{2,1,0:T(8,128)S(1)} %get-tuple-element.17), kind=kLoop, calls=%fused_computation.8 | loop fusion | flops 524288 | bytes 3670016 | tf_op jit(solution)/shard_map/mul | solution.py:177
  (29 shorter events, 0.2 us)
Async XLA Ops:
  0.0 1.4 copy-start.2
  2.9 8.9 %copy-start = (f32[16,64,128]{2,1,0:T(8,128)S(1)}, f32[16,64,128]{2,1,0:T(8,128)}, u32[]{:S(2)}) copy-start(f32[16,64,128]{2,1,0:T(8,128)} %param.9) | copy-start | bytes 1572868
  2.9 8.9 %copy-start.1 = (f32[16,64,128]{2,1,0:T(8,128)S(1)}, f32[16,64,128]{2,1,0:T(8,128)}, u32[]{:S(2)}) copy-start(f32[16,64,128]{2,1,0:T(8,128)} %param.8) | copy-start | bytes 1572868
  4.5 43.5 %all-to-all-start = ((f32[2,16,64,128]{3,1,0,2:T(8,128)}), f32[2,16,64,128]{3,1,0,2:T(8,128)}, u32[]{:S(2)}, u32[]{:S(2)}) async-start(f32[2,16,64,128]{3,1,0,2:T(8,128)} %copy.18), calls=%async_computation | async-start | bytes 2097152 | tf_op jit(solution)/shard_map/all_to_all | solution.py:146
  11.8 6.6 %collective-permute-start = (f32[3,16,4,128]{3,2,1,0:T(4,128)S(1)}, f32[3,16,4,128]{3,2,1,0:T(4,128)S(1)}, u32[]{:S(2)}, u32[]{:S(2)}) collective-permute-start(f32[3,16,4,128]{3,2,1,0:T(4,128)S(1)} %get-tuple-element.11), channel_id=1, source_target_pairs={{4,0},{8,4},{12,8},{16,12},{20,16},{24,20},{28,24},{32,28},{36,32}... | collective-permute-start | bytes 294920 | tf_op jit(solution)/shard_map/ppermute | solution.py:20
  16.8 6.8 %collective-permute-start.1 = (f32[3,16,4,128]{3,2,1,0:T(4,128)S(1)}, f32[3,16,4,128]{3,2,1,0:T(4,128)S(1)}, u32[]{:S(2)}, u32[]{:S(2)}) collective-permute-start(f32[3,16,4,128]{3,2,1,0:T(4,128)S(1)} %get-tuple-element.12), channel_id=1, source_target_pairs={{0,4},{4,8},{8,12},{12,16},{16,20},{20,24},{24,28},{28,32},{32,36}... | collective-permute-start | bytes 294920 | tf_op jit(solution)/shard_map/ppermute | solution.py:19
  18.4 5.2 %copy-start.8 = (f32[3,16,4,128]{3,2,1,0:T(4,128)}, f32[3,16,4,128]{3,2,1,0:T(4,128)S(1)}, u32[]{:S(2)}) copy-start(f32[3,16,4,128]{3,2,1,0:T(4,128)S(1)} %collective-permute-done) | copy-start | bytes 294916
  23.6 0.6 copy-start.9
  24.2 0.7 copy-start.4
  31.1 10.2 %collective-permute-start.3 = (f32[3,16,80,4]{2,1,3,0:T(8,128)}, f32[3,16,80,4]{2,1,3,0:T(8,128)}, u32[]{:S(2)}, u32[]{:S(2)}) collective-permute-start(f32[3,16,80,4]{2,1,3,0:T(8,128)} %copy.14), channel_id=1, source_target_pairs={{0,1},{1,2},{2,3},{4,5},{5,6},{6,7},{8,9},{9,10},{10,11},{12,13},{... | collective-permute-start | bytes 184328 | tf_op jit(solution)/shard_map/ppermute | solution.py:26
  32.4 7.4 %collective-permute-start.2 = (f32[3,16,80,4]{2,1,3,0:T(8,128)}, f32[3,16,80,4]{2,1,3,0:T(8,128)}, u32[]{:S(2)}, u32[]{:S(2)}) collective-permute-start(f32[3,16,80,4]{2,1,3,0:T(8,128)} %copy.13), channel_id=1, source_target_pairs={{1,0},{2,1},{3,2},{5,4},{6,5},{7,6},{9,8},{10,9},{11,10},{13,12},{... | collective-permute-start | bytes 184328 | tf_op jit(solution)/shard_map/ppermute | solution.py:25
  38.9 0.9 copy-start.5
  48.0 1.4 copy-start.7
  82.7 3.2 %collective-permute-start.4 = (f32[2,16,4,128]{3,2,1,0:T(4,128)S(1)}, f32[2,16,4,128]{3,2,1,0:T(4,128)S(1)}, u32[]{:S(2)}, u32[]{:S(2)}) collective-permute-start(f32[2,16,4,128]{3,2,1,0:T(4,128)S(1)} %get-tuple-element.15), channel_id=1, source_target_pairs={{4,0},{8,4},{12,8},{16,12},{20,16},{24,20},{28,24},{32,28},{36,32}... | collective-permute-start | bytes 196616 | tf_op jit(solution)/shard_map/ppermute | solution.py:20
  82.8 6.5 %collective-permute-start.5 = (f32[2,16,4,128]{3,2,1,0:T(4,128)S(1)}, f32[2,16,4,128]{3,2,1,0:T(4,128)S(1)}, u32[]{:S(2)}, u32[]{:S(2)}) collective-permute-start(f32[2,16,4,128]{3,2,1,0:T(4,128)S(1)} %get-tuple-element.16), channel_id=1, source_target_pairs={{0,4},{4,8},{8,12},{12,16},{16,20},{20,24},{24,28},{28,32},{32,36}... | collective-permute-start | bytes 196616 | tf_op jit(solution)/shard_map/ppermute | solution.py:19
  92.6 6.3 %collective-permute-start.6 = (f32[2,16,80,4]{2,1,3,0:T(8,128)S(1)}, f32[2,16,80,4]{2,1,3,0:T(8,128)S(1)}, u32[]{:S(2)}, u32[]{:S(2)}) collective-permute-start(f32[2,16,80,4]{2,1,3,0:T(8,128)S(1)} %copy.21), channel_id=1, source_target_pairs={{1,0},{2,1},{3,2},{5,4},{6,5},{7,6},{9,8},{10,9},{11,10},{13,12},{... | collective-permute-start | bytes 122888 | tf_op jit(solution)/shard_map/ppermute | solution.py:25
  97.3 3.2 %collective-permute-start.7 = (f32[2,16,80,4]{2,1,3,0:T(8,128)S(1)}, f32[2,16,80,4]{2,1,3,0:T(8,128)S(1)}, u32[]{:S(2)}, u32[]{:S(2)}) collective-permute-start(f32[2,16,80,4]{2,1,3,0:T(8,128)S(1)} %copy.22), channel_id=1, source_target_pairs={{0,1},{1,2},{2,3},{4,5},{5,6},{6,7},{8,9},{9,10},{10,11},{12,13},{... | collective-permute-start | bytes 122888 | tf_op jit(solution)/shard_map/ppermute | solution.py:26
  122.8 27.3 %copy-start.6 = (f32[2,64,2,64]{3,2,1,0:T(2,128)S(1)}, f32[2,64,2,64]{3,2,1,0:T(2,128)}, u32[]{:S(2)}) copy-start(f32[2,64,2,64]{3,2,1,0:T(2,128)} %copy-done.5) | copy-start | bytes 196612
  152.6 20.8 %copy-start.3 = (f32[2,16,64,128]{3,2,1,0:T(8,128)S(1)}, f32[2,16,64,128]{3,2,1,0:T(8,128)}, u32[]{:S(2)}) copy-start(f32[2,16,64,128]{3,2,1,0:T(8,128)} %param.7) | copy-start | bytes 3145732

commit v5 on v4

--- a/solution.py
+++ b/solution.py
@@ -29,20 +29,21 @@
 
 
 def diffusion_kernel(steps, rows, cols, v_ref, o_ref):
+    fields, depth = o_ref.shape[0], o_ref.shape[1]
     height, span = v_ref.shape[2], v_ref.shape[3]
-    fields = o_ref.shape[0]
-    along_i = v_ref[fields, 0]
-    along_j = v_ref[fields + 1, 0]
-    sea = v_ref[fields + 2, 0]
-    weight_i = along_i * sea * pltpu.roll(sea, height - 1, 0)
-    weight_j = along_j * sea * pltpu.roll(sea, span - 1, 1)
-    for f in range(fields):
-        values = v_ref[f, 0]
-        for s in range(steps):
-            flux_i = weight_i * (pltpu.roll(values, height - 1, 0) - values)
-            flux_j = weight_j * (pltpu.roll(values, span - 1, 1) - values)
-            values = values + flux_i - pltpu.roll(flux_i, 1, 0) + flux_j - pltpu.roll(flux_j, 1, 1)
-        o_ref[f, 0] = values[:rows, :cols]
+    for level in range(depth):
+        along_i = v_ref[fields, level]
+        along_j = v_ref[fields + 1, level]
+        sea = v_ref[fields + 2, level]
+        weight_i = along_i * sea * pltpu.roll(sea, height - 1, 0)
+        weight_j = along_j * sea * pltpu.roll(sea, span - 1, 1)
+        for f in range(fields):
+            values = v_ref[f, level]
+            for s in range(steps):
+                flux_i = weight_i * (pltpu.roll(values, height - 1, 0) - values)
+                flux_j = weight_j * (pltpu.roll(values, span - 1, 1) - values)
+                values = values + flux_i - pltpu.roll(flux_i, 1, 0) + flux_j - pltpu.roll(flux_j, 1, 1)
+            o_ref[f, level] = values[:rows, :cols]
 
 
 def diffusion(values, coefs, steps):
@@ -52,9 +53,9 @@
     return pl.pallas_call(
         functools.partial(diffusion_kernel, steps, rows, cols),
         out_shape=jax.ShapeDtypeStruct(values.shape, values.dtype),
-        grid=(levels,),
-        in_specs=[pl.BlockSpec((ext.shape[0], 1, height, span), lambda l: (0, l, 0, 0))],
-        out_specs=pl.BlockSpec((fields, 1, rows, cols), lambda l: (0, l, 0, 0)),
+        grid=(levels // 4,),
+        in_specs=[pl.BlockSpec((ext.shape[0], 4, height, span), lambda l: (0, l, 0, 0))],
+        out_specs=pl.BlockSpec((fields, 4, rows, cols), lambda l: (0, l, 0, 0)),
     )(ext)
 
 

time: 177 us -> 177 us (level)
  no operation moved by 1% of the time
where the time goes in v5:
time: 177 us
  Pallas kernels  92.5 us (52%)
  starting transfers between devices  26.4 us (15%)
  local copies, waits for them, and re-layouts  24.7 us (14%)
  other arithmetic  16.4 us (9%)
  waiting for transfers between devices  13 us (7%)
  matrix products  3.56 us (2%)
    pallas_call x3, Pallas kernels, lev_exchange(): pl.pallas_call(kernel, out_shape=jax.ShapeDtypeStruct(tuple(out_shape), x...  75.7 us
    pallas_call x1, Pallas kernels, diffusion(): pl.pallas_call(functools.partial(diffusion_kernel, steps, rows, cols), ou...  16.8 us
    ppermute x2, starting transfers between devices, circular(): east = lax.ppermute(tall[..., :width], 'gy', left)  9.84 us
    ppermute x2, waiting for transfers between devices, circular(): north = lax.ppermute(x[:, :, rows - width:], 'gx', up)  8.56 us
    slice x4, local copies, waits for them, and re-layouts, circular(): east = lax.ppermute(tall[..., :width], 'gy', left)  7.96 us
    all_to_all x1, starting transfers between devices, to_columns(): return lax.all_to_all(x, 'lev', 2, 1, tiled=True)  7.28 us
    ppermute x2, starting transfers between devices, circular(): south = lax.ppermute(x[:, :, :width], 'gx', down)  5.09 us
    concatenate x1, other arithmetic, diffusion(): ext = jnp.concatenate([circular(values, steps), coefs])  4.96 us
  transfers between devices with their start and end apart: 9, of which 5 were waited for; matrix products, arithmetic and copies ran while one was open for 10% of the time, Pallas kernels for 0%

profile of v5, /device:TPU:33, one launch (start us, length us, event | category | flops | bytes accessed | tf_op | source)
XLA Modules:
  0.0 176.8 jit_solution(8155100423005420581)
XLA Ops:
  0.0 1.2 fusion.7
  1.3 0.1 copy-done.2
  1.4 1.5 multiply_multiply_fusion.1
  2.9 1.6 copy.18
  4.5 7.3 %all-to-all-start = ((f32[2,16,64,128]{3,1,0,2:T(8,128)}), f32[2,16,64,128]{3,1,0,2:T(8,128)}, u32[]{:S(2)}, u32[]{:S(2)}) async-start(f32[2,16,64,128]{3,1,0,2:T(8,128)} %copy.18), calls=%async_computation | async-start | bytes 2097152 | tf_op jit(solution)/shard_map/all_to_all | solution.py:147
  11.8 5.0 %collective-permute-start = (f32[3,16,4,128]{3,2,1,0:T(4,128)S(1)}, f32[3,16,4,128]{3,2,1,0:T(4,128)S(1)}, u32[]{:S(2)}, u32[]{:S(2)}) collective-permute-start(f32[3,16,4,128]{3,2,1,0:T(4,128)S(1)} %get-tuple-element.11), channel_id=1, source_target_pairs={{4,0},{8,4},{12,8},{16,12},{20,16},{24,20},{28,24},{32,28},{36,32}... | collective-permute-start | bytes 294920 | tf_op jit(solution)/shard_map/ppermute | solution.py:20
  16.8 1.6 collective-permute-done
  18.4 5.1 %collective-permute-done.1 = f32[3,16,4,128]{3,2,1,0:T(4,128)S(1)} collective-permute-done((f32[3,16,4,128]{3,2,1,0:T(4,128)S(1)}, f32[3,16,4,128]{3,2,1,0:T(4,128)S(1)}, u32[]{:S(2)}, u32[]{:S(2)}) %collective-permute-start.1) | collective-permute-done | bytes 98336 | tf_op jit(solution)/shard_map/ppermute | solution.py:19
  23.6 0.6 copy-done.9
  24.2 0.7 copy-done.4
  24.9 0.2 pad_maximum_fusion.2
  25.1 1.9 %fusion.4 = (f32[3,16,80,4]{3,2,1,0:T(8,128)}, f32[3,16,80,4]{3,2,1,0:T(8,128)S(1)}) fusion(f32[3,16,80,128]{3,2,1,0:T(8,128)S(1)} %pad_maximum_fusion.2), kind=kLoop, calls=%fused_computation.19 | loop fusion | bytes 245760 | tf_op jit(solution)/shard_map/slice | solution.py:25
  27.0 2.8 %copy.13 = f32[3,16,80,4]{2,1,3,0:T(8,128)} copy(f32[3,16,80,4]{3,2,1,0:T(8,128)} %get-tuple-element.9) | data formatting | bytes 122880 | tf_op jit(solution)/shard_map/slice | solution.py:25
  29.8 1.2 copy.14
  31.1 1.3 collective-permute-start.3
  32.4 5.6 %collective-permute-start.2 = (f32[3,16,80,4]{2,1,3,0:T(8,128)}, f32[3,16,80,4]{2,1,3,0:T(8,128)}, u32[]{:S(2)}, u32[]{:S(2)}) collective-permute-start(f32[3,16,80,4]{2,1,3,0:T(8,128)} %copy.13), channel_id=1, source_target_pairs={{1,0},{2,1},{3,2},{5,4},{6,5},{7,6},{9,8},{10,9},{11,10},{13,12},{... | collective-permute-start | bytes 184328 | tf_op jit(solution)/shard_map/ppermute | solution.py:25
  37.9 0.9 convert_add_fusion
  38.8 0.1 reshape.4
  38.9 0.8 copy.17
  39.7 0.1 pad.19.clone
  39.8 1.5 copy.15
  41.3 2.8 %copy.16 = f32[3,16,80,4]{3,2,1,0:T(8,128)} copy(f32[3,16,80,4]{2,1,3,0:T(8,128)} %collective-permute-done.3) | data formatting | bytes 122880 | tf_op jit(solution)/shard_map/ppermute | solution.py:26
  44.2 3.8 %pad_maximum_fusion.1 = f32[3,16,80,256]{3,2,1,0:T(8,128)} fusion(f32[3,16,80,4]{3,2,1,0:T(8,128)} %copy.16, f32[3,16,80,4]{3,2,1,0:T(8,128)S(1)} %copy.15, f32[3,16,4,128]{3,2,1,0:T(4,128)} %copy-done.9, f32[3,16,8,128]{3,2,1,0:T(8,128)} %copy-done.4, f32[3,16,4,128]{3,2,1,0:T(4,128)} %copy-done.8, f32[1,16,64,128]{3,2,1,0:T(8,128)S(1)} %get-tuple-element.18, ...), kind=kLoop, calls=%fused_computation.1 | loop fusion | flops 7864320 | bytes 6022144 | tf_op jit(solution)/shard_map/concatenate | solution.py:28
  48.0 1.4 copy.19
  49.4 1.1 convolution_bitcast_fusion.1
  50.5 1.6 copy.20.x_ref
  52.1 29.3 %shard_map.64 = f32[2,16,64,128]{3,2,1,0:T(8,128)} custom-call(f32[2,64,16,128]{3,2,1,0:T(8,128)} %copy.20.x_ref), custom_call_target="tpu_custom_call" | custom-call | tf_op jit(solution)/shard_map/pallas_call | solution.py:129
  81.3 1.3 broadcast_multiply_fusion
  82.7 0.1 collective-permute-start.4
  82.8 1.5 collective-permute-start.5
  84.2 1.6 collective-permute-done.4
  85.9 3.4 %collective-permute-done.5 = f32[2,16,4,128]{3,2,1,0:T(4,128)S(1)} collective-permute-done((f32[2,16,4,128]{3,2,1,0:T(4,128)S(1)}, f32[2,16,4,128]{3,2,1,0:T(4,128)S(1)}, u32[]{:S(2)}, u32[]{:S(2)}) %collective-permute-start.5) | collective-permute-done | bytes 65568 | tf_op jit(solution)/shard_map/ppermute | solution.py:19
  89.3 0.1 pad_maximum_fusion.3
  89.4 1.5 fusion.5
  90.9 1.7 copy.21
  92.6 4.3 %collective-permute-start.6 = (f32[2,16,80,4]{2,1,3,0:T(8,128)S(1)}, f32[2,16,80,4]{2,1,3,0:T(8,128)S(1)}, u32[]{:S(2)}, u32[]{:S(2)}) collective-permute-start(f32[2,16,80,4]{2,1,3,0:T(8,128)S(1)} %copy.21), channel_id=1, source_target_pairs={{1,0},{2,1},{3,2},{5,4},{6,5},{7,6},{9,8},{10,9},{11,10},{13,12},{... | collective-permute-start | bytes 122888 | tf_op jit(solution)/shard_map/ppermute | solution.py:25
  96.9 0.4 copy.22
  97.3 1.5 collective-permute-start.7
  98.9 0.5 copy.23
  99.4 1.1 collective-permute-done.7
  100.5 1.5 copy.24
  102.0 5.0 %pad_maximum_fusion.v_ref = f32[5,16,80,256]{3,2,1,0:T(8,128)} fusion(f32[3,16,80,256]{3,2,1,0:T(8,128)} %pad_maximum_fusion.1, f32[2,16,80,4]{3,2,1,0:T(8,128)} %copy.24, f32[2,16,80,4]{3,2,1,0:T(8,128)S(1)} %copy.23, f32[2,16,4,128]{3,2,1,0:T(4,128)S(1)} %collective-permute-done.5, f32[2,16,8,128]{3,2,1,0:T(8,128)S(1)} %broadcast_in_dim.20, ...), kind=kLoop, calls=%fused_computation | loop fusion | flops 11468800 | bytes 11883520 | tf_op jit(solution)/shard_map/concatenate | solution.py:51
  107.0 16.8 %shard_map.65.x_ref = f32[2,16,64,128]{3,2,1,0:T(8,128)} custom-call(f32[5,16,80,256]{3,2,1,0:T(8,128)} %pad_maximum_fusion.v_ref), custom_call_target="tpu_custom_call" | custom-call | tf_op jit(solution)/shard_map/pallas_call | solution.py:53
  123.8 27.3 %shard_map.66 = f32[2,64,16,128]{3,2,1,0:T(8,128)} custom-call(f32[2,16,64,128]{3,2,1,0:T(8,128)} %shard_map.65.x_ref), custom_call_target="tpu_custom_call" | custom-call | tf_op jit(solution)/shard_map/pallas_call | solution.py:129
  151.1 2.5 %convolution_bitcast_fusion = f32[2,64,16,128]{3,1,2,0:T(8,128)S(1)} fusion(f32[2,64,16,128]{3,2,1,0:T(8,128)} %shard_map.66, f32[2,64,2,64,1]{3,2,1,0,4:T(2,128)S(1)} %bitcast.35), kind=kOutput, calls=%fused_computation.3 | convolution fusion | flops 402653184 | bytes 2162688 | tf_op jit(solution)/shard_map/abcd,cdij->abij/dot_general | solution.py:158
  153.6 1.6 copy.27.x_ref
  155.2 19.2 %shard_map.67 = f32[2,16,64,128]{3,2,1,0:T(8,128)} custom-call(f32[2,64,16,128]{3,2,1,0:T(8,128)} %copy.27.x_ref), custom_call_target="tpu_custom_call" | custom-call | tf_op jit(solution)/shard_map/pallas_call | solution.py:129
  174.4 2.4 %multiply_multiply_fusion = f32[2,16,64,128]{3,2,1,0:T(8,128)} fusion(f32[2,16,64,128]{3,2,1,0:T(8,128)} %shard_map.67, f32[2,16,64,128]{3,2,1,0:T(8,128)S(1)} %copy-done.3, f32[16,64,128]{2,1,0:T(8,128)S(1)} %get-tuple-element.17), kind=kLoop, calls=%fused_computation.8 | loop fusion | flops 524288 | bytes 3670016 | tf_op jit(solution)/shard_map/mul | solution.py:178
  (29 shorter events, 0.2 us)
Async XLA Ops:
  0.0 1.4 copy-start.2
  2.9 8.9 %copy-start = (f32[16,64,128]{2,1,0:T(8,128)S(1)}, f32[16,64,128]{2,1,0:T(8,128)}, u32[]{:S(2)}) copy-start(f32[16,64,128]{2,1,0:T(8,128)} %param.9) | copy-start | bytes 1572868
  2.9 8.9 %copy-start.1 = (f32[16,64,128]{2,1,0:T(8,128)S(1)}, f32[16,64,128]{2,1,0:T(8,128)}, u32[]{:S(2)}) copy-start(f32[16,64,128]{2,1,0:T(8,128)} %param.8) | copy-start | bytes 1572868
  4.5 43.5 %all-to-all-start = ((f32[2,16,64,128]{3,1,0,2:T(8,128)}), f32[2,16,64,128]{3,1,0,2:T(8,128)}, u32[]{:S(2)}, u32[]{:S(2)}) async-start(f32[2,16,64,128]{3,1,0,2:T(8,128)} %copy.18), calls=%async_computation | async-start | bytes 2097152 | tf_op jit(solution)/shard_map/all_to_all | solution.py:147
  11.8 6.6 %collective-permute-start = (f32[3,16,4,128]{3,2,1,0:T(4,128)S(1)}, f32[3,16,4,128]{3,2,1,0:T(4,128)S(1)}, u32[]{:S(2)}, u32[]{:S(2)}) collective-permute-start(f32[3,16,4,128]{3,2,1,0:T(4,128)S(1)} %get-tuple-element.11), channel_id=1, source_target_pairs={{4,0},{8,4},{12,8},{16,12},{20,16},{24,20},{28,24},{32,28},{36,32}... | collective-permute-start | bytes 294920 | tf_op jit(solution)/shard_map/ppermute | solution.py:20
  16.8 6.8 %collective-permute-start.1 = (f32[3,16,4,128]{3,2,1,0:T(4,128)S(1)}, f32[3,16,4,128]{3,2,1,0:T(4,128)S(1)}, u32[]{:S(2)}, u32[]{:S(2)}) collective-permute-start(f32[3,16,4,128]{3,2,1,0:T(4,128)S(1)} %get-tuple-element.12), channel_id=1, source_target_pairs={{0,4},{4,8},{8,12},{12,16},{16,20},{20,24},{24,28},{28,32},{32,36}... | collective-permute-start | bytes 294920 | tf_op jit(solution)/shard_map/ppermute | solution.py:19
  18.4 5.2 %copy-start.8 = (f32[3,16,4,128]{3,2,1,0:T(4,128)}, f32[3,16,4,128]{3,2,1,0:T(4,128)S(1)}, u32[]{:S(2)}) copy-start(f32[3,16,4,128]{3,2,1,0:T(4,128)S(1)} %collective-permute-done) | copy-start | bytes 294916
  23.6 0.6 copy-start.9
  24.2 0.7 copy-start.4
  31.1 10.2 %collective-permute-start.3 = (f32[3,16,80,4]{2,1,3,0:T(8,128)}, f32[3,16,80,4]{2,1,3,0:T(8,128)}, u32[]{:S(2)}, u32[]{:S(2)}) collective-permute-start(f32[3,16,80,4]{2,1,3,0:T(8,128)} %copy.14), channel_id=1, source_target_pairs={{0,1},{1,2},{2,3},{4,5},{5,6},{6,7},{8,9},{9,10},{10,11},{12,13},{... | collective-permute-start | bytes 184328 | tf_op jit(solution)/shard_map/ppermute | solution.py:26
  32.4 7.4 %collective-permute-start.2 = (f32[3,16,80,4]{2,1,3,0:T(8,128)}, f32[3,16,80,4]{2,1,3,0:T(8,128)}, u32[]{:S(2)}, u32[]{:S(2)}) collective-permute-start(f32[3,16,80,4]{2,1,3,0:T(8,128)} %copy.13), channel_id=1, source_target_pairs={{1,0},{2,1},{3,2},{5,4},{6,5},{7,6},{9,8},{10,9},{11,10},{13,12},{... | collective-permute-start | bytes 184328 | tf_op jit(solution)/shard_map/ppermute | solution.py:25
  38.9 0.9 copy-start.5
  48.0 1.4 copy-start.7
  82.7 3.2 %collective-permute-start.4 = (f32[2,16,4,128]{3,2,1,0:T(4,128)S(1)}, f32[2,16,4,128]{3,2,1,0:T(4,128)S(1)}, u32[]{:S(2)}, u32[]{:S(2)}) collective-permute-start(f32[2,16,4,128]{3,2,1,0:T(4,128)S(1)} %get-tuple-element.15), channel_id=1, source_target_pairs={{4,0},{8,4},{12,8},{16,12},{20,16},{24,20},{28,24},{32,28},{36,32}... | collective-permute-start | bytes 196616 | tf_op jit(solution)/shard_map/ppermute | solution.py:20
  82.8 6.5 %collective-permute-start.5 = (f32[2,16,4,128]{3,2,1,0:T(4,128)S(1)}, f32[2,16,4,128]{3,2,1,0:T(4,128)S(1)}, u32[]{:S(2)}, u32[]{:S(2)}) collective-permute-start(f32[2,16,4,128]{3,2,1,0:T(4,128)S(1)} %get-tuple-element.16), channel_id=1, source_target_pairs={{0,4},{4,8},{8,12},{12,16},{16,20},{20,24},{24,28},{28,32},{32,36}... | collective-permute-start | bytes 196616 | tf_op jit(solution)/shard_map/ppermute | solution.py:19
  92.6 6.3 %collective-permute-start.6 = (f32[2,16,80,4]{2,1,3,0:T(8,128)S(1)}, f32[2,16,80,4]{2,1,3,0:T(8,128)S(1)}, u32[]{:S(2)}, u32[]{:S(2)}) collective-permute-start(f32[2,16,80,4]{2,1,3,0:T(8,128)S(1)} %copy.21), channel_id=1, source_target_pairs={{1,0},{2,1},{3,2},{5,4},{6,5},{7,6},{9,8},{10,9},{11,10},{13,12},{... | collective-permute-start | bytes 122888 | tf_op jit(solution)/shard_map/ppermute | solution.py:25
  97.3 3.2 %collective-permute-start.7 = (f32[2,16,80,4]{2,1,3,0:T(8,128)S(1)}, f32[2,16,80,4]{2,1,3,0:T(8,128)S(1)}, u32[]{:S(2)}, u32[]{:S(2)}) collective-permute-start(f32[2,16,80,4]{2,1,3,0:T(8,128)S(1)} %copy.22), channel_id=1, source_target_pairs={{0,1},{1,2},{2,3},{4,5},{5,6},{6,7},{8,9},{9,10},{10,11},{12,13},{... | collective-permute-start | bytes 122888 | tf_op jit(solution)/shard_map/ppermute | solution.py:26
  123.8 27.3 %copy-start.6 = (f32[2,64,2,64]{3,2,1,0:T(2,128)S(1)}, f32[2,64,2,64]{3,2,1,0:T(2,128)}, u32[]{:S(2)}) copy-start(f32[2,64,2,64]{3,2,1,0:T(2,128)} %copy-done.5) | copy-start | bytes 196612
  153.6 20.8 %copy-start.3 = (f32[2,16,64,128]{3,2,1,0:T(8,128)S(1)}, f32[2,16,64,128]{3,2,1,0:T(8,128)}, u32[]{:S(2)}) copy-start(f32[2,16,64,128]{3,2,1,0:T(8,128)} %param.7) | copy-start | bytes 3145732

commit v6 on v4

--- a/solution.py
+++ b/solution.py
@@ -47,7 +47,7 @@
 
 def diffusion(values, coefs, steps):
     fields, levels, rows, cols = values.shape
-    ext = jnp.concatenate([circular(values, steps), coefs])
+    ext = circular(jnp.concatenate([values, coefs]), steps)
     height, span = ext.shape[2], ext.shape[3]
     return pl.pallas_call(
         functools.partial(diffusion_kernel, steps, rows, cols),
@@ -167,11 +167,8 @@
     balance = jnp.eye(order_count, dtype=jnp.float32) + coupling
     forward = balance.reshape(2, level_count, 2, level_count)
     adjoint = jnp.transpose(forward, (2, 3, 0, 1))
-    coefs = circular(jnp.stack([diffusion_i, diffusion_j, ocean]), steps)
-    columns = to_columns(scaled, False)
-    mixed = jnp.einsum("abcd,cdij->abij", adjoint, columns, precision=lax.Precision.HIGHEST)
-    coefs, mixed = lax.optimization_barrier((coefs, mixed))
-    adjoint_mixed = to_levels(mixed) * ocean[None]
+    coefs = jnp.stack([diffusion_i, diffusion_j, ocean])
+    adjoint_mixed = level_mix(scaled, adjoint) * ocean[None]
     spread = diffusion(adjoint_mixed, coefs, steps)
     forward_mixed = level_mix(spread, forward)
     return ocean[None] * norm_gain * forward_mixed

time: 177 us -> 183 us (1.034)
  the two profiles are of different devices: /device:TPU:33 before, /device:TPU:1 now
where the time goes in v6:
time: 183 us
  Pallas kernels  120 us (66%)
  local copies, waits for them, and re-layouts  20.6 us (11%)
  starting transfers between devices  14.5 us (8%)
  other arithmetic  14.4 us (8%)
  waiting for transfers between devices  7.49 us (4%)
  matrix products  5.1 us (3%)
    pallas_call x4, Pallas kernels, lev_exchange(): pl.pallas_call(kernel, out_shape=jax.ShapeDtypeStruct(tuple(out_shape), x...  104 us
    pallas_call x1, Pallas kernels, diffusion(): pl.pallas_call(functools.partial(diffusion_kernel, steps, rows, cols), ou...  15.8 us
    slice x2, local copies, waits for them, and re-layouts, circular(): east = lax.ppermute(tall[..., :width], 'gy', left)  6.97 us
    concatenate x1, other arithmetic, circular(): return jnp.concatenate([tall, east, middle, west], 3)  5.52 us
    ppermute x1, starting transfers between devices, circular(): east = lax.ppermute(tall[..., :width], 'gy', left)  5.28 us
    ppermute x1, waiting for transfers between devices, circular(): north = lax.ppermute(x[:, :, rows - width:], 'gx', up)  5.22 us
    dot_general x2, matrix products, level_mix(): jnp.einsum('abcd,cdij->abij', matrix, columns, precision=lax.Precision.HI...  5.1 us
    ppermute x1, starting transfers between devices, circular(): south = lax.ppermute(x[:, :, :width], 'gx', down)  4.94 us
  transfers between devices with their start and end apart: 4, of which 2 were waited for; matrix products, arithmetic and copies ran while one was open for 3% of the time, Pallas kernels for 0%

profile of v6, /device:TPU:1, one launch (start us, length us, event | category | flops | bytes accessed | tf_op | source)
XLA Modules:
  0.0 182.5 jit_solution(2145998233894248450)
XLA Ops:
  0.0 0.9 convert_add_fusion
  0.9 0.1 reshape.4
  1.0 0.0 copy-start.3
  1.0 0.1 copy.13
  1.1 1.2 fusion.7
  2.3 2.8 %multiply_multiply_fusion.1.x_ref = f32[2,16,64,128]{3,2,1,0:T(8,128)} fusion(f32[2,16,64,128]{3,2,1,0:T(8,128)} %param.6, f32[2,16,64,128]{3,2,1,0:T(8,128)} %param.7, f32[16,64,128]{2,1,0:T(8,128)S(1)} %get-tuple-element.9), kind=kLoop, calls=%fused_computation.9 | loop fusion | flops 524288 | bytes 3670016 | tf_op jit(solution)/shard_map/mul | solution.py:164
  5.0 0.0 copy-done.3
  5.0 31.6 %shard_map.64 = f32[2,64,16,128]{3,2,1,0:T(8,128)} custom-call(f32[2,16,64,128]{3,2,1,0:T(8,128)} %multiply_multiply_fusion.1.x_ref), custom_call_target="tpu_custom_call" | custom-call | tf_op jit(solution)/shard_map/pallas_call | solution.py:128
  36.6 2.5 %convolution_bitcast_fusion.1 = f32[2,64,16,128]{3,1,2,0:T(8,128)S(1)} fusion(f32[2,64,16,128]{3,2,1,0:T(8,128)} %shard_map.64, f32[2,64,2,64]{1,3,0,2:T(8,128)S(1)} %copy.13), kind=kOutput, calls=%fused_computation.3 | convolution fusion | flops 402653184 | bytes 2162688 | tf_op jit(solution)/shard_map/abcd,cdij->abij/dot_general | solution.py:157
  39.1 0.0 copy-start
  39.1 0.0 copy-start.1
  39.2 1.6 copy.15.x_ref
  40.7 24.5 %shard_map.65 = f32[2,16,64,128]{3,2,1,0:T(8,128)} custom-call(f32[2,64,16,128]{3,2,1,0:T(8,128)} %copy.15.x_ref), custom_call_target="tpu_custom_call" | custom-call | tf_op jit(solution)/shard_map/pallas_call | solution.py:128
  65.3 1.3 broadcast_multiply_fusion
  66.6 0.0 copy-done
  66.6 0.0 copy-done.1
  66.6 0.1 pad_maximum_fusion.5
  66.7 4.9 %collective-permute-start = (f32[5,16,4,128]{3,2,1,0:T(4,128)S(1)}, f32[5,16,4,128]{3,2,1,0:T(4,128)S(1)}, u32[]{:S(2)}, u32[]{:S(2)}) collective-permute-start(f32[5,16,4,128]{3,2,1,0:T(4,128)S(1)} %get-tuple-element.7), channel_id=1, source_target_pairs={{4,0},{8,4},{12,8},{16,12},{20,16},{24,20},{28,24},{32,28},{36,32}... | collective-permute-start | bytes 491528 | tf_op jit(solution)/shard_map/ppermute | solution.py:20
  71.6 0.0 collective-permute-start.1
  71.7 2.3 %collective-permute-done = f32[5,16,4,128]{3,2,1,0:T(4,128)S(1)} collective-permute-done((f32[5,16,4,128]{3,2,1,0:T(4,128)S(1)}, f32[5,16,4,128]{3,2,1,0:T(4,128)S(1)}, u32[]{:S(2)}, u32[]{:S(2)}) %collective-permute-start) | collective-permute-done | bytes 163872 | tf_op jit(solution)/shard_map/ppermute | solution.py:20
  73.9 0.0 copy-start.5
  73.9 5.2 %collective-permute-done.1 = f32[5,16,4,128]{3,2,1,0:T(4,128)S(1)} collective-permute-done((f32[5,16,4,128]{3,2,1,0:T(4,128)S(1)}, f32[5,16,4,128]{3,2,1,0:T(4,128)S(1)}, u32[]{:S(2)}, u32[]{:S(2)}) %collective-permute-start.1) | collective-permute-done | bytes 163872 | tf_op jit(solution)/shard_map/ppermute | solution.py:19
  79.1 0.0 copy-start.6
  79.2 0.0 copy-done.5
  79.2 0.6 copy-done.6
  79.8 0.3 pad_maximum_fusion.1
  80.1 3.8 %fusion.6 = (f32[5,16,80,4]{3,2,1,0:T(8,128)}, f32[5,16,80,4]{3,2,1,0:T(8,128)}) fusion(f32[5,16,80,128]{3,2,1,0:T(8,128)S(1)} %pad_maximum_fusion.1), kind=kLoop, calls=%fused_computation.20 | loop fusion | bytes 409600 | tf_op jit(solution)/shard_map/slice | solution.py:25
  83.9 3.1 %copy.16 = f32[5,16,80,4]{2,1,3,0:T(8,128)} copy(f32[5,16,80,4]{3,2,1,0:T(8,128)} %get-tuple-element.5) | data formatting | bytes 204800 | tf_op jit(solution)/shard_map/slice | solution.py:25
  87.1 5.3 %collective-permute-start.2 = (f32[5,16,80,4]{2,1,3,0:T(8,128)}, f32[5,16,80,4]{2,1,3,0:T(8,128)}, u32[]{:S(2)}, u32[]{:S(2)}) collective-permute-start(f32[5,16,80,4]{2,1,3,0:T(8,128)} %copy.16), channel_id=1, source_target_pairs={{1,0},{2,1},{3,2},{5,4},{6,5},{7,6},{9,8},{10,9},{11,10},{13,12},{... | collective-permute-start | bytes 307208 | tf_op jit(solution)/shard_map/ppermute | solution.py:25
  92.4 3.1 %copy.17 = f32[5,16,80,4]{2,1,3,0:T(8,128)} copy(f32[5,16,80,4]{3,2,1,0:T(8,128)} %get-tuple-element.6) | data formatting | bytes 204800 | tf_op jit(solution)/shard_map/slice | solution.py:26
  95.5 4.2 %collective-permute-start.3 = (f32[5,16,80,4]{2,1,3,0:T(8,128)}, f32[5,16,80,4]{2,1,3,0:T(8,128)}, u32[]{:S(2)}, u32[]{:S(2)}) collective-permute-start(f32[5,16,80,4]{2,1,3,0:T(8,128)} %copy.17), channel_id=1, source_target_pairs={{0,1},{1,2},{2,3},{4,5},{5,6},{6,7},{8,9},{9,10},{10,11},{12,13},{... | collective-permute-start | bytes 307208 | tf_op jit(solution)/shard_map/ppermute | solution.py:26
  99.8 0.1 pad.8.clone
  99.8 0.0 collective-permute-done.2
  99.9 3.2 %copy.18 = f32[5,16,80,4]{3,2,1,0:T(8,128)} copy(f32[5,16,80,4]{2,1,3,0:T(8,128)} %collective-permute-done.2) | data formatting | bytes 204800 | tf_op jit(solution)/shard_map/ppermute | solution.py:25
  103.0 0.0 collective-permute-done.3
  103.0 3.2 %copy.19 = f32[5,16,80,4]{3,2,1,0:T(8,128)} copy(f32[5,16,80,4]{2,1,3,0:T(8,128)} %collective-permute-done.3) | data formatting | bytes 204800 | tf_op jit(solution)/shard_map/ppermute | solution.py:26
  106.2 5.5 %pad_maximum_fusion.v_ref = f32[5,16,80,256]{3,2,1,0:T(8,128)} fusion(f32[5,16,80,4]{3,2,1,0:T(8,128)} %copy.19, f32[5,16,80,4]{3,2,1,0:T(8,128)} %copy.18, f32[5,16,4,128]{3,2,1,0:T(4,128)} %copy-done.6, f32[5,16,8,128]{3,2,1,0:T(8,128)S(1)} %broadcast_in_dim.12, f32[5,16,4,128]{3,2,1,0:T(4,128)} %copy-done.5, f32[1,16,64,128]{3,2,1,0:T(8,128)S(1)} %get-tuple-element.10, ...), kind=kLoop, calls=%fused_computation | loop fusion | flops 14745600 | bytes 10036224 | tf_op jit(solution)/shard_map/concatenate | solution.py:28
  111.7 0.0 copy-start.4
  111.7 15.8 %shard_map.66.x_ref = f32[2,16,64,128]{3,2,1,0:T(8,128)} custom-call(f32[5,16,80,256]{3,2,1,0:T(8,128)} %pad_maximum_fusion.v_ref), custom_call_target="tpu_custom_call" | custom-call | tf_op jit(solution)/shard_map/pallas_call | solution.py:52
  127.6 26.9 %shard_map.67 = f32[2,64,16,128]{3,2,1,0:T(8,128)} custom-call(f32[2,16,64,128]{3,2,1,0:T(8,128)} %shard_map.66.x_ref), custom_call_target="tpu_custom_call" | custom-call | tf_op jit(solution)/shard_map/pallas_call | solution.py:128
  154.5 0.0 copy-start.2
  154.5 0.0 copy-done.4
  154.5 2.6 %convolution_bitcast_fusion = f32[2,64,16,128]{3,1,2,0:T(8,128)S(1)} fusion(f32[2,64,16,128]{3,2,1,0:T(8,128)} %shard_map.67, f32[2,64,2,64,1]{3,2,1,0,4:T(2,128)S(1)} %bitcast.30), kind=kOutput, calls=%fused_computation.2 | convolution fusion | flops 402653184 | bytes 2162688 | tf_op jit(solution)/shard_map/abcd,cdij->abij/dot_general | solution.py:157
  157.1 1.6 copy.22.x_ref
  158.7 21.4 %shard_map.68 = f32[2,16,64,128]{3,2,1,0:T(8,128)} custom-call(f32[2,64,16,128]{3,2,1,0:T(8,128)} %copy.22.x_ref), custom_call_target="tpu_custom_call" | custom-call | tf_op jit(solution)/shard_map/pallas_call | solution.py:128
  180.1 0.0 copy-done.2
  180.1 2.4 %multiply_multiply_fusion = f32[2,16,64,128]{3,2,1,0:T(8,128)} fusion(f32[2,16,64,128]{3,2,1,0:T(8,128)} %shard_map.68, f32[2,16,64,128]{3,2,1,0:T(8,128)S(1)} %copy-done.2, f32[16,64,128]{2,1,0:T(8,128)S(1)} %get-tuple-element.9), kind=kLoop, calls=%fused_computation.8 | loop fusion | flops 524288 | bytes 3670016 | tf_op jit(solution)/shard_map/mul | solution.py:174
  (2 shorter events, 0.0 us)
Async XLA Ops:
  1.0 4.0 %copy-start.3 = (f32[2,64,2,64]{3,2,1,0:T(2,128)}, f32[2,64,2,64]{3,2,1,0:T(2,128)S(1)}, u32[]{:S(2)}) copy-start(f32[2,64,2,64]{3,2,1,0:T(2,128)S(1)} %reshape.4) | copy-start | bytes 196612
  39.1 27.5 %copy-start = (f32[16,64,128]{2,1,0:T(8,128)S(1)}, f32[16,64,128]{2,1,0:T(8,128)}, u32[]{:S(2)}) copy-start(f32[16,64,128]{2,1,0:T(8,128)} %param.9) | copy-start | bytes 1572868
  39.1 27.5 %copy-start.1 = (f32[16,64,128]{2,1,0:T(8,128)S(1)}, f32[16,64,128]{2,1,0:T(8,128)}, u32[]{:S(2)}) copy-start(f32[16,64,128]{2,1,0:T(8,128)} %param.8) | copy-start | bytes 1572868
  66.7 7.2 %collective-permute-start = (f32[5,16,4,128]{3,2,1,0:T(4,128)S(1)}, f32[5,16,4,128]{3,2,1,0:T(4,128)S(1)}, u32[]{:S(2)}, u32[]{:S(2)}) collective-permute-start(f32[5,16,4,128]{3,2,1,0:T(4,128)S(1)} %get-tuple-element.7), channel_id=1, source_target_pairs={{4,0},{8,4},{12,8},{16,12},{20,16},{24,20},{28,24},{32,28},{36,32}... | collective-permute-start | bytes 491528 | tf_op jit(solution)/shard_map/ppermute | solution.py:20
  71.6 7.5 %collective-permute-start.1 = (f32[5,16,4,128]{3,2,1,0:T(4,128)S(1)}, f32[5,16,4,128]{3,2,1,0:T(4,128)S(1)}, u32[]{:S(2)}, u32[]{:S(2)}) collective-permute-start(f32[5,16,4,128]{3,2,1,0:T(4,128)S(1)} %get-tuple-element.8), channel_id=1, source_target_pairs={{0,4},{4,8},{8,12},{12,16},{16,20},{20,24},{24,28},{28,32},{32,36}... | collective-permute-start | bytes 491528 | tf_op jit(solution)/shard_map/ppermute | solution.py:19
  73.9 5.3 %copy-start.5 = (f32[5,16,4,128]{3,2,1,0:T(4,128)}, f32[5,16,4,128]{3,2,1,0:T(4,128)S(1)}, u32[]{:S(2)}) copy-start(f32[5,16,4,128]{3,2,1,0:T(4,128)S(1)} %collective-permute-done) | copy-start | bytes 491524
  79.1 0.7 copy-start.6
  87.1 12.8 %collective-permute-start.2 = (f32[5,16,80,4]{2,1,3,0:T(8,128)}, f32[5,16,80,4]{2,1,3,0:T(8,128)}, u32[]{:S(2)}, u32[]{:S(2)}) collective-permute-start(f32[5,16,80,4]{2,1,3,0:T(8,128)} %copy.16), channel_id=1, source_target_pairs={{1,0},{2,1},{3,2},{5,4},{6,5},{7,6},{9,8},{10,9},{11,10},{13,12},{... | collective-permute-start | bytes 307208 | tf_op jit(solution)/shard_map/ppermute | solution.py:25
  95.5 7.5 %collective-permute-start.3 = (f32[5,16,80,4]{2,1,3,0:T(8,128)}, f32[5,16,80,4]{2,1,3,0:T(8,128)}, u32[]{:S(2)}, u32[]{:S(2)}) collective-permute-start(f32[5,16,80,4]{2,1,3,0:T(8,128)} %copy.17), channel_id=1, source_target_pairs={{0,1},{1,2},{2,3},{4,5},{5,6},{6,7},{8,9},{9,10},{10,11},{12,13},{... | collective-permute-start | bytes 307208 | tf_op jit(solution)/shard_map/ppermute | solution.py:26
  111.7 42.8 %copy-start.4 = (f32[2,64,2,64]{3,2,1,0:T(2,128)S(1)}, f32[2,64,2,64]{3,2,1,0:T(2,128)}, u32[]{:S(2)}) copy-start(f32[2,64,2,64]{3,2,1,0:T(2,128)} %copy-done.3) | copy-start | bytes 196612
  154.5 25.6 %copy-start.2 = (f32[2,16,64,128]{3,2,1,0:T(8,128)S(1)}, f32[2,16,64,128]{3,2,1,0:T(8,128)}, u32[]{:S(2)}) copy-start(f32[2,16,64,128]{3,2,1,0:T(8,128)} %param.7) | copy-start | bytes 3145732

commit v7 on v4

--- a/solution.py
+++ b/solution.py
@@ -28,12 +28,12 @@
     return jnp.concatenate([tall, east, middle, west], 3)
 
 
-def diffusion_kernel(steps, rows, cols, v_ref, o_ref):
+def diffusion_kernel(steps, rows, cols, v_ref, c_ref, o_ref):
     height, span = v_ref.shape[2], v_ref.shape[3]
     fields = o_ref.shape[0]
-    along_i = v_ref[fields, 0]
-    along_j = v_ref[fields + 1, 0]
-    sea = v_ref[fields + 2, 0]
+    along_i = c_ref[0, 0]
+    along_j = c_ref[1, 0]
+    sea = c_ref[2, 0]
     weight_i = along_i * sea * pltpu.roll(sea, height - 1, 0)
     weight_j = along_j * sea * pltpu.roll(sea, span - 1, 1)
     for f in range(fields):
@@ -47,15 +47,18 @@
 
 def diffusion(values, coefs, steps):
     fields, levels, rows, cols = values.shape
-    ext = jnp.concatenate([circular(values, steps), coefs])
+    ext = circular(values, steps)
     height, span = ext.shape[2], ext.shape[3]
     return pl.pallas_call(
         functools.partial(diffusion_kernel, steps, rows, cols),
         out_shape=jax.ShapeDtypeStruct(values.shape, values.dtype),
         grid=(levels,),
-        in_specs=[pl.BlockSpec((ext.shape[0], 1, height, span), lambda l: (0, l, 0, 0))],
+        in_specs=[
+            pl.BlockSpec((fields, 1, height, span), lambda l: (0, l, 0, 0)),
+            pl.BlockSpec((coefs.shape[0], 1, height, span), lambda l: (0, l, 0, 0)),
+        ],
         out_specs=pl.BlockSpec((fields, 1, rows, cols), lambda l: (0, l, 0, 0)),
-    )(ext)
+    )(ext, coefs)
 
 
 def lev_exchange(x, src_axis, dst_axis, half_axis, collective):

time: 177 us -> 175 us (0.989)
    concatenate x1 -> x0, other arithmetic: 4.96 us -> none  [diffusion(): ext = jnp.concatenate([circular(values, steps), coefs])]
    concatenate x1 -> x2, other arithmetic: 3.84 us -> 7.14 us  [circular(): return jnp.concatenate([tall, east, middle, west], 3)]
where the time goes in v7:
time: 175 us; the launch traced here: 174 us
  Pallas kernels  91.8 us (52%)
  starting transfers between devices  26.4 us (15%)
  local copies, waits for them, and re-layouts  24.6 us (14%)
  other arithmetic  14.8 us (8%)
  waiting for transfers between devices  13 us (7%)
  matrix products  3.56 us (2%)
    pallas_call x3, Pallas kernels, lev_exchange(): pl.pallas_call(kernel, out_shape=jax.ShapeDtypeStruct(tuple(out_shape), x...  75.7 us
    pallas_call x1, Pallas kernels, diffusion(): pl.pallas_call(functools.partial(diffusion_kernel, steps, rows, cols), ou...  16 us
    ppermute x2, starting transfers between devices, circular(): east = lax.ppermute(tall[..., :width], 'gy', left)  9.86 us
    ppermute x2, waiting for transfers between devices, circular(): north = lax.ppermute(x[:, :, rows - width:], 'gx', up)  8.56 us
    slice x4, local copies, waits for them, and re-layouts, circular(): east = lax.ppermute(tall[..., :width], 'gy', left)  8.01 us
    all_to_all x1, starting transfers between devices, to_columns(): return lax.all_to_all(x, 'lev', 2, 1, tiled=True)  7.28 us
    concatenate x2, other arithmetic, circular(): return jnp.concatenate([tall, east, middle, west], 3)  7.14 us
    ppermute x2, starting transfers between devices, circular(): south = lax.ppermute(x[:, :, :width], 'gx', down)  5.09 us
  transfers between devices with their start and end apart: 9, of which 5 were waited for; matrix products, arithmetic and copies ran while one was open for 10% of the time, Pallas kernels for 0%

profile of v7, /device:TPU:33, one launch (start us, length us, event | category | flops | bytes accessed | tf_op | source)
XLA Modules:
  0.0 174.5 jit_solution(1710931353572342862)
XLA Ops:
  0.0 1.2 fusion.7
  1.3 0.1 copy-done.2
  1.4 1.5 multiply_multiply_fusion.1
  2.9 1.6 copy.18
  4.5 7.3 %all-to-all-start = ((f32[2,16,64,128]{3,1,0,2:T(8,128)}), f32[2,16,64,128]{3,1,0,2:T(8,128)}, u32[]{:S(2)}, u32[]{:S(2)}) async-start(f32[2,16,64,128]{3,1,0,2:T(8,128)} %copy.18), calls=%async_computation | async-start | bytes 2097152 | tf_op jit(solution)/shard_map/all_to_all | solution.py:149
  11.8 5.0 %collective-permute-start = (f32[3,16,4,128]{3,2,1,0:T(4,128)S(1)}, f32[3,16,4,128]{3,2,1,0:T(4,128)S(1)}, u32[]{:S(2)}, u32[]{:S(2)}) collective-permute-start(f32[3,16,4,128]{3,2,1,0:T(4,128)S(1)} %get-tuple-element.11), channel_id=1, source_target_pairs={{4,0},{8,4},{12,8},{16,12},{20,16},{24,20},{28,24},{32,28},{36,32}... | collective-permute-start | bytes 294920 | tf_op jit(solution)/shard_map/ppermute | solution.py:20
  16.8 1.6 collective-permute-done
  18.4 5.1 %collective-permute-done.1 = f32[3,16,4,128]{3,2,1,0:T(4,128)S(1)} collective-permute-done((f32[3,16,4,128]{3,2,1,0:T(4,128)S(1)}, f32[3,16,4,128]{3,2,1,0:T(4,128)S(1)}, u32[]{:S(2)}, u32[]{:S(2)}) %collective-permute-start.1) | collective-permute-done | bytes 98336 | tf_op jit(solution)/shard_map/ppermute | solution.py:19
  23.6 0.6 copy-done.9
  24.2 0.7 copy-done.4
  24.9 0.2 pad_maximum_fusion.2
  25.1 1.9 %fusion.4 = (f32[3,16,80,4]{3,2,1,0:T(8,128)}, f32[3,16,80,4]{3,2,1,0:T(8,128)S(1)}) fusion(f32[3,16,80,128]{3,2,1,0:T(8,128)S(1)} %pad_maximum_fusion.2), kind=kLoop, calls=%fused_computation.19 | loop fusion | bytes 245760 | tf_op jit(solution)/shard_map/slice | solution.py:25
  27.0 2.8 %copy.13 = f32[3,16,80,4]{2,1,3,0:T(8,128)} copy(f32[3,16,80,4]{3,2,1,0:T(8,128)} %get-tuple-element.9) | data formatting | bytes 122880 | tf_op jit(solution)/shard_map/slice | solution.py:25
  29.9 1.3 copy.14
  31.1 1.3 collective-permute-start.3
  32.4 5.6 %collective-permute-start.2 = (f32[3,16,80,4]{2,1,3,0:T(8,128)}, f32[3,16,80,4]{2,1,3,0:T(8,128)}, u32[]{:S(2)}, u32[]{:S(2)}) collective-permute-start(f32[3,16,80,4]{2,1,3,0:T(8,128)} %copy.13), channel_id=1, source_target_pairs={{1,0},{2,1},{3,2},{5,4},{6,5},{7,6},{9,8},{10,9},{11,10},{13,12},{... | collective-permute-start | bytes 184328 | tf_op jit(solution)/shard_map/ppermute | solution.py:25
  38.0 0.9 convert_add_fusion
  38.8 0.1 reshape.4
  39.0 0.8 copy.17
  39.8 0.1 pad.18.clone
  39.8 1.5 copy.15
  41.4 2.8 %copy.16 = f32[3,16,80,4]{3,2,1,0:T(8,128)} copy(f32[3,16,80,4]{2,1,3,0:T(8,128)} %collective-permute-done.3) | data formatting | bytes 122880 | tf_op jit(solution)/shard_map/ppermute | solution.py:26
  44.2 3.8 %pad_maximum_fusion.c_ref = f32[3,16,80,256]{3,2,1,0:T(8,128)} fusion(f32[3,16,80,4]{3,2,1,0:T(8,128)} %copy.16, f32[3,16,80,4]{3,2,1,0:T(8,128)S(1)} %copy.15, f32[3,16,4,128]{3,2,1,0:T(4,128)} %copy-done.9, f32[3,16,8,128]{3,2,1,0:T(8,128)} %copy-done.4, f32[3,16,4,128]{3,2,1,0:T(4,128)} %copy-done.8, f32[1,16,64,128]{3,2,1,0:T(8,128)S(1)} %get-tuple-element.18, ...), kind=kLoop, calls=%fused_computation | loop fusion | flops 7864320 | bytes 6022144 | tf_op jit(solution)/shard_map/concatenate | solution.py:28
  48.0 1.4 copy.19
  49.4 1.1 convolution_bitcast_fusion.1
  50.4 1.6 copy.20.x_ref
  52.0 29.3 %shard_map.64 = f32[2,16,64,128]{3,2,1,0:T(8,128)} custom-call(f32[2,64,16,128]{3,2,1,0:T(8,128)} %copy.20.x_ref), custom_call_target="tpu_custom_call" | custom-call | tf_op jit(solution)/shard_map/pallas_call | solution.py:131
  81.3 1.3 broadcast_multiply_fusion
  82.6 0.1 collective-permute-start.4
  82.7 1.5 collective-permute-start.5
  84.2 1.6 collective-permute-done.4
  85.8 3.4 %collective-permute-done.5 = f32[2,16,4,128]{3,2,1,0:T(4,128)S(1)} collective-permute-done((f32[2,16,4,128]{3,2,1,0:T(4,128)S(1)}, f32[2,16,4,128]{3,2,1,0:T(4,128)S(1)}, u32[]{:S(2)}, u32[]{:S(2)}) %collective-permute-start.5) | collective-permute-done | bytes 65568 | tf_op jit(solution)/shard_map/ppermute | solution.py:19
  89.3 0.1 pad_maximum_fusion.3
  89.4 1.5 fusion.5
  90.9 1.7 copy.21
  92.6 4.3 %collective-permute-start.6 = (f32[2,16,80,4]{2,1,3,0:T(8,128)S(1)}, f32[2,16,80,4]{2,1,3,0:T(8,128)S(1)}, u32[]{:S(2)}, u32[]{:S(2)}) collective-permute-start(f32[2,16,80,4]{2,1,3,0:T(8,128)S(1)} %copy.21), channel_id=1, source_target_pairs={{1,0},{2,1},{3,2},{5,4},{6,5},{7,6},{9,8},{10,9},{11,10},{13,12},{... | collective-permute-start | bytes 122888 | tf_op jit(solution)/shard_map/ppermute | solution.py:25
  96.9 0.4 copy.22
  97.3 1.5 collective-permute-start.7
  98.8 0.5 copy.23
  99.3 1.2 collective-permute-done.7
  100.5 1.5 copy.24
  102.0 3.4 %pad_maximum_fusion.1.v_ref = f32[2,16,80,256]{3,2,1,0:T(8,128)} fusion(f32[2,16,80,4]{3,2,1,0:T(8,128)} %copy.24, f32[2,16,80,4]{3,2,1,0:T(8,128)S(1)} %copy.23, f32[2,16,4,128]{3,2,1,0:T(4,128)S(1)} %collective-permute-done.5, f32[2,16,8,128]{3,2,1,0:T(8,128)S(1)} %broadcast_in_dim.20, f32[2,16,4,128]{3,2,1,0:T(4,128)S(1)} %collective-permute-done.4, ...), kind=kLoop, calls=%fused_computation.1 | loop fusion | flops 3932160 | bytes 4015104 | tf_op jit(solution)/shard_map/concatenate | solution.py:28
  105.4 16.0 %shard_map.65.x_ref = f32[2,16,64,128]{3,2,1,0:T(8,128)} custom-call(f32[2,16,80,256]{3,2,1,0:T(8,128)} %pad_maximum_fusion.1.v_ref, f32[3,16,80,256]{3,2,1,0:T(8,128)} %pad_maximum_fusion.c_ref), custom_call_target="tpu_custom_call" | custom-call | tf_op jit(solution)/shard_map/pallas_call | solution.py:52
  121.4 27.3 %shard_map.66 = f32[2,64,16,128]{3,2,1,0:T(8,128)} custom-call(f32[2,16,64,128]{3,2,1,0:T(8,128)} %shard_map.65.x_ref), custom_call_target="tpu_custom_call" | custom-call | tf_op jit(solution)/shard_map/pallas_call | solution.py:131
  148.7 2.5 %convolution_bitcast_fusion = f32[2,64,16,128]{3,1,2,0:T(8,128)S(1)} fusion(f32[2,64,16,128]{3,2,1,0:T(8,128)} %shard_map.66, f32[2,64,2,64,1]{3,2,1,0,4:T(2,128)S(1)} %bitcast.35), kind=kOutput, calls=%fused_computation.3 | convolution fusion | flops 402653184 | bytes 2162688 | tf_op jit(solution)/shard_map/abcd,cdij->abij/dot_general | solution.py:160
  151.3 1.6 copy.27.x_ref
  152.8 19.2 %shard_map.67 = f32[2,16,64,128]{3,2,1,0:T(8,128)} custom-call(f32[2,64,16,128]{3,2,1,0:T(8,128)} %copy.27.x_ref), custom_call_target="tpu_custom_call" | custom-call | tf_op jit(solution)/shard_map/pallas_call | solution.py:131
  172.0 2.4 %multiply_multiply_fusion = f32[2,16,64,128]{3,2,1,0:T(8,128)} fusion(f32[2,16,64,128]{3,2,1,0:T(8,128)} %shard_map.67, f32[2,16,64,128]{3,2,1,0:T(8,128)S(1)} %copy-done.3, f32[16,64,128]{2,1,0:T(8,128)S(1)} %get-tuple-element.17), kind=kLoop, calls=%fused_computation.8 | loop fusion | flops 524288 | bytes 3670016 | tf_op jit(solution)/shard_map/mul | solution.py:180
  (27 shorter events, 0.1 us)
Async XLA Ops:
  0.0 1.4 copy-start.2
  2.9 8.9 %copy-start = (f32[16,64,128]{2,1,0:T(8,128)S(1)}, f32[16,64,128]{2,1,0:T(8,128)}, u32[]{:S(2)}) copy-start(f32[16,64,128]{2,1,0:T(8,128)} %param.9) | copy-start | bytes 1572868
  2.9 8.9 %copy-start.1 = (f32[16,64,128]{2,1,0:T(8,128)S(1)}, f32[16,64,128]{2,1,0:T(8,128)}, u32[]{:S(2)}) copy-start(f32[16,64,128]{2,1,0:T(8,128)} %param.8) | copy-start | bytes 1572868
  4.5 43.5 %all-to-all-start = ((f32[2,16,64,128]{3,1,0,2:T(8,128)}), f32[2,16,64,128]{3,1,0,2:T(8,128)}, u32[]{:S(2)}, u32[]{:S(2)}) async-start(f32[2,16,64,128]{3,1,0,2:T(8,128)} %copy.18), calls=%async_computation | async-start | bytes 2097152 | tf_op jit(solution)/shard_map/all_to_all | solution.py:149
  11.8 6.6 %collective-permute-start = (f32[3,16,4,128]{3,2,1,0:T(4,128)S(1)}, f32[3,16,4,128]{3,2,1,0:T(4,128)S(1)}, u32[]{:S(2)}, u32[]{:S(2)}) collective-permute-start(f32[3,16,4,128]{3,2,1,0:T(4,128)S(1)} %get-tuple-element.11), channel_id=1, source_target_pairs={{4,0},{8,4},{12,8},{16,12},{20,16},{24,20},{28,24},{32,28},{36,32}... | collective-permute-start | bytes 294920 | tf_op jit(solution)/shard_map/ppermute | solution.py:20
  16.8 6.8 %collective-permute-start.1 = (f32[3,16,4,128]{3,2,1,0:T(4,128)S(1)}, f32[3,16,4,128]{3,2,1,0:T(4,128)S(1)}, u32[]{:S(2)}, u32[]{:S(2)}) collective-permute-start(f32[3,16,4,128]{3,2,1,0:T(4,128)S(1)} %get-tuple-element.12), channel_id=1, source_target_pairs={{0,4},{4,8},{8,12},{12,16},{16,20},{20,24},{24,28},{28,32},{32,36}... | collective-permute-start | bytes 294920 | tf_op jit(solution)/shard_map/ppermute | solution.py:19
  18.4 5.2 %copy-start.8 = (f32[3,16,4,128]{3,2,1,0:T(4,128)}, f32[3,16,4,128]{3,2,1,0:T(4,128)S(1)}, u32[]{:S(2)}) copy-start(f32[3,16,4,128]{3,2,1,0:T(4,128)S(1)} %collective-permute-done) | copy-start | bytes 294916
  23.6 0.6 copy-start.9
  24.2 0.7 copy-start.4
  31.1 10.2 %collective-permute-start.3 = (f32[3,16,80,4]{2,1,3,0:T(8,128)}, f32[3,16,80,4]{2,1,3,0:T(8,128)}, u32[]{:S(2)}, u32[]{:S(2)}) collective-permute-start(f32[3,16,80,4]{2,1,3,0:T(8,128)} %copy.14), channel_id=1, source_target_pairs={{0,1},{1,2},{2,3},{4,5},{5,6},{6,7},{8,9},{9,10},{10,11},{12,13},{... | collective-permute-start | bytes 184328 | tf_op jit(solution)/shard_map/ppermute | solution.py:26
  32.4 7.4 %collective-permute-start.2 = (f32[3,16,80,4]{2,1,3,0:T(8,128)}, f32[3,16,80,4]{2,1,3,0:T(8,128)}, u32[]{:S(2)}, u32[]{:S(2)}) collective-permute-start(f32[3,16,80,4]{2,1,3,0:T(8,128)} %copy.13), channel_id=1, source_target_pairs={{1,0},{2,1},{3,2},{5,4},{6,5},{7,6},{9,8},{10,9},{11,10},{13,12},{... | collective-permute-start | bytes 184328 | tf_op jit(solution)/shard_map/ppermute | solution.py:25
  39.0 0.9 copy-start.5
  48.0 1.4 copy-start.7
  82.6 3.2 %collective-permute-start.4 = (f32[2,16,4,128]{3,2,1,0:T(4,128)S(1)}, f32[2,16,4,128]{3,2,1,0:T(4,128)S(1)}, u32[]{:S(2)}, u32[]{:S(2)}) collective-permute-start(f32[2,16,4,128]{3,2,1,0:T(4,128)S(1)} %get-tuple-element.15), channel_id=1, source_target_pairs={{4,0},{8,4},{12,8},{16,12},{20,16},{24,20},{28,24},{32,28},{36,32}... | collective-permute-start | bytes 196616 | tf_op jit(solution)/shard_map/ppermute | solution.py:20
  82.7 6.5 %collective-permute-start.5 = (f32[2,16,4,128]{3,2,1,0:T(4,128)S(1)}, f32[2,16,4,128]{3,2,1,0:T(4,128)S(1)}, u32[]{:S(2)}, u32[]{:S(2)}) collective-permute-start(f32[2,16,4,128]{3,2,1,0:T(4,128)S(1)} %get-tuple-element.16), channel_id=1, source_target_pairs={{0,4},{4,8},{8,12},{12,16},{16,20},{20,24},{24,28},{28,32},{32,36}... | collective-permute-start | bytes 196616 | tf_op jit(solution)/shard_map/ppermute | solution.py:19
  92.6 6.2 %collective-permute-start.6 = (f32[2,16,80,4]{2,1,3,0:T(8,128)S(1)}, f32[2,16,80,4]{2,1,3,0:T(8,128)S(1)}, u32[]{:S(2)}, u32[]{:S(2)}) collective-permute-start(f32[2,16,80,4]{2,1,3,0:T(8,128)S(1)} %copy.21), channel_id=1, source_target_pairs={{1,0},{2,1},{3,2},{5,4},{6,5},{7,6},{9,8},{10,9},{11,10},{13,12},{... | collective-permute-start | bytes 122888 | tf_op jit(solution)/shard_map/ppermute | solution.py:25
  97.3 3.2 %collective-permute-start.7 = (f32[2,16,80,4]{2,1,3,0:T(8,128)S(1)}, f32[2,16,80,4]{2,1,3,0:T(8,128)S(1)}, u32[]{:S(2)}, u32[]{:S(2)}) collective-permute-start(f32[2,16,80,4]{2,1,3,0:T(8,128)S(1)} %copy.22), channel_id=1, source_target_pairs={{0,1},{1,2},{2,3},{4,5},{5,6},{6,7},{8,9},{9,10},{10,11},{12,13},{... | collective-permute-start | bytes 122888 | tf_op jit(solution)/shard_map/ppermute | solution.py:26
  121.4 27.3 %copy-start.6 = (f32[2,64,2,64]{3,2,1,0:T(2,128)S(1)}, f32[2,64,2,64]{3,2,1,0:T(2,128)}, u32[]{:S(2)}) copy-start(f32[2,64,2,64]{3,2,1,0:T(2,128)} %copy-done.5) | copy-start | bytes 196612
  151.3 20.8 %copy-start.3 = (f32[2,16,64,128]{3,2,1,0:T(8,128)S(1)}, f32[2,16,64,128]{3,2,1,0:T(8,128)}, u32[]{:S(2)}) copy-start(f32[2,16,64,128]{3,2,1,0:T(8,128)} %param.7) | copy-start | bytes 3145732

commit v8 on v7

--- a/solution.py
+++ b/solution.py
@@ -170,11 +170,11 @@
     balance = jnp.eye(order_count, dtype=jnp.float32) + coupling
     forward = balance.reshape(2, level_count, 2, level_count)
     adjoint = jnp.transpose(forward, (2, 3, 0, 1))
-    coefs = circular(jnp.stack([diffusion_i, diffusion_j, ocean]), steps)
-    columns = to_columns(scaled, False)
+    columns = to_columns(scaled)
+    coefs, columns = lax.optimization_barrier((jnp.stack([diffusion_i, diffusion_j, ocean]), columns))
+    coefs = circular(coefs, steps)
     mixed = jnp.einsum("abcd,cdij->abij", adjoint, columns, precision=lax.Precision.HIGHEST)
-    coefs, mixed = lax.optimization_barrier((coefs, mixed))
-    adjoint_mixed = to_levels(mixed) * ocean[None]
+    adjoint_mixed = to_levels(mixed, False) * ocean[None]
     spread = diffusion(adjoint_mixed, coefs, steps)
     forward_mixed = level_mix(spread, forward)
     return ocean[None] * norm_gain * forward_mixed

time: 175 us -> 191 us (1.091)
  the two profiles are of different devices: /device:TPU:33 before, /device:TPU:62 now
where the time goes in v8:
time: 191 us; the launch traced here: 190 us
  Pallas kernels  96.1 us (50%)
  local copies, waits for them, and re-layouts  27.8 us (15%)
  starting transfers between devices  25.1 us (13%)
  waiting for transfers between devices  20.8 us (11%)
  other arithmetic  16.3 us (9%)
  matrix products  3.8 us (2%)
    pallas_call x3, Pallas kernels, lev_exchange(): pl.pallas_call(kernel, out_shape=jax.ShapeDtypeStruct(tuple(out_shape), x...  80 us
    all_to_all x1, waiting for transfers between devices, to_levels(): return lax.all_to_all(x, 'lev', 1, 2, tiled=True)  18.1 us
    pallas_call x1, Pallas kernels, diffusion(): pl.pallas_call(functools.partial(diffusion_kernel, steps, rows, cols), ou...  16 us
    ppermute x2, starting transfers between devices, circular(): north = lax.ppermute(x[:, :, rows - width:], 'gx', up)  9.21 us
    slice x4, local copies, waits for them, and re-layouts, circular(): east = lax.ppermute(tall[..., :width], 'gy', left)  9.17 us
    concatenate x2, other arithmetic, circular(): return jnp.concatenate([tall, east, middle, west], 3)  7.35 us
    ppermute x2, starting transfers between devices, circular(): west = lax.ppermute(tall[..., cols - width:], 'gy', right)  5.13 us
    all_to_all x1, starting transfers between devices, to_levels(): return lax.all_to_all(x, 'lev', 1, 2, tiled=True)  4.84 us
  transfers between devices with their start and end apart: 9, of which 3 were waited for; matrix products, arithmetic and copies ran while one was open for 9% of the time, Pallas kernels for 0%

profile of v8, /device:TPU:62, one launch (start us, length us, event | category | flops | bytes accessed | tf_op | source)
XLA Modules:
  0.0 190.2 jit_solution(894089967532491111)
XLA Ops:
  0.0 1.2 fusion.10
  1.3 0.8 copy-done.2
  2.1 2.5 %multiply_multiply_fusion.1.x_ref = f32[2,16,64,128]{3,2,1,0:T(8,128)} fusion(f32[2,16,64,128]{3,2,1,0:T(8,128)} %param.6, f32[2,16,64,128]{3,2,1,0:T(8,128)S(1)} %copy-done.6, f32[16,64,128]{2,1,0:T(8,128)S(1)} %get-tuple-element.17), kind=kLoop, calls=%fused_computation.13 | loop fusion | flops 524288 | bytes 3670016 | tf_op jit(solution)/shard_map/mul | solution.py:167
  4.6 30.2 %shard_map.64 = f32[2,64,16,128]{3,2,1,0:T(8,128)} custom-call(f32[2,16,64,128]{3,2,1,0:T(8,128)} %multiply_multiply_fusion.1.x_ref), custom_call_target="tpu_custom_call" | custom-call | tf_op jit(solution)/shard_map/pallas_call | solution.py:131
  34.8 1.4 pad_maximum_fusion.3
  36.2 0.1 reshape.4
  36.4 0.1 copy.13
  36.5 1.3 convolution_bitcast_fusion.1
  37.8 1.6 copy.15
  39.4 4.8 %all-to-all-start = ((f32[2,64,16,128]{3,2,0,1:T(8,128)}), f32[2,64,16,128]{3,2,0,1:T(8,128)}, u32[]{:S(2)}, u32[]{:S(2)}) async-start(f32[2,64,16,128]{3,2,0,1:T(8,128)} %copy.15), calls=%async_computation | async-start | bytes 2097152 | tf_op jit(solution)/shard_map/all_to_all | solution.py:155
  44.3 0.8 collective-permute-start.4
  45.1 4.6 %collective-permute-start.5 = (f32[3,16,4,128]{3,2,1,0:T(4,128)S(1)}, f32[3,16,4,128]{3,2,1,0:T(4,128)S(1)}, u32[]{:S(2)}, u32[]{:S(2)}) collective-permute-start(f32[3,16,4,128]{3,2,1,0:T(4,128)S(1)} %get-tuple-element.12), channel_id=1, source_target_pairs={{0,4},{4,8},{8,12},{12,16},{16,20},{20,24},{24,28},{28,32},{32,36}... | collective-permute-start | bytes 294920 | tf_op jit(solution)/shard_map/ppermute | solution.py:19
  49.7 2.6 %collective-permute-done.4 = f32[3,16,4,128]{3,2,1,0:T(4,128)S(1)} collective-permute-done((f32[3,16,4,128]{3,2,1,0:T(4,128)S(1)}, f32[3,16,4,128]{3,2,1,0:T(4,128)S(1)}, u32[]{:S(2)}, u32[]{:S(2)}) %collective-permute-start.4) | collective-permute-done | bytes 98336 | tf_op jit(solution)/shard_map/ppermute | solution.py:20
  52.3 0.6 copy-done.13
  53.0 0.7 copy-done.9
  53.7 0.2 pad_maximum_fusion.2
  53.9 18.1 %all-to-all-done = f32[2,64,16,128]{3,2,0,1:T(8,128)} async-done(((f32[2,64,16,128]{3,2,0,1:T(8,128)}), f32[2,64,16,128]{3,2,0,1:T(8,128)}, u32[]{:S(2)}, u32[]{:S(2)}) %all-to-all-start) | async-done | bytes 1048608 | tf_op jit(solution)/shard_map/all_to_all | solution.py:155
  71.9 1.4 copy.16
  73.4 0.2 bitcast_multiply_fusion
  73.6 1.0 copy-done
  74.5 0.7 fusion.9
  75.2 0.7 collective-permute-start
  75.9 4.6 %collective-permute-start.1 = (f32[2,16,4,128]{3,2,1,0:T(4,128)}, f32[2,16,4,128]{3,2,1,0:T(4,128)}, u32[]{:S(2)}, u32[]{:S(2)}) collective-permute-start(f32[2,16,4,128]{3,2,1,0:T(4,128)} %get-tuple-element.16), channel_id=1, source_target_pairs={{0,4},{4,8},{8,12},{12,16},{16,20},{20,24},{24,28},{28,32},{32,36}... | collective-permute-start | bytes 196616 | tf_op jit(solution)/shard_map/ppermute | solution.py:19
  80.5 2.5 %fusion.6 = (f32[3,16,80,4]{3,2,1,0:T(8,128)}, f32[3,16,80,4]{3,2,1,0:T(8,128)}) fusion(f32[3,16,80,128]{3,2,1,0:T(8,128)S(1)} %pad_maximum_fusion.2), kind=kLoop, calls=%fused_computation.19 | loop fusion | bytes 245760 | tf_op jit(solution)/shard_map/slice | solution.py:25
  83.1 3.0 %copy.21 = f32[3,16,80,4]{2,1,3,0:T(8,128)} copy(f32[3,16,80,4]{3,2,1,0:T(8,128)} %get-tuple-element.9) | data formatting | bytes 122880 | tf_op jit(solution)/shard_map/slice | solution.py:25
  86.0 1.9 %collective-permute-start.6 = (f32[3,16,80,4]{2,1,3,0:T(8,128)}, f32[3,16,80,4]{2,1,3,0:T(8,128)}, u32[]{:S(2)}, u32[]{:S(2)}) collective-permute-start(f32[3,16,80,4]{2,1,3,0:T(8,128)} %copy.21), channel_id=1, source_target_pairs={{1,0},{2,1},{3,2},{5,4},{6,5},{7,6},{9,8},{10,9},{11,10},{13,12},{... | collective-permute-start | bytes 184328 | tf_op jit(solution)/shard_map/ppermute | solution.py:25
  87.9 1.3 copy.22
  89.2 3.0 %collective-permute-start.7 = (f32[3,16,80,4]{2,1,3,0:T(8,128)}, f32[3,16,80,4]{2,1,3,0:T(8,128)S(1)}, u32[]{:S(2)}, u32[]{:S(2)}) collective-permute-start(f32[3,16,80,4]{2,1,3,0:T(8,128)} %copy.22), channel_id=1, source_target_pairs={{0,1},{1,2},{2,3},{4,5},{5,6},{6,7},{8,9},{9,10},{10,11},{12,13},{... | collective-permute-start | bytes 184328 | tf_op jit(solution)/shard_map/ppermute | solution.py:26
  92.2 0.1 pad.16.clone
  92.3 2.9 %copy.23 = f32[3,16,80,4]{3,2,1,0:T(8,128)} copy(f32[3,16,80,4]{2,1,3,0:T(8,128)} %collective-permute-done.6) | data formatting | bytes 122880 | tf_op jit(solution)/shard_map/ppermute | solution.py:25
  95.2 0.1 collective-permute-done.7
  95.3 1.9 %copy.24 = f32[3,16,80,4]{3,2,1,0:T(8,128)} copy(f32[3,16,80,4]{2,1,3,0:T(8,128)S(1)} %collective-permute-done.7) | data formatting | bytes 122880 | tf_op jit(solution)/shard_map/ppermute | solution.py:26
  97.3 1.0 pad_maximum_fusion.4
  98.3 1.9 %fusion.8 = (f32[2,16,80,4]{3,2,1,0:T(8,128)}, f32[2,16,80,4]{3,2,1,0:T(8,128)}) fusion(f32[2,16,80,128]{3,2,1,0:T(8,128)S(1)} %pad_maximum_fusion.4), kind=kLoop, calls=%fused_computation.21 | loop fusion | bytes 163840 | tf_op jit(solution)/shard_map/slice | solution.py:25
  100.2 1.8 copy.17
  102.0 2.4 %collective-permute-start.2 = (f32[2,16,80,4]{2,1,3,0:T(8,128)S(1)}, f32[2,16,80,4]{2,1,3,0:T(8,128)S(1)}, u32[]{:S(2)}, u32[]{:S(2)}) collective-permute-start(f32[2,16,80,4]{2,1,3,0:T(8,128)S(1)} %copy.17), channel_id=1, source_target_pairs={{1,0},{2,1},{3,2},{5,4},{6,5},{7,6},{9,8},{10,9},{11,10},{13,12},{... | collective-permute-start | bytes 122888 | tf_op jit(solution)/shard_map/ppermute | solution.py:25
  104.5 1.7 copy.18
  106.2 2.1 %collective-permute-start.3 = (f32[2,16,80,4]{2,1,3,0:T(8,128)S(1)}, f32[2,16,80,4]{2,1,3,0:T(8,128)S(1)}, u32[]{:S(2)}, u32[]{:S(2)}) collective-permute-start(f32[2,16,80,4]{2,1,3,0:T(8,128)S(1)} %copy.18), channel_id=1, source_target_pairs={{0,1},{1,2},{2,3},{4,5},{5,6},{6,7},{8,9},{9,10},{10,11},{12,13},{... | collective-permute-start | bytes 122888 | tf_op jit(solution)/shard_map/ppermute | solution.py:26
  108.3 4.0 %pad_maximum_fusion.c_ref = f32[3,16,80,256]{3,2,1,0:T(8,128)} fusion(f32[3,16,80,4]{3,2,1,0:T(8,128)} %copy.24, f32[3,16,80,4]{3,2,1,0:T(8,128)} %copy.23, f32[3,16,4,128]{3,2,1,0:T(4,128)S(1)} %copy-done.16, f32[3,16,8,128]{3,2,1,0:T(8,128)S(1)} %copy-done.10, f32[3,16,4,128]{3,2,1,0:T(4,128)S(1)} %copy-done.14, f32[3,16,64,128]{3,2,1,0:T(8,128)S(1)} %pad_maximum_fusion.3, ...), kind=kLoop, calls=%fused_computation | loop fusion | flops 5898240 | bytes 6022144 | tf_op jit(solution)/shard_map/concatenate | solution.py:28
  112.3 0.5 copy.19
  112.8 1.5 copy.20
  114.3 3.4 %pad_maximum_fusion.1.v_ref = f32[2,16,80,256]{3,2,1,0:T(8,128)} fusion(f32[2,16,80,4]{3,2,1,0:T(8,128)} %copy.20, f32[2,16,80,4]{3,2,1,0:T(8,128)S(1)} %copy.19, f32[2,16,4,128]{3,2,1,0:T(4,128)} %collective-permute-done.1, f32[2,16,8,128]{3,2,1,0:T(8,128)S(1)} %broadcast_in_dim.18, f32[2,16,4,128]{3,2,1,0:T(4,128)} %collective-permute-done, ...), kind=kLoop, calls=%fused_computation.1 | loop fusion | flops 3932160 | bytes 4015104 | tf_op jit(solution)/shard_map/concatenate | solution.py:28
  117.7 16.0 %shard_map.65.x_ref = f32[2,16,64,128]{3,2,1,0:T(8,128)} custom-call(f32[2,16,80,256]{3,2,1,0:T(8,128)} %pad_maximum_fusion.1.v_ref, f32[3,16,80,256]{3,2,1,0:T(8,128)} %pad_maximum_fusion.c_ref), custom_call_target="tpu_custom_call" | custom-call | tf_op jit(solution)/shard_map/pallas_call | solution.py:52
  133.7 27.0 %shard_map.66 = f32[2,64,16,128]{3,2,1,0:T(8,128)} custom-call(f32[2,16,64,128]{3,2,1,0:T(8,128)} %shard_map.65.x_ref), custom_call_target="tpu_custom_call" | custom-call | tf_op jit(solution)/shard_map/pallas_call | solution.py:131
  160.8 2.5 %convolution_bitcast_fusion = f32[2,64,16,128]{3,1,2,0:T(8,128)S(1)} fusion(f32[2,64,16,128]{3,2,1,0:T(8,128)} %shard_map.66, f32[2,64,2,64,1]{3,2,1,0,4:T(2,128)S(1)} %bitcast.29), kind=kOutput, calls=%fused_computation.4 | convolution fusion | flops 402653184 | bytes 2162688 | tf_op jit(solution)/shard_map/abcd,cdij->abij/dot_general | solution.py:160
  163.3 1.6 copy.27.x_ref
  164.9 22.9 %shard_map.67 = f32[2,16,64,128]{3,2,1,0:T(8,128)} custom-call(f32[2,64,16,128]{3,2,1,0:T(8,128)} %copy.27.x_ref), custom_call_target="tpu_custom_call" | custom-call | tf_op jit(solution)/shard_map/pallas_call | solution.py:131
  187.8 2.5 %multiply_multiply_fusion = f32[2,16,64,128]{3,2,1,0:T(8,128)} fusion(f32[2,16,64,128]{3,2,1,0:T(8,128)} %shard_map.67, f32[2,16,64,128]{3,2,1,0:T(8,128)S(1)} %copy-done.7, f32[16,64,128]{2,1,0:T(8,128)S(1)} %copy-done.4), kind=kLoop, calls=%fused_computation.12 | loop fusion | flops 524288 | bytes 3670016 | tf_op jit(solution)/shard_map/mul | solution.py:180
  (43 shorter events, 0.2 us)
Async XLA Ops:
  0.0 2.1 %copy-start.6 = (f32[2,16,64,128]{3,2,1,0:T(8,128)S(1)}, f32[2,16,64,128]{3,2,1,0:T(8,128)}, u32[]{:S(2)}) copy-start(f32[2,16,64,128]{3,2,1,0:T(8,128)} %param.7) | copy-start | bytes 3145732
  1.3 0.8 copy-start.2
  34.7 1.5 copy-start.17
  34.8 1.7 copy-start.8
  36.4 3.0 %copy-start.11 = (f32[2,64,2,64]{3,2,1,0:T(2,128)}, f32[2,64,2,64]{3,2,1,0:T(2,128)S(1)}, u32[]{:S(2)}) copy-start(f32[2,64,2,64]{3,2,1,0:T(2,128)S(1)} %reshape.4) | copy-start | bytes 196612
  39.4 32.6 %all-to-all-start = ((f32[2,64,16,128]{3,2,0,1:T(8,128)}), f32[2,64,16,128]{3,2,0,1:T(8,128)}, u32[]{:S(2)}, u32[]{:S(2)}) async-start(f32[2,64,16,128]{3,2,0,1:T(8,128)} %copy.15), calls=%async_computation | async-start | bytes 2097152 | tf_op jit(solution)/shard_map/all_to_all | solution.py:155
  44.3 8.0 %collective-permute-start.4 = (f32[3,16,4,128]{3,2,1,0:T(4,128)S(1)}, f32[3,16,4,128]{3,2,1,0:T(4,128)S(1)}, u32[]{:S(2)}, u32[]{:S(2)}) collective-permute-start(f32[3,16,4,128]{3,2,1,0:T(4,128)S(1)} %get-tuple-element.11), channel_id=1, source_target_pairs={{4,0},{8,4},{12,8},{16,12},{20,16},{24,20},{28,24},{32,28},{36,32}... | collective-permute-start | bytes 294920 | tf_op jit(solution)/shard_map/ppermute | solution.py:20
  45.1 7.2 %collective-permute-start.5 = (f32[3,16,4,128]{3,2,1,0:T(4,128)S(1)}, f32[3,16,4,128]{3,2,1,0:T(4,128)S(1)}, u32[]{:S(2)}, u32[]{:S(2)}) collective-permute-start(f32[3,16,4,128]{3,2,1,0:T(4,128)S(1)} %get-tuple-element.12), channel_id=1, source_target_pairs={{0,4},{4,8},{8,12},{12,16},{16,20},{20,24},{24,28},{28,32},{32,36}... | collective-permute-start | bytes 294920 | tf_op jit(solution)/shard_map/ppermute | solution.py:19
  52.3 0.6 copy-start.13
  52.3 0.7 copy-start.15
  53.0 0.7 copy-start.9
  71.9 1.4 copy-start.3
  73.5 1.0 copy-start
  75.2 22.1 %collective-permute-start = (f32[2,16,4,128]{3,2,1,0:T(4,128)}, f32[2,16,4,128]{3,2,1,0:T(4,128)}, u32[]{:S(2)}, u32[]{:S(2)}) collective-permute-start(f32[2,16,4,128]{3,2,1,0:T(4,128)} %get-tuple-element.15), channel_id=1, source_target_pairs={{4,0},{8,4},{12,8},{16,12},{20,16},{24,20},{28,24},{32,28},{36,32}... | collective-permute-start | bytes 196616 | tf_op jit(solution)/shard_map/ppermute | solution.py:20
  75.9 21.3 %collective-permute-start.1 = (f32[2,16,4,128]{3,2,1,0:T(4,128)}, f32[2,16,4,128]{3,2,1,0:T(4,128)}, u32[]{:S(2)}, u32[]{:S(2)}) collective-permute-start(f32[2,16,4,128]{3,2,1,0:T(4,128)} %get-tuple-element.16), channel_id=1, source_target_pairs={{0,4},{4,8},{8,12},{12,16},{16,20},{20,24},{24,28},{28,32},{32,36}... | collective-permute-start | bytes 196616 | tf_op jit(solution)/shard_map/ppermute | solution.py:19
  83.1 4.9 %copy-start.5 = (f32[3,16,80,4]{3,2,1,0:T(8,128)S(1)}, f32[3,16,80,4]{3,2,1,0:T(8,128)}, u32[]{:S(2)}) copy-start(f32[3,16,80,4]{3,2,1,0:T(8,128)} %get-tuple-element.10) | copy-start | bytes 184324
  86.0 6.3 %collective-permute-start.6 = (f32[3,16,80,4]{2,1,3,0:T(8,128)}, f32[3,16,80,4]{2,1,3,0:T(8,128)}, u32[]{:S(2)}, u32[]{:S(2)}) collective-permute-start(f32[3,16,80,4]{2,1,3,0:T(8,128)} %copy.21), channel_id=1, source_target_pairs={{1,0},{2,1},{3,2},{5,4},{6,5},{7,6},{9,8},{10,9},{11,10},{13,12},{... | collective-permute-start | bytes 184328 | tf_op jit(solution)/shard_map/ppermute | solution.py:25
  89.2 6.1 %collective-permute-start.7 = (f32[3,16,80,4]{2,1,3,0:T(8,128)}, f32[3,16,80,4]{2,1,3,0:T(8,128)S(1)}, u32[]{:S(2)}, u32[]{:S(2)}) collective-permute-start(f32[3,16,80,4]{2,1,3,0:T(8,128)} %copy.22), channel_id=1, source_target_pairs={{0,1},{1,2},{2,3},{4,5},{5,6},{6,7},{8,9},{9,10},{10,11},{12,13},{... | collective-permute-start | bytes 184328 | tf_op jit(solution)/shard_map/ppermute | solution.py:26
  92.3 5.0 %copy-start.1 = (f32[2,16,64,128]{3,2,1,0:T(8,128)S(1)}, f32[2,16,64,128]{3,2,1,0:T(8,128)}, u32[]{:S(2)}) copy-start(f32[2,16,64,128]{3,2,1,0:T(8,128)} %copy-done) | copy-start | bytes 3145732
  100.2 8.1 %copy-start.10 = (f32[3,16,8,128]{3,2,1,0:T(8,128)S(1)}, f32[3,16,8,128]{3,2,1,0:T(8,128)}, u32[]{:S(2)}) copy-start(f32[3,16,8,128]{3,2,1,0:T(8,128)} %copy-done.9) | copy-start | bytes 589828
  100.2 8.1 %copy-start.14 = (f32[3,16,4,128]{3,2,1,0:T(4,128)S(1)}, f32[3,16,4,128]{3,2,1,0:T(4,128)}, u32[]{:S(2)}) copy-start(f32[3,16,4,128]{3,2,1,0:T(4,128)} %copy-done.13) | copy-start | bytes 294916
  100.2 8.1 %copy-start.16 = (f32[3,16,4,128]{3,2,1,0:T(4,128)S(1)}, f32[3,16,4,128]{3,2,1,0:T(4,128)}, u32[]{:S(2)}) copy-start(f32[3,16,4,128]{3,2,1,0:T(4,128)} %copy-done.15) | copy-start | bytes 294916
  102.0 10.3 %collective-permute-start.2 = (f32[2,16,80,4]{2,1,3,0:T(8,128)S(1)}, f32[2,16,80,4]{2,1,3,0:T(8,128)S(1)}, u32[]{:S(2)}, u32[]{:S(2)}) collective-permute-start(f32[2,16,80,4]{2,1,3,0:T(8,128)S(1)} %copy.17), channel_id=1, source_target_pairs={{1,0},{2,1},{3,2},{5,4},{6,5},{7,6},{9,8},{10,9},{11,10},{13,12},{... | collective-permute-start | bytes 122888 | tf_op jit(solution)/shard_map/ppermute | solution.py:25
  106.2 6.6 %collective-permute-start.3 = (f32[2,16,80,4]{2,1,3,0:T(8,128)S(1)}, f32[2,16,80,4]{2,1,3,0:T(8,128)S(1)}, u32[]{:S(2)}, u32[]{:S(2)}) collective-permute-start(f32[2,16,80,4]{2,1,3,0:T(8,128)S(1)} %copy.18), channel_id=1, source_target_pairs={{0,1},{1,2},{2,3},{4,5},{5,6},{6,7},{8,9},{9,10},{10,11},{12,13},{... | collective-permute-start | bytes 122888 | tf_op jit(solution)/shard_map/ppermute | solution.py:26
  133.7 27.0 %copy-start.12 = (f32[2,64,2,64]{3,2,1,0:T(2,128)S(1)}, f32[2,64,2,64]{3,2,1,0:T(2,128)}, u32[]{:S(2)}) copy-start(f32[2,64,2,64]{3,2,1,0:T(2,128)} %copy-done.11) | copy-start | bytes 196612
  163.3 24.5 %copy-start.4 = (f32[16,64,128]{2,1,0:T(8,128)S(1)}, f32[16,64,128]{2,1,0:T(8,128)}, u32[]{:S(2)}) copy-start(f32[16,64,128]{2,1,0:T(8,128)} %copy-done.2) | copy-start | bytes 1572868
  163.3 24.5 %copy-start.7 = (f32[2,16,64,128]{3,2,1,0:T(8,128)S(1)}, f32[2,16,64,128]{3,2,1,0:T(8,128)}, u32[]{:S(2)}) copy-start(f32[2,16,64,128]{3,2,1,0:T(8,128)} %param.7) | copy-start | bytes 3145732

commit v9 on v7

--- a/solution.py
+++ b/solution.py
@@ -11,25 +11,29 @@
 MESH = pl.DeviceIdType.MESH
 
 
-def circular(x, width):
+def pieces(x, height, width):
     fields, levels, rows, cols = x.shape
-    gap_rows = 16 - 2 * width
     up = [(i, (i + 1) % lax.axis_size("gx")) for i in range(lax.axis_size("gx"))]
     down = [(j, i) for i, j in up]
-    north = lax.ppermute(x[:, :, rows - width:], "gx", up)
-    south = lax.ppermute(x[:, :, :width], "gx", down)
-    gap = jnp.zeros((fields, levels, gap_rows, cols), x.dtype)
-    tall = jnp.concatenate([x, south, gap, north], 2)
+    north = lax.ppermute(x[:, :, rows - height:], "gx", up)
+    south = lax.ppermute(x[:, :, :height], "gx", down)
+    tall = jnp.concatenate([x, south, north], 2)
     right = [(i, i + 1) for i in range(lax.axis_size("gy") - 1)]
     left = [(j, i) for i, j in right]
     east = lax.ppermute(tall[..., :width], "gy", left)
     west = lax.ppermute(tall[..., cols - width:], "gy", right)
-    middle = jnp.zeros((fields, levels, rows + 16, 128 - 2 * width), x.dtype)
-    return jnp.concatenate([tall, east, middle, west], 3)
-
-
-def diffusion_kernel(steps, rows, cols, v_ref, c_ref, o_ref):
-    height, span = v_ref.shape[2], v_ref.shape[3]
+    middle = jnp.zeros((fields, levels, rows + 2 * height, 128 - 2 * width), x.dtype)
+    edge = jnp.concatenate([east, middle, west], 3)
+    return tall, south, north, edge
+
+
+def circular(x, height, width):
+    tall, _, _, edge = pieces(x, height, width)
+    return jnp.concatenate([tall, edge], 3)
+
+
+def diffusion_kernel(steps, rows, cols, x_ref, s_ref, n_ref, e_ref, c_ref, o_ref):
+    height, span = c_ref.shape[2], c_ref.shape[3]
     fields = o_ref.shape[0]
     along_i = c_ref[0, 0]
     along_j = c_ref[1, 0]
@@ -37,7 +41,9 @@
     weight_i = along_i * sea * pltpu.roll(sea, height - 1, 0)
     weight_j = along_j * sea * pltpu.roll(sea, span - 1, 1)
     for f in range(fields):
-        values = v_ref[f, 0]
+        values = jnp.concatenate(
+            [jnp.concatenate([x_ref[f, 0], s_ref[f, 0], n_ref[f, 0]], 0), e_ref[f, 0]], 1
+        )
         for s in range(steps):
             flux_i = weight_i * (pltpu.roll(values, height - 1, 0) - values)
             flux_j = weight_j * (pltpu.roll(values, span - 1, 1) - values)
@@ -47,18 +53,22 @@
 
 def diffusion(values, coefs, steps):
     fields, levels, rows, cols = values.shape
-    ext = circular(values, steps)
-    height, span = ext.shape[2], ext.shape[3]
+    _, south, north, edge = pieces(values, 2 * steps, steps)
+    height, span = coefs.shape[2], coefs.shape[3]
+    band = south.shape[2]
     return pl.pallas_call(
         functools.partial(diffusion_kernel, steps, rows, cols),
         out_shape=jax.ShapeDtypeStruct(values.shape, values.dtype),
         grid=(levels,),
         in_specs=[
-            pl.BlockSpec((fields, 1, height, span), lambda l: (0, l, 0, 0)),
+            pl.BlockSpec((fields, 1, rows, cols), lambda l: (0, l, 0, 0)),
+            pl.BlockSpec((fields, 1, band, cols), lambda l: (0, l, 0, 0)),
+            pl.BlockSpec((fields, 1, band, cols), lambda l: (0, l, 0, 0)),
+            pl.BlockSpec((fields, 1, height, 128), lambda l: (0, l, 0, 0)),
             pl.BlockSpec((coefs.shape[0], 1, height, span), lambda l: (0, l, 0, 0)),
         ],
         out_specs=pl.BlockSpec((fields, 1, rows, cols), lambda l: (0, l, 0, 0)),
-    )(ext, coefs)
+    )(values, south, north, edge, coefs)
 
 
 def lev_exchange(x, src_axis, dst_axis, half_axis, collective):
@@ -170,7 +180,7 @@
     balance = jnp.eye(order_count, dtype=jnp.float32) + coupling
     forward = balance.reshape(2, level_count, 2, level_count)
     adjoint = jnp.transpose(forward, (2, 3, 0, 1))
-    coefs = circular(jnp.stack([diffusion_i, diffusion_j, ocean]), steps)
+    coefs = circular(jnp.stack([diffusion_i, diffusion_j, ocean]), 2 * steps, steps)
     columns = to_columns(scaled, False)
     mixed = jnp.einsum("abcd,cdij->abij", adjoint, columns, precision=lax.Precision.HIGHEST)
     coefs, mixed = lax.optimization_barrier((coefs, mixed))

time: 175 us -> 176 us (level)
  the two profiles are of different devices: /device:TPU:33 before, /device:TPU:1 now
where the time goes in v9:
time: 176 us; the launch traced here: 174 us
  Pallas kernels  91.9 us (52%)
  starting transfers between devices  27.9 us (16%)
  local copies, waits for them, and re-layouts  20.7 us (12%)
  waiting for transfers between devices  16.7 us (9%)
  other arithmetic  12.7 us (7%)
  matrix products  3.57 us (2%)
    pallas_call x3, Pallas kernels, lev_exchange(): pl.pallas_call(kernel, out_shape=jax.ShapeDtypeStruct(tuple(out_shape), x...  75.6 us
    pallas_call x1, Pallas kernels, diffusion(): pl.pallas_call(functools.partial(diffusion_kernel, steps, rows, cols), ou...  16.3 us
    ppermute x2, waiting for transfers between devices, pieces(): north = lax.ppermute(x[:, :, rows - height:], 'gx', up)  9.72 us
    all_to_all x1, starting transfers between devices, to_columns(): return lax.all_to_all(x, 'lev', 2, 1, tiled=True)  9.01 us
    ppermute x2, starting transfers between devices, pieces(): east = lax.ppermute(tall[..., :width], 'gy', left)  7.58 us
    ppermute x2, starting transfers between devices, pieces(): south = lax.ppermute(x[:, :, :height], 'gx', down)  6.52 us
    ppermute x2, waiting for transfers between devices, pieces(): south = lax.ppermute(x[:, :, :height], 'gx', down)  6.34 us
    slice x4, local copies, waits for them, and re-layouts, pieces(): east = lax.ppermute(tall[..., :width], 'gy', left)  5.6 us
  transfers between devices with their start and end apart: 9, of which 5 were waited for; matrix products, arithmetic and copies ran while one was open for 10% of the time, Pallas kernels for 0%

profile of v9, /device:TPU:1, one launch (start us, length us, event | category | flops | bytes accessed | tf_op | source)
XLA Modules:
  0.0 173.7 jit_solution(17431952115159120948)
XLA Ops:
  0.0 1.2 fusion.7
  1.3 0.1 copy-done.3
  1.4 1.5 multiply_multiply_fusion.1
  2.9 1.6 copy.18
  4.5 9.0 %all-to-all-start = ((f32[2,16,64,128]{3,1,0,2:T(8,128)}), f32[2,16,64,128]{3,1,0,2:T(8,128)}, u32[]{:S(2)}, u32[]{:S(2)}) async-start(f32[2,16,64,128]{3,1,0,2:T(8,128)} %copy.18), calls=%async_computation | async-start | bytes 2097152 | tf_op jit(solution)/shard_map/all_to_all | solution.py:159
  13.5 5.0 %collective-permute-start = (f32[3,16,8,128]{3,2,1,0:T(8,128)S(1)}, f32[3,16,8,128]{3,2,1,0:T(8,128)S(1)}, u32[]{:S(2)}, u32[]{:S(2)}) collective-permute-start(f32[3,16,8,128]{3,2,1,0:T(8,128)S(1)} %get-tuple-element.11), channel_id=1, source_target_pairs={{4,0},{8,4},{12,8},{16,12},{20,16},{24,20},{28,24},{32,28},{36,32}... | collective-permute-start | bytes 589832 | tf_op jit(solution)/shard_map/ppermute | solution.py:19
  18.5 3.2 %collective-permute-done = f32[3,16,8,128]{3,2,1,0:T(8,128)S(1)} collective-permute-done((f32[3,16,8,128]{3,2,1,0:T(8,128)S(1)}, f32[3,16,8,128]{3,2,1,0:T(8,128)S(1)}, u32[]{:S(2)}, u32[]{:S(2)}) %collective-permute-start) | collective-permute-done | bytes 196640 | tf_op jit(solution)/shard_map/ppermute | solution.py:19
  21.8 5.2 %collective-permute-done.1 = f32[3,16,8,128]{3,2,1,0:T(8,128)S(1)} collective-permute-done((f32[3,16,8,128]{3,2,1,0:T(8,128)S(1)}, f32[3,16,8,128]{3,2,1,0:T(8,128)S(1)}, u32[]{:S(2)}, u32[]{:S(2)}) %collective-permute-start.1) | collective-permute-done | bytes 196640 | tf_op jit(solution)/shard_map/ppermute | solution.py:18
  27.0 0.7 copy-done.8
  27.7 0.2 pad_maximum_fusion.1
  27.9 2.0 %fusion.4 = (f32[3,16,80,4]{3,2,1,0:T(8,128)}, f32[3,16,80,4]{3,2,1,0:T(8,128)S(1)}) fusion(f32[3,16,80,128]{3,2,1,0:T(8,128)S(1)} %pad_maximum_fusion.1), kind=kLoop, calls=%fused_computation.19 | loop fusion | bytes 245760 | tf_op jit(solution)/shard_map/slice | solution.py:23
  29.8 2.8 %copy.13 = f32[3,16,80,4]{2,1,3,0:T(8,128)} copy(f32[3,16,80,4]{3,2,1,0:T(8,128)} %get-tuple-element.9) | data formatting | bytes 122880 | tf_op jit(solution)/shard_map/slice | solution.py:23
  32.6 4.1 %collective-permute-start.2 = (f32[3,16,80,4]{2,1,3,0:T(8,128)}, f32[3,16,80,4]{2,1,3,0:T(8,128)}, u32[]{:S(2)}, u32[]{:S(2)}) collective-permute-start(f32[3,16,80,4]{2,1,3,0:T(8,128)} %copy.13), channel_id=1, source_target_pairs={{1,0},{2,1},{3,2},{5,4},{6,5},{7,6},{9,8},{10,9},{11,10},{13,12},{... | collective-permute-start | bytes 184328 | tf_op jit(solution)/shard_map/ppermute | solution.py:23
  36.7 1.3 copy.14
  38.0 2.5 %collective-permute-start.3 = (f32[3,16,80,4]{2,1,3,0:T(8,128)}, f32[3,16,80,4]{2,1,3,0:T(8,128)}, u32[]{:S(2)}, u32[]{:S(2)}) collective-permute-start(f32[3,16,80,4]{2,1,3,0:T(8,128)} %copy.14), channel_id=1, source_target_pairs={{0,1},{1,2},{2,3},{4,5},{5,6},{6,7},{8,9},{9,10},{10,11},{12,13},{... | collective-permute-start | bytes 184328 | tf_op jit(solution)/shard_map/ppermute | solution.py:24
  40.5 0.9 convert_add_fusion
  41.4 0.1 reshape.4
  41.5 0.8 copy.17
  42.3 0.1 pad.12.clone
  42.4 1.5 copy.15
  43.9 2.8 %copy.16 = f32[3,16,80,4]{3,2,1,0:T(8,128)} copy(f32[3,16,80,4]{2,1,3,0:T(8,128)} %collective-permute-done.3) | data formatting | bytes 122880 | tf_op jit(solution)/shard_map/ppermute | solution.py:24
  46.7 3.6 %pad_maximum_fusion.c_ref = f32[3,16,80,256]{3,2,1,0:T(8,128)} fusion(f32[3,16,80,4]{3,2,1,0:T(8,128)} %copy.16, f32[3,16,80,4]{3,2,1,0:T(8,128)S(1)} %copy.15, f32[3,16,8,128]{3,2,1,0:T(8,128)} %copy-done.8, f32[3,16,8,128]{3,2,1,0:T(8,128)} %copy-done.7, f32[1,16,64,128]{3,2,1,0:T(8,128)S(1)} %get-tuple-element.18, f32[1,16,64,128]{3,2,1,0:T(8,128)S(1)} %bitcast.30, ...), kind=kLoop, calls=%fused_computation | loop fusion | flops 6881280 | bytes 6022144 | tf_op jit(solution)/shard_map/concatenate | solution.py:32
  50.3 1.4 copy.19
  51.7 1.1 convolution_bitcast_fusion.1
  52.8 1.6 copy.20.x_ref
  54.4 28.8 %shard_map.64 = f32[2,16,64,128]{3,2,1,0:T(8,128)} custom-call(f32[2,64,16,128]{3,2,1,0:T(8,128)} %copy.20.x_ref), custom_call_target="tpu_custom_call" | custom-call | tf_op jit(solution)/shard_map/pallas_call | solution.py:141
  83.2 1.3 broadcast_multiply_fusion.x_ref
  84.6 1.5 collective-permute-start.4
  86.1 3.1 %collective-permute-done.4.s_ref = f32[2,16,8,128]{3,2,1,0:T(8,128)S(1)} collective-permute-done((f32[2,16,8,128]{3,2,1,0:T(8,128)S(1)}, f32[2,16,8,128]{3,2,1,0:T(8,128)S(1)}, u32[]{:S(2)}, u32[]{:S(2)}) %collective-permute-start.4) | collective-permute-done | bytes 131104 | tf_op jit(solution)/shard_map/ppermute | solution.py:19
  89.2 4.5 %collective-permute-done.5.n_ref = f32[2,16,8,128]{3,2,1,0:T(8,128)S(1)} collective-permute-done((f32[2,16,8,128]{3,2,1,0:T(8,128)S(1)}, f32[2,16,8,128]{3,2,1,0:T(8,128)S(1)}, u32[]{:S(2)}, u32[]{:S(2)}) %collective-permute-start.5) | collective-permute-done | bytes 131104 | tf_op jit(solution)/shard_map/ppermute | solution.py:18
  93.7 0.1 pad_maximum_fusion.2
  93.8 0.4 fusion.5
  94.3 0.1 copy-done.11
  94.4 0.4 copy.21
  94.8 3.5 %collective-permute-start.6 = (f32[2,16,80,4]{2,1,3,0:T(8,128)S(1)}, f32[2,16,80,4]{2,1,3,0:T(8,128)S(1)}, u32[]{:S(2)}, u32[]{:S(2)}) collective-permute-start(f32[2,16,80,4]{2,1,3,0:T(8,128)S(1)} %copy.21), channel_id=1, source_target_pairs={{1,0},{2,1},{3,2},{5,4},{6,5},{7,6},{9,8},{10,9},{11,10},{13,12},{... | collective-permute-start | bytes 122888 | tf_op jit(solution)/shard_map/ppermute | solution.py:23
  98.3 0.4 copy.22
  98.7 2.2 %collective-permute-start.7 = (f32[2,16,80,4]{2,1,3,0:T(8,128)S(1)}, f32[2,16,80,4]{2,1,3,0:T(8,128)S(1)}, u32[]{:S(2)}, u32[]{:S(2)}) collective-permute-start(f32[2,16,80,4]{2,1,3,0:T(8,128)S(1)} %copy.22), channel_id=1, source_target_pairs={{0,1},{1,2},{2,3},{4,5},{5,6},{6,7},{8,9},{9,10},{10,11},{12,13},{... | collective-permute-start | bytes 122888 | tf_op jit(solution)/shard_map/ppermute | solution.py:24
  101.0 0.1 pad.1.clone
  101.1 0.5 copy.23
  101.5 0.6 collective-permute-done.7
  102.1 0.5 copy.24
  102.6 1.5 pad_maximum_fusion.3.e_ref
  104.1 16.3 %shard_map.65.x_ref = f32[2,16,64,128]{3,2,1,0:T(8,128)} custom-call(f32[2,16,64,128]{3,2,1,0:T(8,128)} %copy-done, f32[2,16,8,128]{3,2,1,0:T(8,128)} %copy-done.10, f32[2,16,8,128]{3,2,1,0:T(8,128)} %copy-done.11, f32[2,16,80,128]{3,2,1,0:T(8,128)} %pad_maximum_fusion.3.e_ref, f32[3,16,80,256]{3,2,1,0:T(8,128)} %pad_maximum_fusion.c_ref), custom_call_target="tpu_custom_call" | custom-call | tf_op jit(solution)/shard_map/pallas_call | solution.py:59
  120.4 27.5 %shard_map.66 = f32[2,64,16,128]{3,2,1,0:T(8,128)} custom-call(f32[2,16,64,128]{3,2,1,0:T(8,128)} %shard_map.65.x_ref), custom_call_target="tpu_custom_call" | custom-call | tf_op jit(solution)/shard_map/pallas_call | solution.py:141
  147.9 2.5 %convolution_bitcast_fusion = f32[2,64,16,128]{3,1,2,0:T(8,128)S(1)} fusion(f32[2,64,16,128]{3,2,1,0:T(8,128)} %shard_map.66, f32[2,64,2,64,1]{3,2,1,0,4:T(2,128)S(1)} %bitcast.35), kind=kOutput, calls=%fused_computation.2 | convolution fusion | flops 402653184 | bytes 2162688 | tf_op jit(solution)/shard_map/abcd,cdij->abij/dot_general | solution.py:170
  150.5 1.6 copy.27.x_ref
  152.1 19.3 %shard_map.67 = f32[2,16,64,128]{3,2,1,0:T(8,128)} custom-call(f32[2,64,16,128]{3,2,1,0:T(8,128)} %copy.27.x_ref), custom_call_target="tpu_custom_call" | custom-call | tf_op jit(solution)/shard_map/pallas_call | solution.py:141
  171.3 2.4 %multiply_multiply_fusion = f32[2,16,64,128]{3,2,1,0:T(8,128)} fusion(f32[2,16,64,128]{3,2,1,0:T(8,128)} %shard_map.67, f32[2,16,64,128]{3,2,1,0:T(8,128)S(1)} %copy-done.4, f32[16,64,128]{2,1,0:T(8,128)S(1)} %get-tuple-element.17), kind=kLoop, calls=%fused_computation.8 | loop fusion | flops 524288 | bytes 3670016 | tf_op jit(solution)/shard_map/mul | solution.py:190
  (30 shorter events, 0.1 us)
Async XLA Ops:
  0.0 1.4 copy-start.3
  2.9 10.6 %copy-start.1 = (f32[16,64,128]{2,1,0:T(8,128)S(1)}, f32[16,64,128]{2,1,0:T(8,128)}, u32[]{:S(2)}) copy-start(f32[16,64,128]{2,1,0:T(8,128)} %param.9) | copy-start | bytes 1572868
  2.9 10.6 %copy-start.2 = (f32[16,64,128]{2,1,0:T(8,128)S(1)}, f32[16,64,128]{2,1,0:T(8,128)}, u32[]{:S(2)}) copy-start(f32[16,64,128]{2,1,0:T(8,128)} %param.8) | copy-start | bytes 1572868
  4.5 45.9 %all-to-all-start = ((f32[2,16,64,128]{3,1,0,2:T(8,128)}), f32[2,16,64,128]{3,1,0,2:T(8,128)}, u32[]{:S(2)}, u32[]{:S(2)}) async-start(f32[2,16,64,128]{3,1,0,2:T(8,128)} %copy.18), calls=%async_computation | async-start | bytes 2097152 | tf_op jit(solution)/shard_map/all_to_all | solution.py:159
  13.5 8.3 %collective-permute-start = (f32[3,16,8,128]{3,2,1,0:T(8,128)S(1)}, f32[3,16,8,128]{3,2,1,0:T(8,128)S(1)}, u32[]{:S(2)}, u32[]{:S(2)}) collective-permute-start(f32[3,16,8,128]{3,2,1,0:T(8,128)S(1)} %get-tuple-element.11), channel_id=1, source_target_pairs={{4,0},{8,4},{12,8},{16,12},{20,16},{24,20},{28,24},{32,28},{36,32}... | collective-permute-start | bytes 589832 | tf_op jit(solution)/shard_map/ppermute | solution.py:19
  18.5 8.5 %collective-permute-start.1 = (f32[3,16,8,128]{3,2,1,0:T(8,128)S(1)}, f32[3,16,8,128]{3,2,1,0:T(8,128)S(1)}, u32[]{:S(2)}, u32[]{:S(2)}) collective-permute-start(f32[3,16,8,128]{3,2,1,0:T(8,128)S(1)} %get-tuple-element.12), channel_id=1, source_target_pairs={{0,4},{4,8},{8,12},{12,16},{16,20},{20,24},{24,28},{28,32},{32,36}... | collective-permute-start | bytes 589832 | tf_op jit(solution)/shard_map/ppermute | solution.py:18
  21.8 5.2 %copy-start.7 = (f32[3,16,8,128]{3,2,1,0:T(8,128)}, f32[3,16,8,128]{3,2,1,0:T(8,128)S(1)}, u32[]{:S(2)}) copy-start(f32[3,16,8,128]{3,2,1,0:T(8,128)S(1)} %collective-permute-done) | copy-start | bytes 589828
  27.0 0.7 copy-start.8
  32.6 9.7 %collective-permute-start.2 = (f32[3,16,80,4]{2,1,3,0:T(8,128)}, f32[3,16,80,4]{2,1,3,0:T(8,128)}, u32[]{:S(2)}, u32[]{:S(2)}) collective-permute-start(f32[3,16,80,4]{2,1,3,0:T(8,128)} %copy.13), channel_id=1, source_target_pairs={{1,0},{2,1},{3,2},{5,4},{6,5},{7,6},{9,8},{10,9},{11,10},{13,12},{... | collective-permute-start | bytes 184328 | tf_op jit(solution)/shard_map/ppermute | solution.py:23
  38.0 5.9 %collective-permute-start.3 = (f32[3,16,80,4]{2,1,3,0:T(8,128)}, f32[3,16,80,4]{2,1,3,0:T(8,128)}, u32[]{:S(2)}, u32[]{:S(2)}) collective-permute-start(f32[3,16,80,4]{2,1,3,0:T(8,128)} %copy.14), channel_id=1, source_target_pairs={{0,1},{1,2},{2,3},{4,5},{5,6},{6,7},{8,9},{9,10},{10,11},{12,13},{... | collective-permute-start | bytes 184328 | tf_op jit(solution)/shard_map/ppermute | solution.py:24
  41.5 0.9 copy-start.5
  50.3 1.4 copy-start.9
  84.5 9.7 %copy-start = (f32[2,16,64,128]{3,2,1,0:T(8,128)}, f32[2,16,64,128]{3,2,1,0:T(8,128)S(1)}, u32[]{:S(2)}) copy-start(f32[2,16,64,128]{3,2,1,0:T(8,128)S(1)} %broadcast_multiply_fusion.x_ref) | copy-start | bytes 3145732
  84.6 4.6 %collective-permute-start.4 = (f32[2,16,8,128]{3,2,1,0:T(8,128)S(1)}, f32[2,16,8,128]{3,2,1,0:T(8,128)S(1)}, u32[]{:S(2)}, u32[]{:S(2)}) collective-permute-start(f32[2,16,8,128]{3,2,1,0:T(8,128)S(1)} %get-tuple-element.16), channel_id=1, source_target_pairs={{4,0},{8,4},{12,8},{16,12},{20,16},{24,20},{28,24},{32,28},{36,32}... | collective-permute-start | bytes 393224 | tf_op jit(solution)/shard_map/ppermute | solution.py:19
  86.1 7.6 %collective-permute-start.5 = (f32[2,16,8,128]{3,2,1,0:T(8,128)S(1)}, f32[2,16,8,128]{3,2,1,0:T(8,128)S(1)}, u32[]{:S(2)}, u32[]{:S(2)}) collective-permute-start(f32[2,16,8,128]{3,2,1,0:T(8,128)S(1)} %get-tuple-element.15), channel_id=1, source_target_pairs={{0,4},{4,8},{8,12},{12,16},{16,20},{20,24},{24,28},{28,32},{32,36}... | collective-permute-start | bytes 393224 | tf_op jit(solution)/shard_map/ppermute | solution.py:18
  89.2 5.0 %copy-start.10 = (f32[2,16,8,128]{3,2,1,0:T(8,128)}, f32[2,16,8,128]{3,2,1,0:T(8,128)S(1)}, u32[]{:S(2)}) copy-start(f32[2,16,8,128]{3,2,1,0:T(8,128)S(1)} %collective-permute-done.4.s_ref) | copy-start | bytes 393220
  93.7 0.7 copy-start.11
  94.8 6.3 %collective-permute-start.6 = (f32[2,16,80,4]{2,1,3,0:T(8,128)S(1)}, f32[2,16,80,4]{2,1,3,0:T(8,128)S(1)}, u32[]{:S(2)}, u32[]{:S(2)}) collective-permute-start(f32[2,16,80,4]{2,1,3,0:T(8,128)S(1)} %copy.21), channel_id=1, source_target_pairs={{1,0},{2,1},{3,2},{5,4},{6,5},{7,6},{9,8},{10,9},{11,10},{13,12},{... | collective-permute-start | bytes 122888 | tf_op jit(solution)/shard_map/ppermute | solution.py:23
  98.7 3.4 %collective-permute-start.7 = (f32[2,16,80,4]{2,1,3,0:T(8,128)S(1)}, f32[2,16,80,4]{2,1,3,0:T(8,128)S(1)}, u32[]{:S(2)}, u32[]{:S(2)}) collective-permute-start(f32[2,16,80,4]{2,1,3,0:T(8,128)S(1)} %copy.22), channel_id=1, source_target_pairs={{0,1},{1,2},{2,3},{4,5},{5,6},{6,7},{8,9},{9,10},{10,11},{12,13},{... | collective-permute-start | bytes 122888 | tf_op jit(solution)/shard_map/ppermute | solution.py:24
  120.4 27.5 %copy-start.6 = (f32[2,64,2,64]{3,2,1,0:T(2,128)S(1)}, f32[2,64,2,64]{3,2,1,0:T(2,128)}, u32[]{:S(2)}) copy-start(f32[2,64,2,64]{3,2,1,0:T(2,128)} %copy-done.5) | copy-start | bytes 196612
  150.5 20.9 %copy-start.4 = (f32[2,16,64,128]{3,2,1,0:T(8,128)S(1)}, f32[2,16,64,128]{3,2,1,0:T(8,128)}, u32[]{:S(2)}) copy-start(f32[2,16,64,128]{3,2,1,0:T(8,128)} %param.7) | copy-start | bytes 3145732

commit v10 on v9

--- a/solution.py
+++ b/solution.py
@@ -32,18 +32,21 @@
     return jnp.concatenate([tall, edge], 3)
 
 
-def diffusion_kernel(steps, rows, cols, x_ref, s_ref, n_ref, e_ref, c_ref, o_ref):
-    height, span = c_ref.shape[2], c_ref.shape[3]
+def plane(t_ref, s_ref, n_ref, e_ref, f):
+    tall = jnp.concatenate([t_ref[f, 0], s_ref[f, 0], n_ref[f, 0]], 0)
+    return jnp.concatenate([tall, e_ref[f, 0]], 1)
+
+
+def diffusion_kernel(steps, rows, cols, x_ref, s_ref, n_ref, e_ref, ct_ref, cs_ref, cn_ref, ce_ref, o_ref):
+    height, span = e_ref.shape[2], 2 * e_ref.shape[3]
     fields = o_ref.shape[0]
-    along_i = c_ref[0, 0]
-    along_j = c_ref[1, 0]
-    sea = c_ref[2, 0]
+    along_i = plane(ct_ref, cs_ref, cn_ref, ce_ref, 0)
+    along_j = plane(ct_ref, cs_ref, cn_ref, ce_ref, 1)
+    sea = plane(ct_ref, cs_ref, cn_ref, ce_ref, 2)
     weight_i = along_i * sea * pltpu.roll(sea, height - 1, 0)
     weight_j = along_j * sea * pltpu.roll(sea, span - 1, 1)
     for f in range(fields):
-        values = jnp.concatenate(
-            [jnp.concatenate([x_ref[f, 0], s_ref[f, 0], n_ref[f, 0]], 0), e_ref[f, 0]], 1
-        )
+        values = plane(x_ref, s_ref, n_ref, e_ref, f)
         for s in range(steps):
             flux_i = weight_i * (pltpu.roll(values, height - 1, 0) - values)
             flux_j = weight_j * (pltpu.roll(values, span - 1, 1) - values)
@@ -53,22 +56,26 @@
 
 def diffusion(values, coefs, steps):
     fields, levels, rows, cols = values.shape
-    _, south, north, edge = pieces(values, 2 * steps, steps)
-    height, span = coefs.shape[2], coefs.shape[3]
-    band = south.shape[2]
+    height = rows + 4 * steps
+    band = 2 * steps
+
+    def specs(channels):
+        return [
+            pl.BlockSpec((channels, 1, rows, cols), lambda l: (0, l, 0, 0)),
+            pl.BlockSpec((channels, 1, band, cols), lambda l: (0, l, 0, 0)),
+            pl.BlockSpec((channels, 1, band, cols), lambda l: (0, l, 0, 0)),
+            pl.BlockSpec((channels, 1, height, 128), lambda l: (0, l, 0, 0)),
+        ]
+
+    _, south, north, edge = pieces(values, band, steps)
+    _, coef_south, coef_north, coef_edge = coefs
     return pl.pallas_call(
         functools.partial(diffusion_kernel, steps, rows, cols),
         out_shape=jax.ShapeDtypeStruct(values.shape, values.dtype),
         grid=(levels,),
-        in_specs=[
-            pl.BlockSpec((fields, 1, rows, cols), lambda l: (0, l, 0, 0)),
-            pl.BlockSpec((fields, 1, band, cols), lambda l: (0, l, 0, 0)),
-            pl.BlockSpec((fields, 1, band, cols), lambda l: (0, l, 0, 0)),
-            pl.BlockSpec((fields, 1, height, 128), lambda l: (0, l, 0, 0)),
-            pl.BlockSpec((coefs.shape[0], 1, height, span), lambda l: (0, l, 0, 0)),
-        ],
+        in_specs=specs(fields) + specs(coef_edge.shape[0]),
         out_specs=pl.BlockSpec((fields, 1, rows, cols), lambda l: (0, l, 0, 0)),
-    )(values, south, north, edge, coefs)
+    )(values, south, north, edge, coefs[0], coef_south, coef_north, coef_edge)
 
 
 def lev_exchange(x, src_axis, dst_axis, half_axis, collective):
@@ -180,7 +187,8 @@
     balance = jnp.eye(order_count, dtype=jnp.float32) + coupling
     forward = balance.reshape(2, level_count, 2, level_count)
     adjoint = jnp.transpose(forward, (2, 3, 0, 1))
-    coefs = circular(jnp.stack([diffusion_i, diffusion_j, ocean]), 2 * steps, steps)
+    stacked = jnp.stack([diffusion_i, diffusion_j, ocean])
+    coefs = (stacked,) + pieces(stacked, 2 * steps, steps)[1:]
     columns = to_columns(scaled, False)
     mixed = jnp.einsum("abcd,cdij->abij", adjoint, columns, precision=lax.Precision.HIGHEST)
     coefs, mixed = lax.optimization_barrier((coefs, mixed))

time: 176 us -> 168 us (0.955)
  the two profiles are of different devices: /device:TPU:1 before, /device:TPU:33 now
where the time goes in v10:
time: 168 us; the launch traced here: 167 us
  Pallas kernels  92.9 us (55%)
  starting transfers between devices  29.3 us (17%)
  local copies, waits for them, and re-layouts  20.9 us (12%)
  other arithmetic  12.6 us (8%)
  waiting for transfers between devices  7.64 us (5%)
  matrix products  3.56 us (2%)
    pallas_call x3, Pallas kernels, lev_exchange(): pl.pallas_call(kernel, out_shape=jax.ShapeDtypeStruct(tuple(out_shape), x...  76.3 us
    pallas_call x1, Pallas kernels, diffusion(): pl.pallas_call(functools.partial(diffusion_kernel, steps, rows, cols), ou...  16.6 us
    ppermute x2, starting transfers between devices, pieces(): east = lax.ppermute(tall[..., :width], 'gy', left)  9.17 us
    ppermute x2, starting transfers between devices, pieces(): south = lax.ppermute(x[:, :, :height], 'gx', down)  8.49 us
    all_to_all x1, starting transfers between devices, to_columns(): return lax.all_to_all(x, 'lev', 2, 1, tiled=True)  7.41 us
    ppermute x2, waiting for transfers between devices, pieces(): north = lax.ppermute(x[:, :, rows - height:], 'gx', up)  6.42 us
    slice x4, local copies, waits for them, and re-layouts, pieces(): east = lax.ppermute(tall[..., :width], 'gy', left)  5.59 us
    concatenate x2, other arithmetic, pieces(): edge = jnp.concatenate([east, middle, west], 3)  4.91 us
  transfers between devices with their start and end apart: 9, of which 3 were waited for; matrix products, arithmetic and copies ran while one was open for 10% of the time, Pallas kernels for 0%

profile of v10, /device:TPU:33, one launch (start us, length us, event | category | flops | bytes accessed | tf_op | source)
XLA Modules:
  0.0 167.1 jit_solution(5278442348967299715)
XLA Ops:
  0.0 1.2 fusion.8
  1.3 0.1 copy-done.2
  1.4 1.5 multiply_multiply_fusion.1
  2.9 1.6 copy.18
  4.4 7.4 %all-to-all-start = ((f32[2,16,64,128]{3,1,0,2:T(8,128)}), f32[2,16,64,128]{3,1,0,2:T(8,128)S(1)}, u32[]{:S(2)}, u32[]{:S(2)}) async-start(f32[2,16,64,128]{3,1,0,2:T(8,128)} %copy.18), calls=%async_computation | async-start | bytes 2097152 | tf_op jit(solution)/shard_map/all_to_all | solution.py:166
  11.9 0.1 pad_maximum_fusion.2.ct_ref
  12.0 1.4 collective-permute-start.1
  13.4 3.7 %collective-permute-start = (f32[3,16,8,128]{3,2,1,0:T(8,128)S(1)}, f32[3,16,8,128]{3,2,1,0:T(8,128)S(1)}, u32[]{:S(2)}, u32[]{:S(2)}) collective-permute-start(f32[3,16,8,128]{3,2,1,0:T(8,128)S(1)} %get-tuple-element.18), channel_id=1, source_target_pairs={{4,0},{8,4},{12,8},{16,12},{20,16},{24,20},{28,24},{32,28},{36,32}... | collective-permute-start | bytes 589832 | tf_op jit(solution)/shard_map/ppermute | solution.py:19
  17.1 4.1 %collective-permute-done.1.cn_ref = f32[3,16,8,128]{3,2,1,0:T(8,128)S(1)} collective-permute-done((f32[3,16,8,128]{3,2,1,0:T(8,128)S(1)}, f32[3,16,8,128]{3,2,1,0:T(8,128)S(1)}, u32[]{:S(2)}, u32[]{:S(2)}) %collective-permute-start.1) | collective-permute-done | bytes 196640 | tf_op jit(solution)/shard_map/ppermute | solution.py:18
  21.2 0.7 copy-done.8
  21.9 0.7 copy-done.9
  22.5 0.2 pad_maximum_fusion
  22.7 2.0 %fusion.4 = (f32[3,16,80,4]{3,2,1,0:T(8,128)}, f32[3,16,80,4]{3,2,1,0:T(8,128)S(1)}) fusion(f32[3,16,80,128]{3,2,1,0:T(8,128)S(1)} %pad_maximum_fusion), kind=kLoop, calls=%fused_computation.17 | loop fusion | bytes 245760 | tf_op jit(solution)/shard_map/slice | solution.py:23
  24.7 2.8 %copy.13 = f32[3,16,80,4]{2,1,3,0:T(8,128)} copy(f32[3,16,80,4]{3,2,1,0:T(8,128)} %get-tuple-element.15) | data formatting | bytes 122880 | tf_op jit(solution)/shard_map/slice | solution.py:23
  27.5 1.3 copy.14
  28.7 1.3 collective-permute-start.3
  30.0 4.9 %collective-permute-start.2 = (f32[3,16,80,4]{2,1,3,0:T(8,128)}, f32[3,16,80,4]{2,1,3,0:T(8,128)}, u32[]{:S(2)}, u32[]{:S(2)}) collective-permute-start(f32[3,16,80,4]{2,1,3,0:T(8,128)} %copy.13), channel_id=1, source_target_pairs={{1,0},{2,1},{3,2},{5,4},{6,5},{7,6},{9,8},{10,9},{11,10},{13,12},{... | collective-permute-start | bytes 184328 | tf_op jit(solution)/shard_map/ppermute | solution.py:23
  34.9 0.9 convert_add_fusion
  35.7 0.1 reshape.4
  35.9 0.8 copy.17
  36.7 1.5 copy.15
  38.3 2.8 %copy.16 = f32[3,16,80,4]{3,2,1,0:T(8,128)} copy(f32[3,16,80,4]{2,1,3,0:T(8,128)} %collective-permute-done.3) | data formatting | bytes 122880 | tf_op jit(solution)/shard_map/ppermute | solution.py:24
  41.1 3.4 %pad_maximum_fusion.1.ce_ref = f32[3,16,80,128]{3,2,1,0:T(8,128)} fusion(f32[3,16,80,4]{3,2,1,0:T(8,128)} %copy.16, f32[3,16,80,4]{3,2,1,0:T(8,128)S(1)} %copy.15, f32[128]{0:T(128)S(1)} %pad.7.clone), kind=kLoop, calls=%fused_computation.1 | loop fusion | flops 983040 | bytes 2089472 | tf_op jit(solution)/shard_map/concatenate | solution.py:26
  44.5 0.1 copy.19
  44.6 0.8 copy-done.10
  45.4 1.1 convolution_bitcast_fusion.1
  46.5 1.6 copy.20.x_ref
  48.1 28.9 %shard_map.64 = f32[2,16,64,128]{3,2,1,0:T(8,128)} custom-call(f32[2,64,16,128]{3,2,1,0:T(8,128)} %copy.20.x_ref), custom_call_target="tpu_custom_call" | custom-call | tf_op jit(solution)/shard_map/pallas_call | solution.py:148
  77.0 1.3 broadcast_multiply_fusion.x_ref
  78.5 4.8 %collective-permute-start.4 = (f32[2,16,8,128]{3,2,1,0:T(8,128)S(1)}, f32[2,16,8,128]{3,2,1,0:T(8,128)S(1)}, u32[]{:S(2)}, u32[]{:S(2)}) collective-permute-start(f32[2,16,8,128]{3,2,1,0:T(8,128)S(1)} %get-tuple-element.22), channel_id=1, source_target_pairs={{4,0},{8,4},{12,8},{16,12},{20,16},{24,20},{28,24},{32,28},{36,32}... | collective-permute-start | bytes 393224 | tf_op jit(solution)/shard_map/ppermute | solution.py:19
  83.2 2.4 %collective-permute-done.5.n_ref = f32[2,16,8,128]{3,2,1,0:T(8,128)S(1)} collective-permute-done((f32[2,16,8,128]{3,2,1,0:T(8,128)S(1)}, f32[2,16,8,128]{3,2,1,0:T(8,128)S(1)}, u32[]{:S(2)}, u32[]{:S(2)}) %collective-permute-start.5) | collective-permute-done | bytes 131104 | tf_op jit(solution)/shard_map/ppermute | solution.py:18
  85.6 0.1 pad_maximum_fusion.3
  85.7 0.4 fusion.6
  86.1 0.1 copy-done.11
  86.3 0.4 copy.21
  86.7 4.3 %collective-permute-start.6 = (f32[2,16,80,4]{2,1,3,0:T(8,128)S(1)}, f32[2,16,80,4]{2,1,3,0:T(8,128)S(1)}, u32[]{:S(2)}, u32[]{:S(2)}) collective-permute-start(f32[2,16,80,4]{2,1,3,0:T(8,128)S(1)} %copy.21), channel_id=1, source_target_pairs={{1,0},{2,1},{3,2},{5,4},{6,5},{7,6},{9,8},{10,9},{11,10},{13,12},{... | collective-permute-start | bytes 122888 | tf_op jit(solution)/shard_map/ppermute | solution.py:23
  91.0 0.4 copy.22
  91.5 1.5 collective-permute-start.7
  93.0 0.5 copy.23
  93.4 1.2 collective-permute-done.7
  94.6 0.5 copy.24
  95.1 1.5 pad_maximum_fusion.4.e_ref
  96.6 16.6 %shard_map.65.x_ref = f32[2,16,64,128]{3,2,1,0:T(8,128)} custom-call(f32[2,16,64,128]{3,2,1,0:T(8,128)} %copy-done, f32[2,16,8,128]{3,2,1,0:T(8,128)} %copy-done.12, f32[2,16,8,128]{3,2,1,0:T(8,128)} %copy-done.11, f32[2,16,80,128]{3,2,1,0:T(8,128)} %pad_maximum_fusion.4.e_ref, f32[3,16,64,128]{3,2,1,0:T(8,128)} %copy-done.1, f32[3,16,8,128]{3,2,1,0:T(8,128)} %copy-done.9, ...), custom_call_target="tpu_custom_call" | custom-call | tf_op jit(solution)/shard_map/pallas_call | solution.py:72
  113.2 27.4 %shard_map.66 = f32[2,64,16,128]{3,2,1,0:T(8,128)} custom-call(f32[2,16,64,128]{3,2,1,0:T(8,128)} %shard_map.65.x_ref), custom_call_target="tpu_custom_call" | custom-call | tf_op jit(solution)/shard_map/pallas_call | solution.py:148
  140.6 2.5 %convolution_bitcast_fusion = f32[2,64,16,128]{3,1,2,0:T(8,128)S(1)} fusion(f32[2,64,16,128]{3,2,1,0:T(8,128)} %shard_map.66, f32[2,64,2,64,1]{3,2,1,0,4:T(2,128)S(1)} %bitcast.34), kind=kOutput, calls=%fused_computation.3 | convolution fusion | flops 402653184 | bytes 2162688 | tf_op jit(solution)/shard_map/abcd,cdij->abij/dot_general | solution.py:177
  143.1 1.6 copy.27.x_ref
  144.7 20.0 %shard_map.67 = f32[2,16,64,128]{3,2,1,0:T(8,128)} custom-call(f32[2,64,16,128]{3,2,1,0:T(8,128)} %copy.27.x_ref), custom_call_target="tpu_custom_call" | custom-call | tf_op jit(solution)/shard_map/pallas_call | solution.py:148
  164.7 2.4 %multiply_multiply_fusion = f32[2,16,64,128]{3,2,1,0:T(8,128)} fusion(f32[2,16,64,128]{3,2,1,0:T(8,128)} %shard_map.67, f32[2,16,64,128]{3,2,1,0:T(8,128)S(1)} %copy-done.3, f32[16,64,128]{2,1,0:T(8,128)S(1)} %get-tuple-element.23), kind=kLoop, calls=%fused_computation.9 | loop fusion | flops 524288 | bytes 3670016 | tf_op jit(solution)/shard_map/mul | solution.py:198
  (32 shorter events, 0.3 us)
Async XLA Ops:
  0.0 1.4 copy-start.2
  4.4 7.4 %copy-start.4 = (f32[16,64,128]{2,1,0:T(8,128)S(1)}, f32[16,64,128]{2,1,0:T(8,128)}, u32[]{:S(2)}) copy-start(f32[16,64,128]{2,1,0:T(8,128)} %param.9) | copy-start | bytes 1572868
  4.4 7.4 %copy-start.5 = (f32[16,64,128]{2,1,0:T(8,128)S(1)}, f32[16,64,128]{2,1,0:T(8,128)}, u32[]{:S(2)}) copy-start(f32[16,64,128]{2,1,0:T(8,128)} %param.8) | copy-start | bytes 1572868
  4.4 40.1 %all-to-all-start = ((f32[2,16,64,128]{3,1,0,2:T(8,128)}), f32[2,16,64,128]{3,1,0,2:T(8,128)S(1)}, u32[]{:S(2)}, u32[]{:S(2)}) async-start(f32[2,16,64,128]{3,1,0,2:T(8,128)} %copy.18), calls=%async_computation | async-start | bytes 2097152 | tf_op jit(solution)/shard_map/all_to_all | solution.py:166
  12.0 10.7 %copy-start.1 = (f32[3,16,64,128]{3,2,1,0:T(8,128)}, f32[3,16,64,128]{3,2,1,0:T(8,128)S(1)}, u32[]{:S(2)}) copy-start(f32[3,16,64,128]{3,2,1,0:T(8,128)S(1)} %pad_maximum_fusion.2.ct_ref) | copy-start | bytes 4718596
  12.0 9.2 %collective-permute-start.1 = (f32[3,16,8,128]{3,2,1,0:T(8,128)S(1)}, f32[3,16,8,128]{3,2,1,0:T(8,128)S(1)}, u32[]{:S(2)}, u32[]{:S(2)}) collective-permute-start(f32[3,16,8,128]{3,2,1,0:T(8,128)S(1)} %get-tuple-element.17), channel_id=1, source_target_pairs={{0,4},{4,8},{8,12},{12,16},{16,20},{20,24},{24,28},{28,32},{32,36}... | collective-permute-start | bytes 589832 | tf_op jit(solution)/shard_map/ppermute | solution.py:18
  13.4 7.8 %collective-permute-start = (f32[3,16,8,128]{3,2,1,0:T(8,128)S(1)}, f32[3,16,8,128]{3,2,1,0:T(8,128)S(1)}, u32[]{:S(2)}, u32[]{:S(2)}) collective-permute-start(f32[3,16,8,128]{3,2,1,0:T(8,128)S(1)} %get-tuple-element.18), channel_id=1, source_target_pairs={{4,0},{8,4},{12,8},{16,12},{20,16},{24,20},{28,24},{32,28},{36,32}... | collective-permute-start | bytes 589832 | tf_op jit(solution)/shard_map/ppermute | solution.py:19
  21.2 0.7 copy-start.8
  21.9 0.7 copy-start.9
  28.7 9.5 %collective-permute-start.3 = (f32[3,16,80,4]{2,1,3,0:T(8,128)}, f32[3,16,80,4]{2,1,3,0:T(8,128)}, u32[]{:S(2)}, u32[]{:S(2)}) collective-permute-start(f32[3,16,80,4]{2,1,3,0:T(8,128)} %copy.14), channel_id=1, source_target_pairs={{0,1},{1,2},{2,3},{4,5},{5,6},{6,7},{8,9},{9,10},{10,11},{12,13},{... | collective-permute-start | bytes 184328 | tf_op jit(solution)/shard_map/ppermute | solution.py:24
  30.0 6.7 %collective-permute-start.2 = (f32[3,16,80,4]{2,1,3,0:T(8,128)}, f32[3,16,80,4]{2,1,3,0:T(8,128)}, u32[]{:S(2)}, u32[]{:S(2)}) collective-permute-start(f32[3,16,80,4]{2,1,3,0:T(8,128)} %copy.13), channel_id=1, source_target_pairs={{1,0},{2,1},{3,2},{5,4},{6,5},{7,6},{9,8},{10,9},{11,10},{13,12},{... | collective-permute-start | bytes 184328 | tf_op jit(solution)/shard_map/ppermute | solution.py:23
  35.9 0.9 copy-start.6
  44.5 0.9 copy-start.10
  78.3 7.4 %copy-start = (f32[2,16,64,128]{3,2,1,0:T(8,128)}, f32[2,16,64,128]{3,2,1,0:T(8,128)S(1)}, u32[]{:S(2)}) copy-start(f32[2,16,64,128]{3,2,1,0:T(8,128)S(1)} %broadcast_multiply_fusion.x_ref) | copy-start | bytes 3145732
  78.4 7.2 %collective-permute-start.5 = (f32[2,16,8,128]{3,2,1,0:T(8,128)S(1)}, f32[2,16,8,128]{3,2,1,0:T(8,128)S(1)}, u32[]{:S(2)}, u32[]{:S(2)}) collective-permute-start(f32[2,16,8,128]{3,2,1,0:T(8,128)S(1)} %get-tuple-element.21), channel_id=1, source_target_pairs={{0,4},{4,8},{8,12},{12,16},{16,20},{20,24},{24,28},{28,32},{32,36}... | collective-permute-start | bytes 393224 | tf_op jit(solution)/shard_map/ppermute | solution.py:18
  78.5 7.1 %collective-permute-start.4 = (f32[2,16,8,128]{3,2,1,0:T(8,128)S(1)}, f32[2,16,8,128]{3,2,1,0:T(8,128)S(1)}, u32[]{:S(2)}, u32[]{:S(2)}) collective-permute-start(f32[2,16,8,128]{3,2,1,0:T(8,128)S(1)} %get-tuple-element.22), channel_id=1, source_target_pairs={{4,0},{8,4},{12,8},{16,12},{20,16},{24,20},{28,24},{32,28},{36,32}... | collective-permute-start | bytes 393224 | tf_op jit(solution)/shard_map/ppermute | solution.py:19
  85.6 0.6 copy-start.11
  85.6 0.7 copy-start.12
  86.7 6.2 %collective-permute-start.6 = (f32[2,16,80,4]{2,1,3,0:T(8,128)S(1)}, f32[2,16,80,4]{2,1,3,0:T(8,128)S(1)}, u32[]{:S(2)}, u32[]{:S(2)}) collective-permute-start(f32[2,16,80,4]{2,1,3,0:T(8,128)S(1)} %copy.21), channel_id=1, source_target_pairs={{1,0},{2,1},{3,2},{5,4},{6,5},{7,6},{9,8},{10,9},{11,10},{13,12},{... | collective-permute-start | bytes 122888 | tf_op jit(solution)/shard_map/ppermute | solution.py:23
  91.5 3.2 %collective-permute-start.7 = (f32[2,16,80,4]{2,1,3,0:T(8,128)S(1)}, f32[2,16,80,4]{2,1,3,0:T(8,128)S(1)}, u32[]{:S(2)}, u32[]{:S(2)}) collective-permute-start(f32[2,16,80,4]{2,1,3,0:T(8,128)S(1)} %copy.22), channel_id=1, source_target_pairs={{0,1},{1,2},{2,3},{4,5},{5,6},{6,7},{8,9},{9,10},{10,11},{12,13},{... | collective-permute-start | bytes 122888 | tf_op jit(solution)/shard_map/ppermute | solution.py:24
  113.2 27.4 %copy-start.7 = (f32[2,64,2,64]{3,2,1,0:T(2,128)S(1)}, f32[2,64,2,64]{3,2,1,0:T(2,128)}, u32[]{:S(2)}) copy-start(f32[2,64,2,64]{3,2,1,0:T(2,128)} %copy-done.6) | copy-start | bytes 196612
  144.7 20.0 %copy-start.3 = (f32[2,16,64,128]{3,2,1,0:T(8,128)S(1)}, f32[2,16,64,128]{3,2,1,0:T(8,128)}, u32[]{:S(2)}) copy-start(f32[2,16,64,128]{3,2,1,0:T(8,128)} %param.7) | copy-start | bytes 3145732

commit v11 on v10

--- a/solution.py
+++ b/solution.py
@@ -46,7 +46,7 @@
     weight_i = along_i * sea * pltpu.roll(sea, height - 1, 0)
     weight_j = along_j * sea * pltpu.roll(sea, span - 1, 1)
     for f in range(fields):
-        values = plane(x_ref, s_ref, n_ref, e_ref, f)
+        values = plane(x_ref, s_ref, n_ref, e_ref, f) * sea
         for s in range(steps):
             flux_i = weight_i * (pltpu.roll(values, height - 1, 0) - values)
             flux_j = weight_j * (pltpu.roll(values, span - 1, 1) - values)
@@ -192,7 +192,7 @@
     columns = to_columns(scaled, False)
     mixed = jnp.einsum("abcd,cdij->abij", adjoint, columns, precision=lax.Precision.HIGHEST)
     coefs, mixed = lax.optimization_barrier((coefs, mixed))
-    adjoint_mixed = to_levels(mixed) * ocean[None]
+    adjoint_mixed = to_levels(mixed)
     spread = diffusion(adjoint_mixed, coefs, steps)
     forward_mixed = level_mix(spread, forward)
     return ocean[None] * norm_gain * forward_mixed

time: 168 us -> 169 us (level)
  no operation moved by 1% of the time
where the time goes in v11:
time: 169 us; the launch traced here: 168 us
  Pallas kernels  92.9 us (55%)
  starting transfers between devices  29.3 us (17%)
  local copies, waits for them, and re-layouts  21.7 us (13%)
  other arithmetic  12.6 us (7%)
  waiting for transfers between devices  7.64 us (5%)
  matrix products  3.56 us (2%)
    pallas_call x3, Pallas kernels, lev_exchange(): pl.pallas_call(kernel, out_shape=jax.ShapeDtypeStruct(tuple(out_shape), x...  76.3 us
    pallas_call x1, Pallas kernels, diffusion(): pl.pallas_call(functools.partial(diffusion_kernel, steps, rows, cols), ou...  16.6 us
    ppermute x2, starting transfers between devices, pieces(): east = lax.ppermute(tall[..., :width], 'gy', left)  9.17 us
    ppermute x2, starting transfers between devices, pieces(): south = lax.ppermute(x[:, :, :height], 'gx', down)  8.49 us
    all_to_all x1, starting transfers between devices, to_columns(): return lax.all_to_all(x, 'lev', 2, 1, tiled=True)  7.41 us
    ppermute x2, waiting for transfers between devices, pieces(): north = lax.ppermute(x[:, :, rows - height:], 'gx', up)  6.42 us
    slice x4, local copies, waits for them, and re-layouts, pieces(): east = lax.ppermute(tall[..., :width], 'gy', left)  5.58 us
    concatenate x2, other arithmetic, pieces(): edge = jnp.concatenate([east, middle, west], 3)  4.93 us
  transfers between devices with their start and end apart: 9, of which 3 were waited for; matrix products, arithmetic and copies ran while one was open for 10% of the time, Pallas kernels for 0%

profile of v11, /device:TPU:33, one launch (start us, length us, event | category | flops | bytes accessed | tf_op | source)
XLA Modules:
  0.0 167.9 jit_solution(1649254571435395031)
XLA Ops:
  0.0 1.2 fusion.8
  1.3 0.1 copy-done.1
  1.4 1.5 multiply_multiply_fusion.1
  2.9 1.6 copy.18
  4.4 7.4 %all-to-all-start = ((f32[2,16,64,128]{3,1,0,2:T(8,128)}), f32[2,16,64,128]{3,1,0,2:T(8,128)S(1)}, u32[]{:S(2)}, u32[]{:S(2)}) async-start(f32[2,16,64,128]{3,1,0,2:T(8,128)} %copy.18), calls=%async_computation | async-start | bytes 2097152 | tf_op jit(solution)/shard_map/all_to_all | solution.py:166
  11.9 0.1 pad_maximum_fusion.2.ct_ref
  12.0 1.4 collective-permute-start.1
  13.4 3.7 %collective-permute-start = (f32[3,16,8,128]{3,2,1,0:T(8,128)S(1)}, f32[3,16,8,128]{3,2,1,0:T(8,128)S(1)}, u32[]{:S(2)}, u32[]{:S(2)}) collective-permute-start(f32[3,16,8,128]{3,2,1,0:T(8,128)S(1)} %get-tuple-element.18), channel_id=1, source_target_pairs={{4,0},{8,4},{12,8},{16,12},{20,16},{24,20},{28,24},{32,28},{36,32}... | collective-permute-start | bytes 589832 | tf_op jit(solution)/shard_map/ppermute | solution.py:19
  17.1 4.1 %collective-permute-done.1.cn_ref = f32[3,16,8,128]{3,2,1,0:T(8,128)S(1)} collective-permute-done((f32[3,16,8,128]{3,2,1,0:T(8,128)S(1)}, f32[3,16,8,128]{3,2,1,0:T(8,128)S(1)}, u32[]{:S(2)}, u32[]{:S(2)}) %collective-permute-start.1) | collective-permute-done | bytes 196640 | tf_op jit(solution)/shard_map/ppermute | solution.py:18
  21.2 0.7 copy-done.7
  21.9 0.7 copy-done.8
  22.5 0.2 pad_maximum_fusion
  22.7 1.9 %fusion.4 = (f32[3,16,80,4]{3,2,1,0:T(8,128)}, f32[3,16,80,4]{3,2,1,0:T(8,128)S(1)}) fusion(f32[3,16,80,128]{3,2,1,0:T(8,128)S(1)} %pad_maximum_fusion), kind=kLoop, calls=%fused_computation.16 | loop fusion | bytes 245760 | tf_op jit(solution)/shard_map/slice | solution.py:23
  24.7 2.8 %copy.13 = f32[3,16,80,4]{2,1,3,0:T(8,128)} copy(f32[3,16,80,4]{3,2,1,0:T(8,128)} %get-tuple-element.15) | data formatting | bytes 122880 | tf_op jit(solution)/shard_map/slice | solution.py:23
  27.5 1.3 copy.14
  28.7 1.3 collective-permute-start.3
  30.0 4.9 %collective-permute-start.2 = (f32[3,16,80,4]{2,1,3,0:T(8,128)}, f32[3,16,80,4]{2,1,3,0:T(8,128)}, u32[]{:S(2)}, u32[]{:S(2)}) collective-permute-start(f32[3,16,80,4]{2,1,3,0:T(8,128)} %copy.13), channel_id=1, source_target_pairs={{1,0},{2,1},{3,2},{5,4},{6,5},{7,6},{9,8},{10,9},{11,10},{13,12},{... | collective-permute-start | bytes 184328 | tf_op jit(solution)/shard_map/ppermute | solution.py:23
  34.9 0.9 convert_add_fusion
  35.7 0.1 reshape.4
  35.9 0.8 copy.17
  36.7 1.5 copy.15
  38.3 2.9 %copy.16 = f32[3,16,80,4]{3,2,1,0:T(8,128)} copy(f32[3,16,80,4]{2,1,3,0:T(8,128)} %collective-permute-done.3) | data formatting | bytes 122880 | tf_op jit(solution)/shard_map/ppermute | solution.py:24
  41.1 3.4 %pad_maximum_fusion.1.ce_ref = f32[3,16,80,128]{3,2,1,0:T(8,128)} fusion(f32[3,16,80,4]{3,2,1,0:T(8,128)} %copy.16, f32[3,16,80,4]{3,2,1,0:T(8,128)S(1)} %copy.15, f32[128]{0:T(128)S(1)} %pad.7.clone), kind=kLoop, calls=%fused_computation.1 | loop fusion | flops 983040 | bytes 2089472 | tf_op jit(solution)/shard_map/concatenate | solution.py:26
  44.5 0.1 copy.19
  44.7 0.8 copy-done.9
  45.4 1.1 convolution_bitcast_fusion.1
  46.5 1.6 copy.20.x_ref
  48.1 29.0 %shard_map.64.x_ref = f32[2,16,64,128]{3,2,1,0:T(8,128)} custom-call(f32[2,64,16,128]{3,2,1,0:T(8,128)} %copy.20.x_ref), custom_call_target="tpu_custom_call" | custom-call | tf_op jit(solution)/shard_map/pallas_call | solution.py:148
  77.0 1.0 fusion.7
  78.0 0.1 collective-permute-start.5
  78.1 4.8 %collective-permute-start.4 = (f32[2,16,8,128]{3,2,1,0:T(8,128)S(1)}, f32[2,16,8,128]{3,2,1,0:T(8,128)S(1)}, u32[]{:S(2)}, u32[]{:S(2)}) collective-permute-start(f32[2,16,8,128]{3,2,1,0:T(8,128)S(1)} %get-tuple-element.22), channel_id=1, source_target_pairs={{4,0},{8,4},{12,8},{16,12},{20,16},{24,20},{28,24},{32,28},{36,32}... | collective-permute-start | bytes 393224 | tf_op jit(solution)/shard_map/ppermute | solution.py:19
  82.9 2.4 %collective-permute-done.5.n_ref = f32[2,16,8,128]{3,2,1,0:T(8,128)S(1)} collective-permute-done((f32[2,16,8,128]{3,2,1,0:T(8,128)S(1)}, f32[2,16,8,128]{3,2,1,0:T(8,128)S(1)}, u32[]{:S(2)}, u32[]{:S(2)}) %collective-permute-start.5) | collective-permute-done | bytes 131104 | tf_op jit(solution)/shard_map/ppermute | solution.py:18
  85.3 1.4 pad_maximum_fusion.3
  86.7 0.4 fusion.6
  87.1 0.4 copy.21
  87.6 4.3 %collective-permute-start.6 = (f32[2,16,80,4]{2,1,3,0:T(8,128)S(1)}, f32[2,16,80,4]{2,1,3,0:T(8,128)S(1)}, u32[]{:S(2)}, u32[]{:S(2)}) collective-permute-start(f32[2,16,80,4]{2,1,3,0:T(8,128)S(1)} %copy.21), channel_id=1, source_target_pairs={{1,0},{2,1},{3,2},{5,4},{6,5},{7,6},{9,8},{10,9},{11,10},{13,12},{... | collective-permute-start | bytes 122888 | tf_op jit(solution)/shard_map/ppermute | solution.py:23
  91.9 0.4 copy.22
  92.3 1.5 collective-permute-start.7
  93.8 0.5 copy.23
  94.2 1.2 collective-permute-done.7
  95.4 0.5 copy.24
  95.9 1.5 pad_maximum_fusion.4.e_ref
  97.4 16.6 %shard_map.65.x_ref = f32[2,16,64,128]{3,2,1,0:T(8,128)} custom-call(f32[2,16,64,128]{3,2,1,0:T(8,128)} %shard_map.64.x_ref, f32[2,16,8,128]{3,2,1,0:T(8,128)} %copy-done.11, f32[2,16,8,128]{3,2,1,0:T(8,128)} %copy-done.10, f32[2,16,80,128]{3,2,1,0:T(8,128)} %pad_maximum_fusion.4.e_ref, f32[3,16,64,128]{3,2,1,0:T(8,128)} %copy-done, ...), custom_call_target="tpu_custom_call" | custom-call | tf_op jit(solution)/shard_map/pallas_call | solution.py:72
  114.0 27.4 %shard_map.66 = f32[2,64,16,128]{3,2,1,0:T(8,128)} custom-call(f32[2,16,64,128]{3,2,1,0:T(8,128)} %shard_map.65.x_ref), custom_call_target="tpu_custom_call" | custom-call | tf_op jit(solution)/shard_map/pallas_call | solution.py:148
  141.4 2.5 %convolution_bitcast_fusion = f32[2,64,16,128]{3,1,2,0:T(8,128)S(1)} fusion(f32[2,64,16,128]{3,2,1,0:T(8,128)} %shard_map.66, f32[2,64,2,64,1]{3,2,1,0,4:T(2,128)S(1)} %bitcast.34), kind=kOutput, calls=%fused_computation.3 | convolution fusion | flops 402653184 | bytes 2162688 | tf_op jit(solution)/shard_map/abcd,cdij->abij/dot_general | solution.py:177
  143.9 1.6 copy.27.x_ref
  145.5 20.0 %shard_map.67 = f32[2,16,64,128]{3,2,1,0:T(8,128)} custom-call(f32[2,64,16,128]{3,2,1,0:T(8,128)} %copy.27.x_ref), custom_call_target="tpu_custom_call" | custom-call | tf_op jit(solution)/shard_map/pallas_call | solution.py:148
  165.5 2.4 %multiply_multiply_fusion = f32[2,16,64,128]{3,2,1,0:T(8,128)} fusion(f32[2,16,64,128]{3,2,1,0:T(8,128)} %shard_map.67, f32[2,16,64,128]{3,2,1,0:T(8,128)S(1)} %copy-done.2, f32[16,64,128]{2,1,0:T(8,128)S(1)} %get-tuple-element.23), kind=kLoop, calls=%fused_computation.9 | loop fusion | flops 524288 | bytes 3670016 | tf_op jit(solution)/shard_map/mul | solution.py:198
  (29 shorter events, 0.2 us)
Async XLA Ops:
  0.0 1.4 copy-start.1
  4.4 7.4 %copy-start.3 = (f32[16,64,128]{2,1,0:T(8,128)S(1)}, f32[16,64,128]{2,1,0:T(8,128)}, u32[]{:S(2)}) copy-start(f32[16,64,128]{2,1,0:T(8,128)} %param.9) | copy-start | bytes 1572868
  4.4 7.4 %copy-start.4 = (f32[16,64,128]{2,1,0:T(8,128)S(1)}, f32[16,64,128]{2,1,0:T(8,128)}, u32[]{:S(2)}) copy-start(f32[16,64,128]{2,1,0:T(8,128)} %param.8) | copy-start | bytes 1572868
  4.4 40.1 %all-to-all-start = ((f32[2,16,64,128]{3,1,0,2:T(8,128)}), f32[2,16,64,128]{3,1,0,2:T(8,128)S(1)}, u32[]{:S(2)}, u32[]{:S(2)}) async-start(f32[2,16,64,128]{3,1,0,2:T(8,128)} %copy.18), calls=%async_computation | async-start | bytes 2097152 | tf_op jit(solution)/shard_map/all_to_all | solution.py:166
  12.0 10.7 %copy-start = (f32[3,16,64,128]{3,2,1,0:T(8,128)}, f32[3,16,64,128]{3,2,1,0:T(8,128)S(1)}, u32[]{:S(2)}) copy-start(f32[3,16,64,128]{3,2,1,0:T(8,128)S(1)} %pad_maximum_fusion.2.ct_ref) | copy-start | bytes 4718596
  12.0 9.2 %collective-permute-start.1 = (f32[3,16,8,128]{3,2,1,0:T(8,128)S(1)}, f32[3,16,8,128]{3,2,1,0:T(8,128)S(1)}, u32[]{:S(2)}, u32[]{:S(2)}) collective-permute-start(f32[3,16,8,128]{3,2,1,0:T(8,128)S(1)} %get-tuple-element.17), channel_id=1, source_target_pairs={{0,4},{4,8},{8,12},{12,16},{16,20},{20,24},{24,28},{28,32},{32,36}... | collective-permute-start | bytes 589832 | tf_op jit(solution)/shard_map/ppermute | solution.py:18
  13.4 7.8 %collective-permute-start = (f32[3,16,8,128]{3,2,1,0:T(8,128)S(1)}, f32[3,16,8,128]{3,2,1,0:T(8,128)S(1)}, u32[]{:S(2)}, u32[]{:S(2)}) collective-permute-start(f32[3,16,8,128]{3,2,1,0:T(8,128)S(1)} %get-tuple-element.18), channel_id=1, source_target_pairs={{4,0},{8,4},{12,8},{16,12},{20,16},{24,20},{28,24},{32,28},{36,32}... | collective-permute-start | bytes 589832 | tf_op jit(solution)/shard_map/ppermute | solution.py:19
  21.2 0.7 copy-start.7
  21.9 0.7 copy-start.8
  28.7 9.5 %collective-permute-start.3 = (f32[3,16,80,4]{2,1,3,0:T(8,128)}, f32[3,16,80,4]{2,1,3,0:T(8,128)}, u32[]{:S(2)}, u32[]{:S(2)}) collective-permute-start(f32[3,16,80,4]{2,1,3,0:T(8,128)} %copy.14), channel_id=1, source_target_pairs={{0,1},{1,2},{2,3},{4,5},{5,6},{6,7},{8,9},{9,10},{10,11},{12,13},{... | collective-permute-start | bytes 184328 | tf_op jit(solution)/shard_map/ppermute | solution.py:24
  30.0 6.7 %collective-permute-start.2 = (f32[3,16,80,4]{2,1,3,0:T(8,128)}, f32[3,16,80,4]{2,1,3,0:T(8,128)}, u32[]{:S(2)}, u32[]{:S(2)}) collective-permute-start(f32[3,16,80,4]{2,1,3,0:T(8,128)} %copy.13), channel_id=1, source_target_pairs={{1,0},{2,1},{3,2},{5,4},{6,5},{7,6},{9,8},{10,9},{11,10},{13,12},{... | collective-permute-start | bytes 184328 | tf_op jit(solution)/shard_map/ppermute | solution.py:23
  35.9 0.9 copy-start.5
  44.5 0.9 copy-start.9
  78.0 7.2 %collective-permute-start.5 = (f32[2,16,8,128]{3,2,1,0:T(8,128)S(1)}, f32[2,16,8,128]{3,2,1,0:T(8,128)S(1)}, u32[]{:S(2)}, u32[]{:S(2)}) collective-permute-start(f32[2,16,8,128]{3,2,1,0:T(8,128)S(1)} %get-tuple-element.21), channel_id=1, source_target_pairs={{0,4},{4,8},{8,12},{12,16},{16,20},{20,24},{24,28},{28,32},{32,36}... | collective-permute-start | bytes 393224 | tf_op jit(solution)/shard_map/ppermute | solution.py:18
  78.1 7.1 %collective-permute-start.4 = (f32[2,16,8,128]{3,2,1,0:T(8,128)S(1)}, f32[2,16,8,128]{3,2,1,0:T(8,128)S(1)}, u32[]{:S(2)}, u32[]{:S(2)}) collective-permute-start(f32[2,16,8,128]{3,2,1,0:T(8,128)S(1)} %get-tuple-element.22), channel_id=1, source_target_pairs={{4,0},{8,4},{12,8},{16,12},{20,16},{24,20},{28,24},{32,28},{36,32}... | collective-permute-start | bytes 393224 | tf_op jit(solution)/shard_map/ppermute | solution.py:19
  85.3 1.9 %copy-start.10 = (f32[2,16,8,128]{3,2,1,0:T(8,128)}, f32[2,16,8,128]{3,2,1,0:T(8,128)S(1)}, u32[]{:S(2)}) copy-start(f32[2,16,8,128]{3,2,1,0:T(8,128)S(1)} %collective-permute-done.5.n_ref) | copy-start | bytes 393220
  85.3 1.9 %copy-start.11 = (f32[2,16,8,128]{3,2,1,0:T(8,128)}, f32[2,16,8,128]{3,2,1,0:T(8,128)S(1)}, u32[]{:S(2)}) copy-start(f32[2,16,8,128]{3,2,1,0:T(8,128)S(1)} %collective-permute-done.4.s_ref) | copy-start | bytes 393220
  87.6 6.2 %collective-permute-start.6 = (f32[2,16,80,4]{2,1,3,0:T(8,128)S(1)}, f32[2,16,80,4]{2,1,3,0:T(8,128)S(1)}, u32[]{:S(2)}, u32[]{:S(2)}) collective-permute-start(f32[2,16,80,4]{2,1,3,0:T(8,128)S(1)} %copy.21), channel_id=1, source_target_pairs={{1,0},{2,1},{3,2},{5,4},{6,5},{7,6},{9,8},{10,9},{11,10},{13,12},{... | collective-permute-start | bytes 122888 | tf_op jit(solution)/shard_map/ppermute | solution.py:23
  92.3 3.2 %collective-permute-start.7 = (f32[2,16,80,4]{2,1,3,0:T(8,128)S(1)}, f32[2,16,80,4]{2,1,3,0:T(8,128)S(1)}, u32[]{:S(2)}, u32[]{:S(2)}) collective-permute-start(f32[2,16,80,4]{2,1,3,0:T(8,128)S(1)} %copy.22), channel_id=1, source_target_pairs={{0,1},{1,2},{2,3},{4,5},{5,6},{6,7},{8,9},{9,10},{10,11},{12,13},{... | collective-permute-start | bytes 122888 | tf_op jit(solution)/shard_map/ppermute | solution.py:24
  114.0 27.4 %copy-start.6 = (f32[2,64,2,64]{3,2,1,0:T(2,128)S(1)}, f32[2,64,2,64]{3,2,1,0:T(2,128)}, u32[]{:S(2)}) copy-start(f32[2,64,2,64]{3,2,1,0:T(2,128)} %copy-done.5) | copy-start | bytes 196612
  145.5 20.0 %copy-start.2 = (f32[2,16,64,128]{3,2,1,0:T(8,128)S(1)}, f32[2,16,64,128]{3,2,1,0:T(8,128)}, u32[]{:S(2)}) copy-start(f32[2,16,64,128]{3,2,1,0:T(8,128)} %param.7) | copy-start | bytes 3145732

commit v12 on v10

--- a/solution.py
+++ b/solution.py
@@ -17,36 +17,37 @@
     down = [(j, i) for i, j in up]
     north = lax.ppermute(x[:, :, rows - height:], "gx", up)
     south = lax.ppermute(x[:, :, :height], "gx", down)
-    tall = jnp.concatenate([x, south, north], 2)
+    band = jnp.concatenate([south, north], 2)
+    tall = jnp.concatenate([x, band], 2)
     right = [(i, i + 1) for i in range(lax.axis_size("gy") - 1)]
     left = [(j, i) for i, j in right]
     east = lax.ppermute(tall[..., :width], "gy", left)
     west = lax.ppermute(tall[..., cols - width:], "gy", right)
     middle = jnp.zeros((fields, levels, rows + 2 * height, 128 - 2 * width), x.dtype)
     edge = jnp.concatenate([east, middle, west], 3)
-    return tall, south, north, edge
+    return tall, band, edge
 
 
 def circular(x, height, width):
-    tall, _, _, edge = pieces(x, height, width)
+    tall, _, edge = pieces(x, height, width)
     return jnp.concatenate([tall, edge], 3)
 
 
-def plane(t_ref, s_ref, n_ref, e_ref, f):
-    tall = jnp.concatenate([t_ref[f, 0], s_ref[f, 0], n_ref[f, 0]], 0)
+def plane(t_ref, b_ref, e_ref, f):
+    tall = jnp.concatenate([t_ref[f, 0], b_ref[f, 0]], 0)
     return jnp.concatenate([tall, e_ref[f, 0]], 1)
 
 
-def diffusion_kernel(steps, rows, cols, x_ref, s_ref, n_ref, e_ref, ct_ref, cs_ref, cn_ref, ce_ref, o_ref):
+def diffusion_kernel(steps, rows, cols, x_ref, b_ref, e_ref, ct_ref, cb_ref, ce_ref, o_ref):
     height, span = e_ref.shape[2], 2 * e_ref.shape[3]
     fields = o_ref.shape[0]
-    along_i = plane(ct_ref, cs_ref, cn_ref, ce_ref, 0)
-    along_j = plane(ct_ref, cs_ref, cn_ref, ce_ref, 1)
-    sea = plane(ct_ref, cs_ref, cn_ref, ce_ref, 2)
+    along_i = plane(ct_ref, cb_ref, ce_ref, 0)
+    along_j = plane(ct_ref, cb_ref, ce_ref, 1)
+    sea = plane(ct_ref, cb_ref, ce_ref, 2)
     weight_i = along_i * sea * pltpu.roll(sea, height - 1, 0)
     weight_j = along_j * sea * pltpu.roll(sea, span - 1, 1)
     for f in range(fields):
-        values = plane(x_ref, s_ref, n_ref, e_ref, f)
+        values = plane(x_ref, b_ref, e_ref, f)
         for s in range(steps):
             flux_i = weight_i * (pltpu.roll(values, height - 1, 0) - values)
             flux_j = weight_j * (pltpu.roll(values, span - 1, 1) - values)
@@ -56,26 +57,25 @@
 
 def diffusion(values, coefs, steps):
     fields, levels, rows, cols = values.shape
-    height = rows + 4 * steps
+    height = rows + 2 * steps
     band = 2 * steps
 
     def specs(channels):
         return [
             pl.BlockSpec((channels, 1, rows, cols), lambda l: (0, l, 0, 0)),
             pl.BlockSpec((channels, 1, band, cols), lambda l: (0, l, 0, 0)),
-            pl.BlockSpec((channels, 1, band, cols), lambda l: (0, l, 0, 0)),
             pl.BlockSpec((channels, 1, height, 128), lambda l: (0, l, 0, 0)),
         ]
 
-    _, south, north, edge = pieces(values, band, steps)
-    _, coef_south, coef_north, coef_edge = coefs
+    _, halo, edge = pieces(values, steps, steps)
+    _, coef_halo, coef_edge = coefs
     return pl.pallas_call(
         functools.partial(diffusion_kernel, steps, rows, cols),
         out_shape=jax.ShapeDtypeStruct(values.shape, values.dtype),
         grid=(levels,),
         in_specs=specs(fields) + specs(coef_edge.shape[0]),
         out_specs=pl.BlockSpec((fields, 1, rows, cols), lambda l: (0, l, 0, 0)),
-    )(values, south, north, edge, coefs[0], coef_south, coef_north, coef_edge)
+    )(values, halo, edge, coefs[0], coef_halo, coef_edge)
 
 
 def lev_exchange(x, src_axis, dst_axis, half_axis, collective):
@@ -188,7 +188,7 @@
     forward = balance.reshape(2, level_count, 2, level_count)
     adjoint = jnp.transpose(forward, (2, 3, 0, 1))
     stacked = jnp.stack([diffusion_i, diffusion_j, ocean])
-    coefs = (stacked,) + pieces(stacked, 2 * steps, steps)[1:]
+    coefs = (stacked,) + pieces(stacked, steps, steps)[1:]
     columns = to_columns(scaled, False)
     mixed = jnp.einsum("abcd,cdij->abij", adjoint, columns, precision=lax.Precision.HIGHEST)
     coefs, mixed = lax.optimization_barrier((coefs, mixed))

time: 168 us -> 174 us (1.036)
  the two profiles are of different devices: /device:TPU:33 before, /device:TPU:1 now
where the time goes in v12:
time: 174 us; the launch traced here: 172 us
  Pallas kernels  89.5 us (51%)
  starting transfers between devices  28.8 us (17%)
  waiting for transfers between devices  17.4 us (10%)
  local copies, waits for them, and re-layouts  16.9 us (10%)
  other arithmetic  16 us (9%)
  matrix products  3.56 us (2%)
    pallas_call x3, Pallas kernels, lev_exchange(): pl.pallas_call(kernel, out_shape=jax.ShapeDtypeStruct(tuple(out_shape), x...  73.5 us
    pallas_call x1, Pallas kernels, diffusion(): pl.pallas_call(functools.partial(diffusion_kernel, steps, rows, cols), ou...  16 us
    ppermute x2, starting transfers between devices, pieces(): west = lax.ppermute(tall[..., cols - width:], 'gy', right)  9.21 us
    all_to_all x1, starting transfers between devices, to_columns(): return lax.all_to_all(x, 'lev', 2, 1, tiled=True)  9.14 us
    ppermute x2, waiting for transfers between devices, pieces(): north = lax.ppermute(x[:, :, rows - height:], 'gx', up)  8.56 us
    slice x4, local copies, waits for them, and re-layouts, pieces(): east = lax.ppermute(tall[..., :width], 'gy', left)  5.26 us
    ppermute x2, waiting for transfers between devices, pieces(): east = lax.ppermute(tall[..., :width], 'gy', left)  5.19 us
    ppermute x2, starting transfers between devices, pieces(): south = lax.ppermute(x[:, :, :height], 'gx', down)  5.01 us
  transfers between devices with their start and end apart: 9, of which 6 were waited for; matrix products, arithmetic and copies ran while one was open for 10% of the time, Pallas kernels for 0%

profile of v12, /device:TPU:1, one launch (start us, length us, event | category | flops | bytes accessed | tf_op | source)
XLA Modules:
  0.0 172.5 jit_solution(13066160718290478307)
XLA Ops:
  0.0 1.2 fusion.8
  1.3 0.1 copy-done.3
  1.4 1.5 multiply_multiply_fusion.1
  2.9 1.6 copy.18
  4.4 9.1 %all-to-all-start = ((f32[2,16,64,128]{3,1,0,2:T(8,128)}), f32[2,16,64,128]{3,1,0,2:T(8,128)}, u32[]{:S(2)}, u32[]{:S(2)}) async-start(f32[2,16,64,128]{3,1,0,2:T(8,128)} %copy.18), calls=%async_computation | async-start | bytes 2097152 | tf_op jit(solution)/shard_map/all_to_all | solution.py:166
  13.6 1.2 pad_maximum_fusion.2.ct_ref
  14.8 0.8 fusion.5
  15.6 4.9 %collective-permute-start = (f32[3,16,4,128]{3,2,1,0:T(4,128)}, f32[3,16,4,128]{3,2,1,0:T(4,128)S(1)}, u32[]{:S(2)}, u32[]{:S(2)}) collective-permute-start(f32[3,16,4,128]{3,2,1,0:T(4,128)} %get-tuple-element.15), channel_id=1, source_target_pairs={{4,0},{8,4},{12,8},{16,12},{20,16},{24,20},{28,24},{32,28},{36,32}... | collective-permute-start | bytes 294920 | tf_op jit(solution)/shard_map/ppermute | solution.py:19
  20.6 0.1 reshape.4
  20.7 0.1 copy.17
  20.9 1.6 collective-permute-done
  22.5 5.1 %collective-permute-done.1 = f32[3,16,4,128]{3,2,1,0:T(4,128)} collective-permute-done((f32[3,16,4,128]{3,2,1,0:T(4,128)}, f32[3,16,4,128]{3,2,1,0:T(4,128)}, u32[]{:S(2)}, u32[]{:S(2)}) %collective-permute-start.1) | collective-permute-done | bytes 98336 | tf_op jit(solution)/shard_map/ppermute | solution.py:18
  27.7 1.2 pad_maximum_fusion
  28.9 2.3 %fusion.4 = (f32[3,16,72,4]{3,2,1,0:T(8,128)}, f32[3,16,72,4]{3,2,1,0:T(8,128)}) fusion(f32[3,16,72,128]{3,2,1,0:T(8,128)S(1)} %pad_maximum_fusion), kind=kLoop, calls=%fused_computation.19 | loop fusion | bytes 221184 | tf_op jit(solution)/shard_map/slice | solution.py:24
  31.2 2.2 %copy.13 = f32[3,16,72,4]{2,1,3,0:T(8,128)S(1)} copy(f32[3,16,72,4]{3,2,1,0:T(8,128)} %get-tuple-element.13) | data formatting | bytes 110592 | tf_op jit(solution)/shard_map/slice | solution.py:24
  33.4 0.6 copy.14
  34.0 4.9 %collective-permute-start.3 = (f32[3,16,72,4]{2,1,3,0:T(8,128)S(1)}, f32[3,16,72,4]{2,1,3,0:T(8,128)S(1)}, u32[]{:S(2)}, u32[]{:S(2)}) collective-permute-start(f32[3,16,72,4]{2,1,3,0:T(8,128)S(1)} %copy.14), channel_id=1, source_target_pairs={{0,1},{1,2},{2,3},{4,5},{5,6},{6,7},{8,9},{9,10},{10,11},{12,13},{... | collective-permute-start | bytes 165896 | tf_op jit(solution)/shard_map/ppermute | solution.py:25
  38.9 1.9 %collective-permute-start.2 = (f32[3,16,72,4]{2,1,3,0:T(8,128)S(1)}, f32[3,16,72,4]{2,1,3,0:T(8,128)S(1)}, u32[]{:S(2)}, u32[]{:S(2)}) collective-permute-start(f32[3,16,72,4]{2,1,3,0:T(8,128)S(1)} %copy.13), channel_id=1, source_target_pairs={{1,0},{2,1},{3,2},{5,4},{6,5},{7,6},{9,8},{10,9},{11,10},{13,12},{... | collective-permute-start | bytes 165896 | tf_op jit(solution)/shard_map/ppermute | solution.py:24
  40.9 1.6 pad_maximum_fusion.5.cb_ref
  42.5 2.4 %collective-permute-done.2 = f32[3,16,72,4]{2,1,3,0:T(8,128)S(1)} collective-permute-done((f32[3,16,72,4]{2,1,3,0:T(8,128)S(1)}, f32[3,16,72,4]{2,1,3,0:T(8,128)S(1)}, u32[]{:S(2)}, u32[]{:S(2)}) %collective-permute-start.2) | collective-permute-done | bytes 55328 | tf_op jit(solution)/shard_map/ppermute | solution.py:24
  44.9 0.6 copy.15
  45.5 1.8 %copy.16 = f32[3,16,72,4]{3,2,1,0:T(8,128)} copy(f32[3,16,72,4]{2,1,3,0:T(8,128)S(1)} %collective-permute-done.3) | data formatting | bytes 110592 | tf_op jit(solution)/shard_map/ppermute | solution.py:25
  47.3 3.2 %pad_maximum_fusion.1.ce_ref = f32[3,16,72,128]{3,2,1,0:T(8,128)} fusion(f32[3,16,72,4]{3,2,1,0:T(8,128)} %copy.16, f32[3,16,72,4]{3,2,1,0:T(8,128)S(1)} %copy.15, f32[128]{0:T(128)S(1)} %pad.9.clone), kind=kLoop, calls=%fused_computation.1 | loop fusion | flops 884736 | bytes 1880576 | tf_op jit(solution)/shard_map/concatenate | solution.py:27
  50.5 1.4 copy.19
  51.9 1.1 convolution_bitcast_fusion.1
  53.0 1.6 copy.20.x_ref
  54.6 26.4 %shard_map.64 = f32[2,16,64,128]{3,2,1,0:T(8,128)} custom-call(f32[2,64,16,128]{3,2,1,0:T(8,128)} %copy.20.x_ref), custom_call_target="tpu_custom_call" | custom-call | tf_op jit(solution)/shard_map/pallas_call | solution.py:148
  81.0 1.3 broadcast_multiply_fusion.x_ref
  82.4 1.5 collective-permute-start.5
  83.9 2.1 %collective-permute-done.4 = f32[2,16,4,128]{3,2,1,0:T(4,128)S(1)} collective-permute-done((f32[2,16,4,128]{3,2,1,0:T(4,128)S(1)}, f32[2,16,4,128]{3,2,1,0:T(4,128)S(1)}, u32[]{:S(2)}, u32[]{:S(2)}) %collective-permute-start.4) | collective-permute-done | bytes 65568 | tf_op jit(solution)/shard_map/ppermute | solution.py:19
  86.0 3.4 %collective-permute-done.5 = f32[2,16,4,128]{3,2,1,0:T(4,128)S(1)} collective-permute-done((f32[2,16,4,128]{3,2,1,0:T(4,128)S(1)}, f32[2,16,4,128]{3,2,1,0:T(4,128)S(1)}, u32[]{:S(2)}, u32[]{:S(2)}) %collective-permute-start.5) | collective-permute-done | bytes 65568 | tf_op jit(solution)/shard_map/ppermute | solution.py:18
  89.4 0.1 pad_maximum_fusion.3
  89.5 0.4 fusion.6
  89.9 0.4 copy.21
  90.3 0.4 copy.22
  90.7 4.3 %collective-permute-start.7 = (f32[2,16,72,4]{2,1,3,0:T(8,128)S(1)}, f32[2,16,72,4]{2,1,3,0:T(8,128)S(1)}, u32[]{:S(2)}, u32[]{:S(2)}) collective-permute-start(f32[2,16,72,4]{2,1,3,0:T(8,128)S(1)} %copy.22), channel_id=1, source_target_pairs={{0,1},{1,2},{2,3},{4,5},{5,6},{6,7},{8,9},{9,10},{10,11},{12,13},{... | collective-permute-start | bytes 110600 | tf_op jit(solution)/shard_map/ppermute | solution.py:25
  95.0 2.1 %collective-permute-start.6 = (f32[2,16,72,4]{2,1,3,0:T(8,128)S(1)}, f32[2,16,72,4]{2,1,3,0:T(8,128)S(1)}, u32[]{:S(2)}, u32[]{:S(2)}) collective-permute-start(f32[2,16,72,4]{2,1,3,0:T(8,128)S(1)} %copy.21), channel_id=1, source_target_pairs={{1,0},{2,1},{3,2},{5,4},{6,5},{7,6},{9,8},{10,9},{11,10},{13,12},{... | collective-permute-start | bytes 110600 | tf_op jit(solution)/shard_map/ppermute | solution.py:24
  97.1 0.7 pad_maximum_fusion.6.b_ref
  97.8 2.8 %collective-permute-done.6 = f32[2,16,72,4]{2,1,3,0:T(8,128)S(1)} collective-permute-done((f32[2,16,72,4]{2,1,3,0:T(8,128)S(1)}, f32[2,16,72,4]{2,1,3,0:T(8,128)S(1)}, u32[]{:S(2)}, u32[]{:S(2)}) %collective-permute-start.6) | collective-permute-done | bytes 36896 | tf_op jit(solution)/shard_map/ppermute | solution.py:24
  100.6 0.4 copy.23
  101.1 0.4 copy.24
  101.5 1.4 pad_maximum_fusion.4.e_ref
  102.9 16.0 %shard_map.65.x_ref = f32[2,16,64,128]{3,2,1,0:T(8,128)} custom-call(f32[2,16,64,128]{3,2,1,0:T(8,128)} %copy-done, f32[2,16,8,128]{3,2,1,0:T(8,128)} %pad_maximum_fusion.6.b_ref, f32[2,16,72,128]{3,2,1,0:T(8,128)} %pad_maximum_fusion.4.e_ref, f32[3,16,64,128]{3,2,1,0:T(8,128)} %copy-done.1, f32[3,16,8,128]{3,2,1,0:T(8,128)} %pad_maximum_fusion.5.cb_ref, ...), custom_call_target="tpu_custom_call" | custom-call | tf_op jit(solution)/shard_map/pallas_call | solution.py:72
  118.9 25.6 %shard_map.66 = f32[2,64,16,128]{3,2,1,0:T(8,128)} custom-call(f32[2,16,64,128]{3,2,1,0:T(8,128)} %shard_map.65.x_ref), custom_call_target="tpu_custom_call" | custom-call | tf_op jit(solution)/shard_map/pallas_call | solution.py:148
  144.5 2.5 %convolution_bitcast_fusion = f32[2,64,16,128]{3,1,2,0:T(8,128)S(1)} fusion(f32[2,64,16,128]{3,2,1,0:T(8,128)} %shard_map.66, f32[2,64,2,64,1]{3,2,1,0,4:T(2,128)S(1)} %bitcast.33), kind=kOutput, calls=%fused_computation.3 | convolution fusion | flops 402653184 | bytes 2162688 | tf_op jit(solution)/shard_map/abcd,cdij->abij/dot_general | solution.py:177
  147.0 1.6 copy.27.x_ref
  148.6 21.4 %shard_map.67 = f32[2,16,64,128]{3,2,1,0:T(8,128)} custom-call(f32[2,64,16,128]{3,2,1,0:T(8,128)} %copy.27.x_ref), custom_call_target="tpu_custom_call" | custom-call | tf_op jit(solution)/shard_map/pallas_call | solution.py:148
  170.1 2.4 %multiply_multiply_fusion = f32[2,16,64,128]{3,2,1,0:T(8,128)} fusion(f32[2,16,64,128]{3,2,1,0:T(8,128)} %shard_map.67, f32[2,16,64,128]{3,2,1,0:T(8,128)S(1)} %copy-done.4, f32[16,64,128]{2,1,0:T(8,128)S(1)} %get-tuple-element.21), kind=kLoop, calls=%fused_computation.9 | loop fusion | flops 524288 | bytes 3670016 | tf_op jit(solution)/shard_map/mul | solution.py:198
  (22 shorter events, 0.2 us)
Async XLA Ops:
  0.0 1.4 copy-start.3
  4.4 9.1 %copy-start.5 = (f32[16,64,128]{2,1,0:T(8,128)S(1)}, f32[16,64,128]{2,1,0:T(8,128)}, u32[]{:S(2)}) copy-start(f32[16,64,128]{2,1,0:T(8,128)} %param.9) | copy-start | bytes 1572868
  4.4 46.1 %all-to-all-start = ((f32[2,16,64,128]{3,1,0,2:T(8,128)}), f32[2,16,64,128]{3,1,0,2:T(8,128)}, u32[]{:S(2)}, u32[]{:S(2)}) async-start(f32[2,16,64,128]{3,1,0,2:T(8,128)} %copy.18), calls=%async_computation | async-start | bytes 2097152 | tf_op jit(solution)/shard_map/all_to_all | solution.py:166
  13.6 7.0 %copy-start.6 = (f32[128,128]{1,0:T(8,128)S(1)}, f32[128,128]{1,0:T(8,128)}, u32[]{:S(2)}) copy-start(f32[128,128]{1,0:T(8,128)} %param.11) | copy-start | bytes 196612
  14.8 14.1 %copy-start.1 = (f32[3,16,64,128]{3,2,1,0:T(8,128)}, f32[3,16,64,128]{3,2,1,0:T(8,128)S(1)}, u32[]{:S(2)}) copy-start(f32[3,16,64,128]{3,2,1,0:T(8,128)S(1)} %pad_maximum_fusion.2.ct_ref) | copy-start | bytes 4718596
  15.6 6.9 %collective-permute-start = (f32[3,16,4,128]{3,2,1,0:T(4,128)}, f32[3,16,4,128]{3,2,1,0:T(4,128)S(1)}, u32[]{:S(2)}, u32[]{:S(2)}) collective-permute-start(f32[3,16,4,128]{3,2,1,0:T(4,128)} %get-tuple-element.15), channel_id=1, source_target_pairs={{4,0},{8,4},{12,8},{16,12},{20,16},{24,20},{28,24},{32,28},{36,32}... | collective-permute-start | bytes 294920 | tf_op jit(solution)/shard_map/ppermute | solution.py:19
  20.6 7.1 %collective-permute-start.1 = (f32[3,16,4,128]{3,2,1,0:T(4,128)}, f32[3,16,4,128]{3,2,1,0:T(4,128)}, u32[]{:S(2)}, u32[]{:S(2)}) collective-permute-start(f32[3,16,4,128]{3,2,1,0:T(4,128)} %get-tuple-element.16), channel_id=1, source_target_pairs={{0,4},{4,8},{8,12},{12,16},{16,20},{20,24},{24,28},{28,32},{32,36}... | collective-permute-start | bytes 294920 | tf_op jit(solution)/shard_map/ppermute | solution.py:18
  31.2 2.2 %copy-start.2 = (f32[3,16,72,4]{3,2,1,0:T(8,128)S(1)}, f32[3,16,72,4]{3,2,1,0:T(8,128)}, u32[]{:S(2)}) copy-start(f32[3,16,72,4]{3,2,1,0:T(8,128)} %get-tuple-element.14) | copy-start | bytes 165892
  34.0 11.5 %collective-permute-start.3 = (f32[3,16,72,4]{2,1,3,0:T(8,128)S(1)}, f32[3,16,72,4]{2,1,3,0:T(8,128)S(1)}, u32[]{:S(2)}, u32[]{:S(2)}) collective-permute-start(f32[3,16,72,4]{2,1,3,0:T(8,128)S(1)} %copy.14), channel_id=1, source_target_pairs={{0,1},{1,2},{2,3},{4,5},{5,6},{6,7},{8,9},{9,10},{10,11},{12,13},{... | collective-permute-start | bytes 165896 | tf_op jit(solution)/shard_map/ppermute | solution.py:25
  38.9 5.9 %collective-permute-start.2 = (f32[3,16,72,4]{2,1,3,0:T(8,128)S(1)}, f32[3,16,72,4]{2,1,3,0:T(8,128)S(1)}, u32[]{:S(2)}, u32[]{:S(2)}) collective-permute-start(f32[3,16,72,4]{2,1,3,0:T(8,128)S(1)} %copy.13), channel_id=1, source_target_pairs={{1,0},{2,1},{3,2},{5,4},{6,5},{7,6},{9,8},{10,9},{11,10},{13,12},{... | collective-permute-start | bytes 165896 | tf_op jit(solution)/shard_map/ppermute | solution.py:24
  82.3 7.6 %copy-start = (f32[2,16,64,128]{3,2,1,0:T(8,128)}, f32[2,16,64,128]{3,2,1,0:T(8,128)S(1)}, u32[]{:S(2)}) copy-start(f32[2,16,64,128]{3,2,1,0:T(8,128)S(1)} %broadcast_multiply_fusion.x_ref) | copy-start | bytes 3145732
  82.4 3.6 %collective-permute-start.4 = (f32[2,16,4,128]{3,2,1,0:T(4,128)S(1)}, f32[2,16,4,128]{3,2,1,0:T(4,128)S(1)}, u32[]{:S(2)}, u32[]{:S(2)}) collective-permute-start(f32[2,16,4,128]{3,2,1,0:T(4,128)S(1)} %get-tuple-element.19), channel_id=1, source_target_pairs={{4,0},{8,4},{12,8},{16,12},{20,16},{24,20},{28,24},{32,28},{36,32}... | collective-permute-start | bytes 196616 | tf_op jit(solution)/shard_map/ppermute | solution.py:19
  82.4 7.0 %collective-permute-start.5 = (f32[2,16,4,128]{3,2,1,0:T(4,128)S(1)}, f32[2,16,4,128]{3,2,1,0:T(4,128)S(1)}, u32[]{:S(2)}, u32[]{:S(2)}) collective-permute-start(f32[2,16,4,128]{3,2,1,0:T(4,128)S(1)} %get-tuple-element.20), channel_id=1, source_target_pairs={{0,4},{4,8},{8,12},{12,16},{16,20},{20,24},{24,28},{28,32},{32,36}... | collective-permute-start | bytes 196616 | tf_op jit(solution)/shard_map/ppermute | solution.py:18
  90.7 10.3 %collective-permute-start.7 = (f32[2,16,72,4]{2,1,3,0:T(8,128)S(1)}, f32[2,16,72,4]{2,1,3,0:T(8,128)S(1)}, u32[]{:S(2)}, u32[]{:S(2)}) collective-permute-start(f32[2,16,72,4]{2,1,3,0:T(8,128)S(1)} %copy.22), channel_id=1, source_target_pairs={{0,1},{1,2},{2,3},{4,5},{5,6},{6,7},{8,9},{9,10},{10,11},{12,13},{... | collective-permute-start | bytes 110600 | tf_op jit(solution)/shard_map/ppermute | solution.py:25
  95.0 5.6 %collective-permute-start.6 = (f32[2,16,72,4]{2,1,3,0:T(8,128)S(1)}, f32[2,16,72,4]{2,1,3,0:T(8,128)S(1)}, u32[]{:S(2)}, u32[]{:S(2)}) collective-permute-start(f32[2,16,72,4]{2,1,3,0:T(8,128)S(1)} %copy.21), channel_id=1, source_target_pairs={{1,0},{2,1},{3,2},{5,4},{6,5},{7,6},{9,8},{10,9},{11,10},{13,12},{... | collective-permute-start | bytes 110600 | tf_op jit(solution)/shard_map/ppermute | solution.py:24
  148.6 21.4 %copy-start.4 = (f32[2,16,64,128]{3,2,1,0:T(8,128)S(1)}, f32[2,16,64,128]{3,2,1,0:T(8,128)}, u32[]{:S(2)}) copy-start(f32[2,16,64,128]{3,2,1,0:T(8,128)} %param.7) | copy-start | bytes 3145732

commit v13 on v10

--- a/solution.py
+++ b/solution.py
@@ -22,31 +22,32 @@
     left = [(j, i) for i, j in right]
     east = lax.ppermute(tall[..., :width], "gy", left)
     west = lax.ppermute(tall[..., cols - width:], "gy", right)
-    middle = jnp.zeros((fields, levels, rows + 2 * height, 128 - 2 * width), x.dtype)
-    edge = jnp.concatenate([east, middle, west], 3)
-    return tall, south, north, edge
+    return tall, south, north, east, west
 
 
 def circular(x, height, width):
-    tall, _, _, edge = pieces(x, height, width)
-    return jnp.concatenate([tall, edge], 3)
-
-
-def plane(t_ref, s_ref, n_ref, e_ref, f):
+    tall, _, _, east, west = pieces(x, height, width)
+    middle = jnp.zeros(tall.shape[:3] + (128 - 2 * width,), x.dtype)
+    return jnp.concatenate([tall, east, middle, west], 3)
+
+
+def plane(t_ref, s_ref, n_ref, e_ref, w_ref, f):
     tall = jnp.concatenate([t_ref[f, 0], s_ref[f, 0], n_ref[f, 0]], 0)
-    return jnp.concatenate([tall, e_ref[f, 0]], 1)
-
-
-def diffusion_kernel(steps, rows, cols, x_ref, s_ref, n_ref, e_ref, ct_ref, cs_ref, cn_ref, ce_ref, o_ref):
-    height, span = e_ref.shape[2], 2 * e_ref.shape[3]
+    east, west = e_ref[f, 0], w_ref[f, 0]
+    middle = jnp.zeros((tall.shape[0], 128 - east.shape[1] - west.shape[1]), tall.dtype)
+    return jnp.concatenate([tall, east, middle, west], 1)
+
+
+def diffusion_kernel(steps, rows, cols, x_ref, s_ref, n_ref, e_ref, w_ref, ct_ref, cs_ref, cn_ref, ce_ref, cw_ref, o_ref):
+    height, span = e_ref.shape[2], 2 * x_ref.shape[3]
     fields = o_ref.shape[0]
-    along_i = plane(ct_ref, cs_ref, cn_ref, ce_ref, 0)
-    along_j = plane(ct_ref, cs_ref, cn_ref, ce_ref, 1)
-    sea = plane(ct_ref, cs_ref, cn_ref, ce_ref, 2)
+    along_i = plane(ct_ref, cs_ref, cn_ref, ce_ref, cw_ref, 0)
+    along_j = plane(ct_ref, cs_ref, cn_ref, ce_ref, cw_ref, 1)
+    sea = plane(ct_ref, cs_ref, cn_ref, ce_ref, cw_ref, 2)
     weight_i = along_i * sea * pltpu.roll(sea, height - 1, 0)
     weight_j = along_j * sea * pltpu.roll(sea, span - 1, 1)
     for f in range(fields):
-        values = plane(x_ref, s_ref, n_ref, e_ref, f)
+        values = plane(x_ref, s_ref, n_ref, e_ref, w_ref, f)
         for s in range(steps):
             flux_i = weight_i * (pltpu.roll(values, height - 1, 0) - values)
             flux_j = weight_j * (pltpu.roll(values, span - 1, 1) - values)
@@ -64,18 +65,19 @@
             pl.BlockSpec((channels, 1, rows, cols), lambda l: (0, l, 0, 0)),
             pl.BlockSpec((channels, 1, band, cols), lambda l: (0, l, 0, 0)),
             pl.BlockSpec((channels, 1, band, cols), lambda l: (0, l, 0, 0)),
-            pl.BlockSpec((channels, 1, height, 128), lambda l: (0, l, 0, 0)),
+            pl.BlockSpec((channels, 1, height, steps), lambda l: (0, l, 0, 0)),
+            pl.BlockSpec((channels, 1, height, steps), lambda l: (0, l, 0, 0)),
         ]
 
-    _, south, north, edge = pieces(values, band, steps)
-    _, coef_south, coef_north, coef_edge = coefs
+    _, south, north, east, west = pieces(values, band, steps)
+    _, coef_south, coef_north, coef_east, coef_west = coefs
     return pl.pallas_call(
         functools.partial(diffusion_kernel, steps, rows, cols),
         out_shape=jax.ShapeDtypeStruct(values.shape, values.dtype),
         grid=(levels,),
-        in_specs=specs(fields) + specs(coef_edge.shape[0]),
+        in_specs=specs(fields) + specs(coef_east.shape[0]),
         out_specs=pl.BlockSpec((fields, 1, rows, cols), lambda l: (0, l, 0, 0)),
-    )(values, south, north, edge, coefs[0], coef_south, coef_north, coef_edge)
+    )(values, south, north, east, west, coefs[0], coef_south, coef_north, coef_east, coef_west)
 
 
 def lev_exchange(x, src_axis, dst_axis, half_axis, collective):

time: 168 us -> 168 us (level)
  the two profiles are of different devices: /device:TPU:33 before, /device:TPU:76 now
where the time goes in v13:
time: 168 us; the launch traced here: 167 us
  Pallas kernels  97.8 us (58%)
  local copies, waits for them, and re-layouts  21.8 us (13%)
  starting transfers between devices  19.5 us (12%)
  waiting for transfers between devices  15.3 us (9%)
  other arithmetic  9.07 us (5%)
  matrix products  3.56 us (2%)
    pallas_call x3, Pallas kernels, lev_exchange(): pl.pallas_call(kernel, out_shape=jax.ShapeDtypeStruct(tuple(out_shape), x...  79.6 us
    pallas_call x1, Pallas kernels, diffusion(): pl.pallas_call(functools.partial(diffusion_kernel, steps, rows, cols), ou...  18.2 us
    all_to_all x1, starting transfers between devices, to_columns(): return lax.all_to_all(x, 'lev', 2, 1, tiled=True)  8.24 us
    ppermute x2, waiting for transfers between devices, pieces(): north = lax.ppermute(x[:, :, rows - height:], 'gx', up)  6.3 us
    all_to_all x1, waiting for transfers between devices, to_columns(): return lax.all_to_all(x, 'lev', 2, 1, tiled=True)  5.96 us
    slice x4, local copies, waits for them, and re-layouts, pieces(): west = lax.ppermute(tall[..., cols - width:], 'gy', right)  5.63 us
    optimization_barrier x3, local copies, waits for them, and re-layouts, shards(): coefs, mixed = lax.optimization_barrier((coefs, mixed))  5.43 us
    ppermute x2, starting transfers between devices, pieces(): west = lax.ppermute(tall[..., cols - width:], 'gy', right)  4.34 us
  transfers between devices with their start and end apart: 9, of which 5 were waited for; matrix products, arithmetic and copies ran while one was open for 11% of the time, Pallas kernels for 0%

profile of v13, /device:TPU:76, one launch (start us, length us, event | category | flops | bytes accessed | tf_op | source)
XLA Modules:
  0.0 167.3 jit_solution(4015126530805597860)
XLA Ops:
  0.0 1.2 fusion.8
  1.3 0.1 copy-done.3
  1.4 1.5 multiply_multiply_fusion.1
  2.9 1.6 copy.16
  4.4 8.2 %all-to-all-start = ((f32[2,16,64,128]{3,1,0,2:T(8,128)}), f32[2,16,64,128]{3,1,0,2:T(8,128)}, u32[]{:S(2)}, u32[]{:S(2)}) async-start(f32[2,16,64,128]{3,1,0,2:T(8,128)} %copy.16), calls=%async_computation | async-start | bytes 2097152 | tf_op jit(solution)/shard_map/all_to_all | solution.py:168
  12.7 1.2 pad_maximum_fusion.1.ct_ref
  13.9 0.9 fusion.5
  14.8 1.6 collective-permute-start.1
  16.4 0.4 collective-permute-start
  16.8 0.1 reshape.4
  17.0 0.8 copy.15
  17.7 3.4 %collective-permute-done.1.cn_ref = f32[3,16,8,128]{3,2,1,0:T(8,128)S(1)} collective-permute-done((f32[3,16,8,128]{3,2,1,0:T(8,128)}, f32[3,16,8,128]{3,2,1,0:T(8,128)S(1)}, u32[]{:S(2)}, u32[]{:S(2)}) %collective-permute-start.1) | collective-permute-done | bytes 196640 | tf_op jit(solution)/shard_map/ppermute | solution.py:18
  21.1 1.4 collective-permute-done.cs_ref
  22.5 1.3 pad_maximum_fusion
  23.8 2.5 %fusion.4 = (f32[3,16,80,4]{3,2,1,0:T(8,128)}, f32[3,16,80,4]{3,2,1,0:T(8,128)}) fusion(f32[3,16,80,128]{3,2,1,0:T(8,128)S(1)} %pad_maximum_fusion), kind=kLoop, calls=%fused_computation.15 | loop fusion | bytes 245760 | tf_op jit(solution)/shard_map/slice | solution.py:24
  26.3 2.3 %copy.14 = f32[3,16,80,4]{2,1,3,0:T(8,128)S(1)} copy(f32[3,16,80,4]{3,2,1,0:T(8,128)} %get-tuple-element.17) | data formatting | bytes 122880 | tf_op jit(solution)/shard_map/slice | solution.py:24
  28.6 0.0 copy-start.9
  28.6 0.6 copy.13
  29.2 1.3 collective-permute-start.2
  30.5 3.0 %collective-permute-start.3 = (f32[3,16,80,4]{2,1,3,0:T(8,128)S(1)}, f32[3,16,80,4]{2,1,3,0:T(8,128)S(1)}, u32[]{:S(2)}, u32[]{:S(2)}) collective-permute-start(f32[3,16,80,4]{2,1,3,0:T(8,128)S(1)} %copy.14), channel_id=1, source_target_pairs={{0,1},{1,2},{2,3},{4,5},{5,6},{6,7},{8,9},{9,10},{10,11},{12,13},{... | collective-permute-start | bytes 184328 | tf_op jit(solution)/shard_map/ppermute | solution.py:24
  33.6 6.0 %all-to-all-done = f32[2,16,64,128]{3,1,0,2:T(8,128)} async-done(((f32[2,16,64,128]{3,1,0,2:T(8,128)}), f32[2,16,64,128]{3,1,0,2:T(8,128)}, u32[]{:S(2)}, u32[]{:S(2)}) %all-to-all-start) | async-done | bytes 1048608 | tf_op jit(solution)/shard_map/all_to_all | solution.py:168
  39.5 1.4 copy.17
  40.9 1.1 convolution_bitcast_fusion.1
  42.0 1.6 copy.18.x_ref
  43.6 24.0 %shard_map.64 = f32[2,16,64,128]{3,2,1,0:T(8,128)} custom-call(f32[2,64,16,128]{3,2,1,0:T(8,128)} %copy.18.x_ref), custom_call_target="tpu_custom_call" | custom-call | tf_op jit(solution)/shard_map/pallas_call | solution.py:150
  67.6 1.3 broadcast_multiply_fusion.x_ref
  68.9 0.0 copy-start
  69.0 1.7 %collective-permute-start.5 = (f32[2,16,8,128]{3,2,1,0:T(8,128)S(1)}, f32[2,16,8,128]{3,2,1,0:T(8,128)S(1)}, u32[]{:S(2)}, u32[]{:S(2)}) collective-permute-start(f32[2,16,8,128]{3,2,1,0:T(8,128)S(1)} %get-tuple-element.23), channel_id=1, source_target_pairs={{0,4},{4,8},{8,12},{12,16},{16,20},{20,24},{24,28},{28,32},{32,36}... | collective-permute-start | bytes 393224 | tf_op jit(solution)/shard_map/ppermute | solution.py:18
  70.7 0.4 collective-permute-start.4
  71.1 2.9 %collective-permute-done.5.n_ref = f32[2,16,8,128]{3,2,1,0:T(8,128)S(1)} collective-permute-done((f32[2,16,8,128]{3,2,1,0:T(8,128)S(1)}, f32[2,16,8,128]{3,2,1,0:T(8,128)S(1)}, u32[]{:S(2)}, u32[]{:S(2)}) %collective-permute-start.5) | collective-permute-done | bytes 131104 | tf_op jit(solution)/shard_map/ppermute | solution.py:18
  74.0 1.6 collective-permute-done.4.s_ref
  75.6 0.1 pad_maximum_fusion.2
  75.8 0.4 fusion.6
  76.2 0.1 copy-done.8
  76.3 0.4 copy.20
  76.7 1.3 collective-permute-start.7
  78.0 0.4 copy.19
  78.4 1.5 collective-permute-start.6
  79.9 1.9 %copy.23.ce_ref = f32[3,16,80,4]{3,2,1,0:T(8,128)} copy(f32[3,16,80,4]{2,1,3,0:T(8,128)S(1)} %copy-done.11) | data formatting | bytes 122880 | tf_op jit(solution)/shard_map/optimization_barrier | solution.py:196
  81.9 1.9 %copy.24.cw_ref = f32[3,16,80,4]{3,2,1,0:T(8,128)} copy(f32[3,16,80,4]{2,1,3,0:T(8,128)S(1)} %copy-done.13) | data formatting | bytes 122880 | tf_op jit(solution)/shard_map/optimization_barrier | solution.py:196
  83.8 1.6 copy.22.w_ref
  85.4 1.6 copy.21.e_ref
  86.9 18.2 %shard_map.65.x_ref = f32[2,16,64,128]{3,2,1,0:T(8,128)} custom-call(f32[2,16,64,128]{3,2,1,0:T(8,128)} %copy-done, f32[2,16,8,128]{3,2,1,0:T(8,128)} %copy-done.8, f32[2,16,8,128]{3,2,1,0:T(8,128)} %copy-done.7, f32[2,16,80,4]{3,2,1,0:T(8,128)} %copy.21.e_ref, f32[2,16,80,4]{3,2,1,0:T(8,128)} %copy.22.w_ref, f32[3,16,64,128]{3,2,1,0:T(8,128)} %copy-done.1, ...), custom_call_target="tpu_custom_call" | custom-call | tf_op jit(solution)/shard_map/pallas_call | solution.py:74
  105.1 28.1 %shard_map.66 = f32[2,64,16,128]{3,2,1,0:T(8,128)} custom-call(f32[2,16,64,128]{3,2,1,0:T(8,128)} %shard_map.65.x_ref), custom_call_target="tpu_custom_call" | custom-call | tf_op jit(solution)/shard_map/pallas_call | solution.py:150
  133.2 2.5 %convolution_bitcast_fusion = f32[2,64,16,128]{3,1,2,0:T(8,128)S(1)} fusion(f32[2,64,16,128]{3,2,1,0:T(8,128)} %shard_map.66, f32[2,64,2,64,1]{3,2,1,0,4:T(2,128)S(1)} %bitcast.33), kind=kOutput, calls=%fused_computation.2 | convolution fusion | flops 402653184 | bytes 2162688 | tf_op jit(solution)/shard_map/abcd,cdij->abij/dot_general | solution.py:179
  135.7 1.6 copy.27.x_ref
  137.3 27.6 %shard_map.67 = f32[2,16,64,128]{3,2,1,0:T(8,128)} custom-call(f32[2,64,16,128]{3,2,1,0:T(8,128)} %copy.27.x_ref), custom_call_target="tpu_custom_call" | custom-call | tf_op jit(solution)/shard_map/pallas_call | solution.py:150
  164.9 2.4 %multiply_multiply_fusion = f32[2,16,64,128]{3,2,1,0:T(8,128)} fusion(f32[2,16,64,128]{3,2,1,0:T(8,128)} %shard_map.67, f32[2,16,64,128]{3,2,1,0:T(8,128)S(1)} %copy-done.4, f32[16,64,128]{2,1,0:T(8,128)S(1)} %get-tuple-element.25), kind=kLoop, calls=%fused_computation.7 | loop fusion | flops 524288 | bytes 3670016 | tf_op jit(solution)/shard_map/mul | solution.py:200
  (32 shorter events, 0.1 us)
Async XLA Ops:
  0.0 1.4 copy-start.3
  4.4 8.2 %copy-start.5 = (f32[16,64,128]{2,1,0:T(8,128)S(1)}, f32[16,64,128]{2,1,0:T(8,128)}, u32[]{:S(2)}) copy-start(f32[16,64,128]{2,1,0:T(8,128)} %param.9) | copy-start | bytes 1572868
  4.4 35.1 %all-to-all-start = ((f32[2,16,64,128]{3,1,0,2:T(8,128)}), f32[2,16,64,128]{3,1,0,2:T(8,128)}, u32[]{:S(2)}, u32[]{:S(2)}) async-start(f32[2,16,64,128]{3,1,0,2:T(8,128)} %copy.16), calls=%async_computation | async-start | bytes 2097152 | tf_op jit(solution)/shard_map/all_to_all | solution.py:168
  12.7 4.1 %copy-start.14 = (f32[128,128]{1,0:T(8,128)S(1)}, f32[128,128]{1,0:T(8,128)}, u32[]{:S(2)}) copy-start(f32[128,128]{1,0:T(8,128)} %param.11) | copy-start | bytes 196612
  13.9 9.9 %copy-start.1 = (f32[3,16,64,128]{3,2,1,0:T(8,128)}, f32[3,16,64,128]{3,2,1,0:T(8,128)S(1)}, u32[]{:S(2)}) copy-start(f32[3,16,64,128]{3,2,1,0:T(8,128)S(1)} %pad_maximum_fusion.1.ct_ref) | copy-start | bytes 4718596
  14.8 6.3 %collective-permute-start.1 = (f32[3,16,8,128]{3,2,1,0:T(8,128)}, f32[3,16,8,128]{3,2,1,0:T(8,128)S(1)}, u32[]{:S(2)}, u32[]{:S(2)}) collective-permute-start(f32[3,16,8,128]{3,2,1,0:T(8,128)} %get-tuple-element.19), channel_id=1, source_target_pairs={{0,4},{4,8},{8,12},{12,16},{16,20},{20,24},{24,28},{28,32},{32,36}... | collective-permute-start | bytes 589832 | tf_op jit(solution)/shard_map/ppermute | solution.py:18
  16.4 6.1 %collective-permute-start = (f32[3,16,8,128]{3,2,1,0:T(8,128)}, f32[3,16,8,128]{3,2,1,0:T(8,128)}, u32[]{:S(2)}, u32[]{:S(2)}) collective-permute-start(f32[3,16,8,128]{3,2,1,0:T(8,128)} %get-tuple-element.20), channel_id=1, source_target_pairs={{4,0},{8,4},{12,8},{16,12},{20,16},{24,20},{28,24},{32,28},{36,32}... | collective-permute-start | bytes 589832 | tf_op jit(solution)/shard_map/ppermute | solution.py:19
  21.1 2.7 %copy-start.6 = (f32[3,16,8,128]{3,2,1,0:T(8,128)}, f32[3,16,8,128]{3,2,1,0:T(8,128)S(1)}, u32[]{:S(2)}) copy-start(f32[3,16,8,128]{3,2,1,0:T(8,128)S(1)} %collective-permute-done.1.cn_ref) | copy-start | bytes 589828
  26.3 2.3 %copy-start.2 = (f32[3,16,80,4]{3,2,1,0:T(8,128)S(1)}, f32[3,16,80,4]{3,2,1,0:T(8,128)}, u32[]{:S(2)}) copy-start(f32[3,16,80,4]{3,2,1,0:T(8,128)} %get-tuple-element.18) | copy-start | bytes 184324
  28.6 12.3 %copy-start.9 = (f32[2,64,2,64]{1,3,0,2:T(8,128)S(1)}, f32[2,64,2,64]{1,3,0,2:T(8,128)}, u32[]{:S(2)}) copy-start(f32[2,64,2,64]{1,3,0,2:T(8,128)} %copy.15) | copy-start | bytes 196612
  29.2 12.8 %collective-permute-start.2 = (f32[3,16,80,4]{2,1,3,0:T(8,128)S(1)}, f32[3,16,80,4]{2,1,3,0:T(8,128)S(1)}, u32[]{:S(2)}, u32[]{:S(2)}) collective-permute-start(f32[3,16,80,4]{2,1,3,0:T(8,128)S(1)} %copy.13), channel_id=1, source_target_pairs={{1,0},{2,1},{3,2},{5,4},{6,5},{7,6},{9,8},{10,9},{11,10},{13,12},{... | collective-permute-start | bytes 184328 | tf_op jit(solution)/shard_map/ppermute | solution.py:23
  30.5 11.5 %collective-permute-start.3 = (f32[3,16,80,4]{2,1,3,0:T(8,128)S(1)}, f32[3,16,80,4]{2,1,3,0:T(8,128)S(1)}, u32[]{:S(2)}, u32[]{:S(2)}) collective-permute-start(f32[3,16,80,4]{2,1,3,0:T(8,128)S(1)} %copy.14), channel_id=1, source_target_pairs={{0,1},{1,2},{2,3},{4,5},{5,6},{6,7},{8,9},{9,10},{10,11},{12,13},{... | collective-permute-start | bytes 184328 | tf_op jit(solution)/shard_map/ppermute | solution.py:24
  42.0 25.6 %copy-start.10 = (f32[3,16,80,4]{2,1,3,0:T(8,128)}, f32[3,16,80,4]{2,1,3,0:T(8,128)S(1)}, u32[]{:S(2)}) copy-start(f32[3,16,80,4]{2,1,3,0:T(8,128)S(1)} %collective-permute-done.2) | copy-start | bytes 184324
  42.0 25.6 %copy-start.12 = (f32[3,16,80,4]{2,1,3,0:T(8,128)}, f32[3,16,80,4]{2,1,3,0:T(8,128)S(1)}, u32[]{:S(2)}) copy-start(f32[3,16,80,4]{2,1,3,0:T(8,128)S(1)} %collective-permute-done.3) | copy-start | bytes 184324
  68.9 6.8 %copy-start = (f32[2,16,64,128]{3,2,1,0:T(8,128)}, f32[2,16,64,128]{3,2,1,0:T(8,128)S(1)}, u32[]{:S(2)}) copy-start(f32[2,16,64,128]{3,2,1,0:T(8,128)S(1)} %broadcast_multiply_fusion.x_ref) | copy-start | bytes 3145732
  69.0 5.0 %collective-permute-start.5 = (f32[2,16,8,128]{3,2,1,0:T(8,128)S(1)}, f32[2,16,8,128]{3,2,1,0:T(8,128)S(1)}, u32[]{:S(2)}, u32[]{:S(2)}) collective-permute-start(f32[2,16,8,128]{3,2,1,0:T(8,128)S(1)} %get-tuple-element.23), channel_id=1, source_target_pairs={{0,4},{4,8},{8,12},{12,16},{16,20},{20,24},{24,28},{28,32},{32,36}... | collective-permute-start | bytes 393224 | tf_op jit(solution)/shard_map/ppermute | solution.py:18
  70.7 5.0 %collective-permute-start.4 = (f32[2,16,8,128]{3,2,1,0:T(8,128)S(1)}, f32[2,16,8,128]{3,2,1,0:T(8,128)S(1)}, u32[]{:S(2)}, u32[]{:S(2)}) collective-permute-start(f32[2,16,8,128]{3,2,1,0:T(8,128)S(1)} %get-tuple-element.24), channel_id=1, source_target_pairs={{4,0},{8,4},{12,8},{16,12},{20,16},{24,20},{28,24},{32,28},{36,32}... | collective-permute-start | bytes 393224 | tf_op jit(solution)/shard_map/ppermute | solution.py:19
  74.0 2.2 %copy-start.7 = (f32[2,16,8,128]{3,2,1,0:T(8,128)}, f32[2,16,8,128]{3,2,1,0:T(8,128)S(1)}, u32[]{:S(2)}) copy-start(f32[2,16,8,128]{3,2,1,0:T(8,128)S(1)} %collective-permute-done.5.n_ref) | copy-start | bytes 393220
  75.6 0.6 copy-start.8
  76.3 3.7 %copy-start.11 = (f32[3,16,80,4]{2,1,3,0:T(8,128)S(1)}, f32[3,16,80,4]{2,1,3,0:T(8,128)}, u32[]{:S(2)}) copy-start(f32[3,16,80,4]{2,1,3,0:T(8,128)} %copy-done.10) | copy-start | bytes 184324
  76.7 7.1 %collective-permute-start.7 = (f32[2,16,80,4]{2,1,3,0:T(8,128)S(1)}, f32[2,16,80,4]{2,1,3,0:T(8,128)S(1)}, u32[]{:S(2)}, u32[]{:S(2)}) collective-permute-start(f32[2,16,80,4]{2,1,3,0:T(8,128)S(1)} %copy.20), channel_id=1, source_target_pairs={{0,1},{1,2},{2,3},{4,5},{5,6},{6,7},{8,9},{9,10},{10,11},{12,13},{... | collective-permute-start | bytes 122888 | tf_op jit(solution)/shard_map/ppermute | solution.py:24
  78.0 3.9 %copy-start.13 = (f32[3,16,80,4]{2,1,3,0:T(8,128)S(1)}, f32[3,16,80,4]{2,1,3,0:T(8,128)}, u32[]{:S(2)}) copy-start(f32[3,16,80,4]{2,1,3,0:T(8,128)} %copy-done.12) | copy-start | bytes 184324
  78.4 6.9 %collective-permute-start.6 = (f32[2,16,80,4]{2,1,3,0:T(8,128)S(1)}, f32[2,16,80,4]{2,1,3,0:T(8,128)S(1)}, u32[]{:S(2)}, u32[]{:S(2)}) collective-permute-start(f32[2,16,80,4]{2,1,3,0:T(8,128)S(1)} %copy.19), channel_id=1, source_target_pairs={{1,0},{2,1},{3,2},{5,4},{6,5},{7,6},{9,8},{10,9},{11,10},{13,12},{... | collective-permute-start | bytes 122888 | tf_op jit(solution)/shard_map/ppermute | solution.py:23
  137.3 27.6 %copy-start.4 = (f32[2,16,64,128]{3,2,1,0:T(8,128)S(1)}, f32[2,16,64,128]{3,2,1,0:T(8,128)}, u32[]{:S(2)}) copy-start(f32[2,16,64,128]{3,2,1,0:T(8,128)} %param.7) | copy-start | bytes 3145732

commit v14 on v10

--- a/solution.py
+++ b/solution.py
@@ -42,9 +42,9 @@
     fields = o_ref.shape[0]
     along_i = plane(ct_ref, cs_ref, cn_ref, ce_ref, 0)
     along_j = plane(ct_ref, cs_ref, cn_ref, ce_ref, 1)
-    sea = plane(ct_ref, cs_ref, cn_ref, ce_ref, 2)
-    weight_i = along_i * sea * pltpu.roll(sea, height - 1, 0)
-    weight_j = along_j * sea * pltpu.roll(sea, span - 1, 1)
+    sea = (along_i > 0).astype(along_i.dtype)
+    weight_i = along_i * pltpu.roll(sea, height - 1, 0)
+    weight_j = along_j * pltpu.roll(sea, span - 1, 1)
     for f in range(fields):
         values = plane(x_ref, s_ref, n_ref, e_ref, f)
         for s in range(steps):
@@ -187,7 +187,7 @@
     balance = jnp.eye(order_count, dtype=jnp.float32) + coupling
     forward = balance.reshape(2, level_count, 2, level_count)
     adjoint = jnp.transpose(forward, (2, 3, 0, 1))
-    stacked = jnp.stack([diffusion_i, diffusion_j, ocean])
+    stacked = jnp.stack([diffusion_i * ocean, diffusion_j * ocean])
     coefs = (stacked,) + pieces(stacked, 2 * steps, steps)[1:]
     columns = to_columns(scaled, False)
     mixed = jnp.einsum("abcd,cdij->abij", adjoint, columns, precision=lax.Precision.HIGHEST)

time: 168 us -> 162 us (0.964)
  the two profiles are of different devices: /device:TPU:33 before, /device:TPU:1 now
where the time goes in v14:
time: 162 us; the launch traced here: 161 us
  Pallas kernels  88.1 us (54%)
  starting transfers between devices  31.3 us (19%)
  local copies, waits for them, and re-layouts  14 us (9%)
  waiting for transfers between devices  12.8 us (8%)
  other arithmetic  10.8 us (7%)
  matrix products  3.56 us (2%)
    pallas_call x3, Pallas kernels, lev_exchange(): pl.pallas_call(kernel, out_shape=jax.ShapeDtypeStruct(tuple(out_shape), x...  71.8 us
    pallas_call x1, Pallas kernels, diffusion(): pl.pallas_call(functools.partial(diffusion_kernel, steps, rows, cols), ou...  16.3 us
    all_to_all x1, starting transfers between devices, to_columns(): return lax.all_to_all(x, 'lev', 2, 1, tiled=True)  9.14 us
    ppermute x2, starting transfers between devices, pieces(): south = lax.ppermute(x[:, :, :height], 'gx', down)  7.45 us
    ppermute x2, starting transfers between devices, pieces(): west = lax.ppermute(tall[..., cols - width:], 'gy', right)  7.04 us
    ppermute x2, waiting for transfers between devices, pieces(): east = lax.ppermute(tall[..., :width], 'gy', left)  6.2 us
    ppermute x2, waiting for transfers between devices, pieces(): north = lax.ppermute(x[:, :, rows - height:], 'gx', up)  5.93 us
    ppermute x2, starting transfers between devices, pieces(): east = lax.ppermute(tall[..., :width], 'gy', left)  4.91 us
  transfers between devices with their start and end apart: 9, of which 4 were waited for; matrix products, arithmetic and copies ran while one was open for 5% of the time, Pallas kernels for 0%

profile of v14, /device:TPU:1, one launch (start us, length us, event | category | flops | bytes accessed | tf_op | source)
XLA Modules:
  0.0 160.8 jit_solution(199505163597190775)
XLA Ops:
  0.0 1.2 convert_element_type.6
  1.2 0.2 copy-done.1
  1.4 1.5 multiply_multiply_fusion.1
  2.9 1.6 copy.18
  4.4 9.1 %all-to-all-start = ((f32[2,16,64,128]{3,1,0,2:T(8,128)}), f32[2,16,64,128]{3,1,0,2:T(8,128)}, u32[]{:S(2)}, u32[]{:S(2)}) async-start(f32[2,16,64,128]{3,1,0,2:T(8,128)} %copy.18), calls=%async_computation | async-start | bytes 2097152 | tf_op jit(solution)/shard_map/all_to_all | solution.py:166
  13.6 0.2 multiply_bitcast_fusion.1
  13.8 1.4 collective-permute-start.1
  15.2 3.7 %collective-permute-start = (f32[2,16,8,128]{3,2,1,0:T(8,128)S(1)}, f32[2,16,8,128]{3,2,1,0:T(8,128)S(1)}, u32[]{:S(2)}, u32[]{:S(2)}) collective-permute-start(f32[2,16,8,128]{3,2,1,0:T(8,128)S(1)} %get-tuple-element.22), channel_id=1, source_target_pairs={{4,0},{8,4},{12,8},{16,12},{20,16},{24,20},{28,24},{32,28},{36,32}... | collective-permute-start | bytes 393224 | tf_op jit(solution)/shard_map/ppermute | solution.py:19
  18.9 2.6 %collective-permute-done.1.cn_ref = f32[2,16,8,128]{3,2,1,0:T(8,128)S(1)} collective-permute-done((f32[2,16,8,128]{3,2,1,0:T(8,128)S(1)}, f32[2,16,8,128]{3,2,1,0:T(8,128)S(1)}, u32[]{:S(2)}, u32[]{:S(2)}) %collective-permute-start.1) | collective-permute-done | bytes 131104 | tf_op jit(solution)/shard_map/ppermute | solution.py:18
  21.6 0.1 pad_maximum_fusion.1
  21.7 1.5 fusion.7
  23.2 1.7 %copy.13 = f32[2,16,80,4]{2,1,3,0:T(8,128)S(1)} copy(f32[2,16,80,4]{3,2,1,0:T(8,128)} %get-tuple-element.17) | data formatting | bytes 81920 | tf_op jit(solution)/shard_map/slice | solution.py:23
  24.9 0.4 copy.14
  25.3 4.2 %collective-permute-start.3 = (f32[2,16,80,4]{2,1,3,0:T(8,128)S(1)}, f32[2,16,80,4]{2,1,3,0:T(8,128)S(1)}, u32[]{:S(2)}, u32[]{:S(2)}) collective-permute-start(f32[2,16,80,4]{2,1,3,0:T(8,128)S(1)} %copy.14), channel_id=1, source_target_pairs={{0,1},{1,2},{2,3},{4,5},{5,6},{6,7},{8,9},{9,10},{10,11},{12,13},{... | collective-permute-start | bytes 122888 | tf_op jit(solution)/shard_map/ppermute | solution.py:24
  29.6 1.9 %collective-permute-start.2 = (f32[2,16,80,4]{2,1,3,0:T(8,128)S(1)}, f32[2,16,80,4]{2,1,3,0:T(8,128)S(1)}, u32[]{:S(2)}, u32[]{:S(2)}) collective-permute-start(f32[2,16,80,4]{2,1,3,0:T(8,128)S(1)} %copy.13), channel_id=1, source_target_pairs={{1,0},{2,1},{3,2},{5,4},{6,5},{7,6},{9,8},{10,9},{11,10},{13,12},{... | collective-permute-start | bytes 122888 | tf_op jit(solution)/shard_map/ppermute | solution.py:23
  31.5 1.1 pad_maximum_fusion.ct_ref
  32.6 0.1 reshape.4
  32.7 0.1 copy.17
  32.8 0.1 pad.7.clone
  32.9 6.2 %collective-permute-done.2 = f32[2,16,80,4]{2,1,3,0:T(8,128)S(1)} collective-permute-done((f32[2,16,80,4]{2,1,3,0:T(8,128)S(1)}, f32[2,16,80,4]{2,1,3,0:T(8,128)S(1)}, u32[]{:S(2)}, u32[]{:S(2)}) %collective-permute-start.2) | collective-permute-done | bytes 40992 | tf_op jit(solution)/shard_map/ppermute | solution.py:23
  39.1 0.5 copy.15
  39.6 0.5 copy.16
  40.0 1.5 pad_maximum_fusion.2.ce_ref
  41.5 1.4 copy.19
  42.9 1.1 convolution_bitcast_fusion.1
  43.9 1.6 copy.20.x_ref
  45.5 24.7 %shard_map.64 = f32[2,16,64,128]{3,2,1,0:T(8,128)} custom-call(f32[2,64,16,128]{3,2,1,0:T(8,128)} %copy.20.x_ref), custom_call_target="tpu_custom_call" | custom-call | tf_op jit(solution)/shard_map/pallas_call | solution.py:148
  70.2 1.3 broadcast_multiply_fusion.x_ref
  71.6 1.4 collective-permute-start.5
  72.9 3.7 %collective-permute-start.4 = (f32[2,16,8,128]{3,2,1,0:T(8,128)S(1)}, f32[2,16,8,128]{3,2,1,0:T(8,128)S(1)}, u32[]{:S(2)}, u32[]{:S(2)}) collective-permute-start(f32[2,16,8,128]{3,2,1,0:T(8,128)S(1)} %get-tuple-element.20), channel_id=1, source_target_pairs={{4,0},{8,4},{12,8},{16,12},{20,16},{24,20},{28,24},{32,28},{36,32}... | collective-permute-start | bytes 393224 | tf_op jit(solution)/shard_map/ppermute | solution.py:19
  76.7 3.3 %collective-permute-done.5.n_ref = f32[2,16,8,128]{3,2,1,0:T(8,128)S(1)} collective-permute-done((f32[2,16,8,128]{3,2,1,0:T(8,128)S(1)}, f32[2,16,8,128]{3,2,1,0:T(8,128)S(1)}, u32[]{:S(2)}, u32[]{:S(2)}) %collective-permute-start.5) | collective-permute-done | bytes 131104 | tf_op jit(solution)/shard_map/ppermute | solution.py:18
  80.0 0.1 pad_maximum_fusion.3
  80.1 0.5 copy-done.8
  80.7 0.4 fusion.6
  81.1 0.4 copy.21
  81.5 3.0 %collective-permute-start.6 = (f32[2,16,80,4]{2,1,3,0:T(8,128)S(1)}, f32[2,16,80,4]{2,1,3,0:T(8,128)S(1)}, u32[]{:S(2)}, u32[]{:S(2)}) collective-permute-start(f32[2,16,80,4]{2,1,3,0:T(8,128)S(1)} %copy.21), channel_id=1, source_target_pairs={{1,0},{2,1},{3,2},{5,4},{6,5},{7,6},{9,8},{10,9},{11,10},{13,12},{... | collective-permute-start | bytes 122888 | tf_op jit(solution)/shard_map/ppermute | solution.py:23
  84.5 0.4 copy.22
  84.9 2.8 %collective-permute-start.7 = (f32[2,16,80,4]{2,1,3,0:T(8,128)S(1)}, f32[2,16,80,4]{2,1,3,0:T(8,128)S(1)}, u32[]{:S(2)}, u32[]{:S(2)}) collective-permute-start(f32[2,16,80,4]{2,1,3,0:T(8,128)S(1)} %copy.22), channel_id=1, source_target_pairs={{0,1},{1,2},{2,3},{4,5},{5,6},{6,7},{8,9},{9,10},{10,11},{12,13},{... | collective-permute-start | bytes 122888 | tf_op jit(solution)/shard_map/ppermute | solution.py:24
  87.8 0.5 copy.23
  88.2 0.7 collective-permute-done.7
  88.9 0.5 copy.24
  89.3 1.5 pad_maximum_fusion.4.e_ref
  90.8 16.3 %shard_map.65.x_ref = f32[2,16,64,128]{3,2,1,0:T(8,128)} custom-call(f32[2,16,64,128]{3,2,1,0:T(8,128)} %copy-done, f32[2,16,8,128]{3,2,1,0:T(8,128)} %copy-done.9, f32[2,16,8,128]{3,2,1,0:T(8,128)} %copy-done.8, f32[2,16,80,128]{3,2,1,0:T(8,128)} %pad_maximum_fusion.4.e_ref, f32[2,16,64,128]{3,2,1,0:T(8,128)} %pad_maximum_fusion.ct_ref, ...), custom_call_target="tpu_custom_call" | custom-call | tf_op jit(solution)/shard_map/pallas_call | solution.py:72
  107.1 27.5 %shard_map.66 = f32[2,64,16,128]{3,2,1,0:T(8,128)} custom-call(f32[2,16,64,128]{3,2,1,0:T(8,128)} %shard_map.65.x_ref), custom_call_target="tpu_custom_call" | custom-call | tf_op jit(solution)/shard_map/pallas_call | solution.py:148
  134.6 2.5 %convolution_bitcast_fusion = f32[2,64,16,128]{3,1,2,0:T(8,128)S(1)} fusion(f32[2,64,16,128]{3,2,1,0:T(8,128)} %shard_map.66, f32[2,64,2,64,1]{3,2,1,0,4:T(2,128)S(1)} %bitcast.29), kind=kOutput, calls=%fused_computation.5 | convolution fusion | flops 402653184 | bytes 2162688 | tf_op jit(solution)/shard_map/abcd,cdij->abij/dot_general | solution.py:177
  137.1 1.6 copy.27.x_ref
  138.7 19.6 %shard_map.67 = f32[2,16,64,128]{3,2,1,0:T(8,128)} custom-call(f32[2,64,16,128]{3,2,1,0:T(8,128)} %copy.27.x_ref), custom_call_target="tpu_custom_call" | custom-call | tf_op jit(solution)/shard_map/pallas_call | solution.py:148
  158.4 2.4 %multiply_multiply_fusion = f32[2,16,64,128]{3,2,1,0:T(8,128)} fusion(f32[2,16,64,128]{3,2,1,0:T(8,128)} %shard_map.67, f32[2,16,64,128]{3,2,1,0:T(8,128)S(1)} %copy-done.2, f32[16,64,128]{2,1,0:T(8,128)S(1)} %convert_element_type.6), kind=kLoop, calls=%fused_computation.13 | loop fusion | flops 524288 | bytes 3670016 | tf_op jit(solution)/shard_map/mul | solution.py:198
  (29 shorter events, 0.2 us)
Async XLA Ops:
  0.0 1.4 copy-start.1
  4.4 9.1 %copy-start.3 = (s32[16,64,128]{2,1,0:T(8,128)S(1)}, s32[16,64,128]{2,1,0:T(8,128)}, u32[]{:S(2)}) copy-start(s32[16,64,128]{2,1,0:T(8,128)} %param.10) | copy-start | bytes 1572868
  4.4 9.1 %copy-start.4 = (f32[16,64,128]{2,1,0:T(8,128)S(1)}, f32[16,64,128]{2,1,0:T(8,128)}, u32[]{:S(2)}) copy-start(f32[16,64,128]{2,1,0:T(8,128)} %param.8) | copy-start | bytes 1572868
  4.4 9.1 %copy-start.5 = (f32[16,64,128]{2,1,0:T(8,128)S(1)}, f32[16,64,128]{2,1,0:T(8,128)}, u32[]{:S(2)}) copy-start(f32[16,64,128]{2,1,0:T(8,128)} %param.9) | copy-start | bytes 1572868
  4.4 37.1 %all-to-all-start = ((f32[2,16,64,128]{3,1,0,2:T(8,128)}), f32[2,16,64,128]{3,1,0,2:T(8,128)}, u32[]{:S(2)}, u32[]{:S(2)}) async-start(f32[2,16,64,128]{3,1,0,2:T(8,128)} %copy.18), calls=%async_computation | async-start | bytes 2097152 | tf_op jit(solution)/shard_map/all_to_all | solution.py:166
  13.8 5.1 %copy-start.10 = (f32[128,128]{1,0:T(8,128)S(1)}, f32[128,128]{1,0:T(8,128)}, u32[]{:S(2)}) copy-start(f32[128,128]{1,0:T(8,128)} %param.11) | copy-start | bytes 196612
  13.8 7.8 %collective-permute-start.1 = (f32[2,16,8,128]{3,2,1,0:T(8,128)S(1)}, f32[2,16,8,128]{3,2,1,0:T(8,128)S(1)}, u32[]{:S(2)}, u32[]{:S(2)}) collective-permute-start(f32[2,16,8,128]{3,2,1,0:T(8,128)S(1)} %get-tuple-element.21), channel_id=1, source_target_pairs={{0,4},{4,8},{8,12},{12,16},{16,20},{20,24},{24,28},{28,32},{32,36}... | collective-permute-start | bytes 393224 | tf_op jit(solution)/shard_map/ppermute | solution.py:18
  15.2 6.4 %collective-permute-start = (f32[2,16,8,128]{3,2,1,0:T(8,128)S(1)}, f32[2,16,8,128]{3,2,1,0:T(8,128)S(1)}, u32[]{:S(2)}, u32[]{:S(2)}) collective-permute-start(f32[2,16,8,128]{3,2,1,0:T(8,128)S(1)} %get-tuple-element.22), channel_id=1, source_target_pairs={{4,0},{8,4},{12,8},{16,12},{20,16},{24,20},{28,24},{32,28},{36,32}... | collective-permute-start | bytes 393224 | tf_op jit(solution)/shard_map/ppermute | solution.py:19
  21.6 1.6 copy-start.6
  21.6 1.6 copy-start.7
  25.3 14.2 %collective-permute-start.3 = (f32[2,16,80,4]{2,1,3,0:T(8,128)S(1)}, f32[2,16,80,4]{2,1,3,0:T(8,128)S(1)}, u32[]{:S(2)}, u32[]{:S(2)}) collective-permute-start(f32[2,16,80,4]{2,1,3,0:T(8,128)S(1)} %copy.14), channel_id=1, source_target_pairs={{0,1},{1,2},{2,3},{4,5},{5,6},{6,7},{8,9},{9,10},{10,11},{12,13},{... | collective-permute-start | bytes 122888 | tf_op jit(solution)/shard_map/ppermute | solution.py:24
  29.6 9.5 %collective-permute-start.2 = (f32[2,16,80,4]{2,1,3,0:T(8,128)S(1)}, f32[2,16,80,4]{2,1,3,0:T(8,128)S(1)}, u32[]{:S(2)}, u32[]{:S(2)}) collective-permute-start(f32[2,16,80,4]{2,1,3,0:T(8,128)S(1)} %copy.13), channel_id=1, source_target_pairs={{1,0},{2,1},{3,2},{5,4},{6,5},{7,6},{9,8},{10,9},{11,10},{13,12},{... | collective-permute-start | bytes 122888 | tf_op jit(solution)/shard_map/ppermute | solution.py:23
  71.5 8.6 %copy-start = (f32[2,16,64,128]{3,2,1,0:T(8,128)}, f32[2,16,64,128]{3,2,1,0:T(8,128)S(1)}, u32[]{:S(2)}) copy-start(f32[2,16,64,128]{3,2,1,0:T(8,128)S(1)} %broadcast_multiply_fusion.x_ref) | copy-start | bytes 3145732
  71.6 8.4 %collective-permute-start.5 = (f32[2,16,8,128]{3,2,1,0:T(8,128)S(1)}, f32[2,16,8,128]{3,2,1,0:T(8,128)S(1)}, u32[]{:S(2)}, u32[]{:S(2)}) collective-permute-start(f32[2,16,8,128]{3,2,1,0:T(8,128)S(1)} %get-tuple-element.19), channel_id=1, source_target_pairs={{0,4},{4,8},{8,12},{12,16},{16,20},{20,24},{24,28},{28,32},{32,36}... | collective-permute-start | bytes 393224 | tf_op jit(solution)/shard_map/ppermute | solution.py:18
  72.9 7.0 %collective-permute-start.4 = (f32[2,16,8,128]{3,2,1,0:T(8,128)S(1)}, f32[2,16,8,128]{3,2,1,0:T(8,128)S(1)}, u32[]{:S(2)}, u32[]{:S(2)}) collective-permute-start(f32[2,16,8,128]{3,2,1,0:T(8,128)S(1)} %get-tuple-element.20), channel_id=1, source_target_pairs={{4,0},{8,4},{12,8},{16,12},{20,16},{24,20},{28,24},{32,28},{36,32}... | collective-permute-start | bytes 393224 | tf_op jit(solution)/shard_map/ppermute | solution.py:19
  79.9 0.7 copy-start.8
  80.0 0.7 copy-start.9
  81.5 6.2 %collective-permute-start.6 = (f32[2,16,80,4]{2,1,3,0:T(8,128)S(1)}, f32[2,16,80,4]{2,1,3,0:T(8,128)S(1)}, u32[]{:S(2)}, u32[]{:S(2)}) collective-permute-start(f32[2,16,80,4]{2,1,3,0:T(8,128)S(1)} %copy.21), channel_id=1, source_target_pairs={{1,0},{2,1},{3,2},{5,4},{6,5},{7,6},{9,8},{10,9},{11,10},{13,12},{... | collective-permute-start | bytes 122888 | tf_op jit(solution)/shard_map/ppermute | solution.py:23
  84.9 3.9 %collective-permute-start.7 = (f32[2,16,80,4]{2,1,3,0:T(8,128)S(1)}, f32[2,16,80,4]{2,1,3,0:T(8,128)S(1)}, u32[]{:S(2)}, u32[]{:S(2)}) collective-permute-start(f32[2,16,80,4]{2,1,3,0:T(8,128)S(1)} %copy.22), channel_id=1, source_target_pairs={{0,1},{1,2},{2,3},{4,5},{5,6},{6,7},{8,9},{9,10},{10,11},{12,13},{... | collective-permute-start | bytes 122888 | tf_op jit(solution)/shard_map/ppermute | solution.py:24
  138.7 19.6 %copy-start.2 = (f32[2,16,64,128]{3,2,1,0:T(8,128)S(1)}, f32[2,16,64,128]{3,2,1,0:T(8,128)}, u32[]{:S(2)}) copy-start(f32[2,16,64,128]{3,2,1,0:T(8,128)} %param.7) | copy-start | bytes 3145732

commit v15 on v14

--- a/solution.py
+++ b/solution.py
@@ -32,21 +32,21 @@
     return jnp.concatenate([tall, edge], 3)
 
 
-def plane(t_ref, s_ref, n_ref, e_ref, f):
-    tall = jnp.concatenate([t_ref[f, 0], s_ref[f, 0], n_ref[f, 0]], 0)
+def plane(center, s_ref, n_ref, e_ref, f):
+    tall = jnp.concatenate([center, s_ref[f, 0], n_ref[f, 0]], 0)
     return jnp.concatenate([tall, e_ref[f, 0]], 1)
 
 
-def diffusion_kernel(steps, rows, cols, x_ref, s_ref, n_ref, e_ref, ct_ref, cs_ref, cn_ref, ce_ref, o_ref):
+def diffusion_kernel(steps, rows, cols, x_ref, ct_ref, s_ref, n_ref, e_ref, o_ref):
     height, span = e_ref.shape[2], 2 * e_ref.shape[3]
     fields = o_ref.shape[0]
-    along_i = plane(ct_ref, cs_ref, cn_ref, ce_ref, 0)
-    along_j = plane(ct_ref, cs_ref, cn_ref, ce_ref, 1)
+    along_i = plane(ct_ref[0, 0], s_ref, n_ref, e_ref, fields)
+    along_j = plane(ct_ref[1, 0], s_ref, n_ref, e_ref, fields + 1)
     sea = (along_i > 0).astype(along_i.dtype)
     weight_i = along_i * pltpu.roll(sea, height - 1, 0)
     weight_j = along_j * pltpu.roll(sea, span - 1, 1)
     for f in range(fields):
-        values = plane(x_ref, s_ref, n_ref, e_ref, f)
+        values = plane(x_ref[f, 0], s_ref, n_ref, e_ref, f)
         for s in range(steps):
             flux_i = weight_i * (pltpu.roll(values, height - 1, 0) - values)
             flux_j = weight_j * (pltpu.roll(values, span - 1, 1) - values)
@@ -58,24 +58,21 @@
     fields, levels, rows, cols = values.shape
     height = rows + 4 * steps
     band = 2 * steps
-
-    def specs(channels):
-        return [
-            pl.BlockSpec((channels, 1, rows, cols), lambda l: (0, l, 0, 0)),
-            pl.BlockSpec((channels, 1, band, cols), lambda l: (0, l, 0, 0)),
-            pl.BlockSpec((channels, 1, band, cols), lambda l: (0, l, 0, 0)),
-            pl.BlockSpec((channels, 1, height, 128), lambda l: (0, l, 0, 0)),
-        ]
-
-    _, south, north, edge = pieces(values, band, steps)
-    _, coef_south, coef_north, coef_edge = coefs
+    channels = fields + coefs.shape[0]
+    _, south, north, edge = pieces(jnp.concatenate([values, coefs]), band, steps)
     return pl.pallas_call(
         functools.partial(diffusion_kernel, steps, rows, cols),
         out_shape=jax.ShapeDtypeStruct(values.shape, values.dtype),
         grid=(levels,),
-        in_specs=specs(fields) + specs(coef_edge.shape[0]),
+        in_specs=[
+            pl.BlockSpec((fields, 1, rows, cols), lambda l: (0, l, 0, 0)),
+            pl.BlockSpec((coefs.shape[0], 1, rows, cols), lambda l: (0, l, 0, 0)),
+            pl.BlockSpec((channels, 1, band, cols), lambda l: (0, l, 0, 0)),
+            pl.BlockSpec((channels, 1, band, cols), lambda l: (0, l, 0, 0)),
+            pl.BlockSpec((channels, 1, height, 128), lambda l: (0, l, 0, 0)),
+        ],
         out_specs=pl.BlockSpec((fields, 1, rows, cols), lambda l: (0, l, 0, 0)),
-    )(values, south, north, edge, coefs[0], coef_south, coef_north, coef_edge)
+    )(values, coefs, south, north, edge)
 
 
 def lev_exchange(x, src_axis, dst_axis, half_axis, collective):
@@ -187,12 +184,8 @@
     balance = jnp.eye(order_count, dtype=jnp.float32) + coupling
     forward = balance.reshape(2, level_count, 2, level_count)
     adjoint = jnp.transpose(forward, (2, 3, 0, 1))
-    stacked = jnp.stack([diffusion_i * ocean, diffusion_j * ocean])
-    coefs = (stacked,) + pieces(stacked, 2 * steps, steps)[1:]
-    columns = to_columns(scaled, False)
-    mixed = jnp.einsum("abcd,cdij->abij", adjoint, columns, precision=lax.Precision.HIGHEST)
-    coefs, mixed = lax.optimization_barrier((coefs, mixed))
-    adjoint_mixed = to_levels(mixed) * ocean[None]
+    coefs = jnp.stack([diffusion_i * ocean, diffusion_j * ocean])
+    adjoint_mixed = level_mix(scaled, adjoint) * ocean[None]
     spread = diffusion(adjoint_mixed, coefs, steps)
     forward_mixed = level_mix(spread, forward)
     return ocean[None] * norm_gain * forward_mixed

time: 162 us -> 177 us (1.093)
  Pallas kernels: 88.1 us -> 118 us
  starting transfers between devices: 31.3 us -> 14.9 us
  waiting for transfers between devices: 12.8 us -> 8.81 us
  other arithmetic: 10.8 us -> 14.3 us
    pallas_call x3 -> x4, Pallas kernels: 71.8 us -> 102 us  [lev_exchange(): pl.pallas_call(kernel, out_shape=jax.ShapeDtypeStruct(tuple(out_shape), x...]
    all_to_all x1 -> x0, starting transfers between devices: 9.14 us -> none  [to_columns(): return lax.all_to_all(x, 'lev', 2, 1, tiled=True)]
    ppermute x2 -> x1, waiting for transfers between devices: 6.2 us -> 0.01 us  [pieces(): east = lax.ppermute(tall[..., :width], 'gy', left)]
    ppermute x2 -> x1, waiting for transfers between devices: 0.01 us -> 3.56 us  [pieces(): south = lax.ppermute(x[:, :, :height], 'gx', down)]
    ppermute x2 -> x1, starting transfers between devices: 2.75 us -> 0.01 us  [pieces(): north = lax.ppermute(x[:, :, rows - height:], 'gx', up)]
    ppermute x2 -> x1, starting transfers between devices: 7.45 us -> 4.93 us  [pieces(): south = lax.ppermute(x[:, :, :height], 'gx', down)]
    dot_general x1 -> x2, matrix products: 2.51 us -> 5.01 us  [level_mix(): jnp.einsum('abcd,cdij->abij', matrix, columns, precision=lax.Precision.HI...]
    ppermute x2 -> x1, local copies, waits for them, and re-layouts: 0.9 us -> 3.24 us  [pieces(): west = lax.ppermute(tall[..., cols - width:], 'gy', right)]
  transfers between devices with their start and end apart: 9 -> 4, of which waited for: 4 -> 2; matrix products, arithmetic and copies ran while one was open for 5% -> 3% of each run, Pallas kernels for 0% -> 0%
where the time goes in v15:
time: 177 us; the launch traced here: 176 us
  Pallas kernels  118 us (67%)
  starting transfers between devices  14.9 us (8%)
  local copies, waits for them, and re-layouts  14.7 us (8%)
  other arithmetic  14.3 us (8%)
  waiting for transfers between devices  8.81 us (5%)
  matrix products  5.01 us (3%)
    pallas_call x4, Pallas kernels, lev_exchange(): pl.pallas_call(kernel, out_shape=jax.ShapeDtypeStruct(tuple(out_shape), x...  102 us
    pallas_call x1, Pallas kernels, diffusion(): pl.pallas_call(functools.partial(diffusion_kernel, steps, rows, cols), ou...  15.9 us
    ppermute x1, waiting for transfers between devices, pieces(): north = lax.ppermute(x[:, :, rows - height:], 'gx', up)  5.24 us
    ppermute x1, starting transfers between devices, pieces(): east = lax.ppermute(tall[..., :width], 'gy', left)  5.07 us
    dot_general x2, matrix products, level_mix(): jnp.einsum('abcd,cdij->abij', matrix, columns, precision=lax.Precision.HI...  5.01 us
    ppermute x1, starting transfers between devices, pieces(): south = lax.ppermute(x[:, :, :height], 'gx', down)  4.93 us
    slice x2, local copies, waits for them, and re-layouts, pieces(): east = lax.ppermute(tall[..., :width], 'gy', left)  4.93 us
    ppermute x1, starting transfers between devices, pieces(): west = lax.ppermute(tall[..., cols - width:], 'gy', right)  4.91 us
  transfers between devices with their start and end apart: 4, of which 2 were waited for; matrix products, arithmetic and copies ran while one was open for 3% of the time, Pallas kernels for 0%

profile of v15, /device:TPU:1, one launch (start us, length us, event | category | flops | bytes accessed | tf_op | source)
XLA Modules:
  0.0 176.1 jit_solution(6044426923189951751)
XLA Ops:
  0.0 1.1 convert_element_type.6
  1.1 0.0 copy-start.9
  1.1 2.8 %multiply_multiply_fusion.1.x_ref = f32[2,16,64,128]{3,2,1,0:T(8,128)} fusion(f32[2,16,64,128]{3,2,1,0:T(8,128)} %param.6, f32[2,16,64,128]{3,2,1,0:T(8,128)} %param.7, f32[16,64,128]{2,1,0:T(8,128)S(1)} %convert_element_type.6), kind=kLoop, calls=%fused_computation.10 | loop fusion | flops 524288 | bytes 3670016 | tf_op jit(solution)/shard_map/mul | solution.py:181
  3.9 31.6 %shard_map.64 = f32[2,64,16,128]{3,2,1,0:T(8,128)} custom-call(f32[2,16,64,128]{3,2,1,0:T(8,128)} %multiply_multiply_fusion.1.x_ref), custom_call_target="tpu_custom_call" | custom-call | tf_op jit(solution)/shard_map/pallas_call | solution.py:145
  35.5 0.0 copy-done.9
  35.5 0.1 reshape.4
  35.7 0.1 copy.13
  35.8 2.5 %convolution_bitcast_fusion.1 = f32[2,64,16,128]{3,1,2,0:T(8,128)S(1)} fusion(f32[2,64,16,128]{3,2,1,0:T(8,128)} %shard_map.64, f32[2,64,2,64]{1,3,0,2:T(8,128)S(1)} %copy.13), kind=kOutput, calls=%fused_computation.3 | convolution fusion | flops 402653184 | bytes 2162688 | tf_op jit(solution)/shard_map/abcd,cdij->abij/dot_general | solution.py:174
  38.3 1.6 copy.15.x_ref
  39.9 24.5 %shard_map.65 = f32[2,16,64,128]{3,2,1,0:T(8,128)} custom-call(f32[2,64,16,128]{3,2,1,0:T(8,128)} %copy.15.x_ref), custom_call_target="tpu_custom_call" | custom-call | tf_op jit(solution)/shard_map/pallas_call | solution.py:145
  64.4 1.3 broadcast_multiply_fusion.x_ref
  65.7 0.0 copy-done.4
  65.7 0.0 copy-done.7
  65.7 0.0 copy-done.8
  65.7 0.0 copy-start
  65.8 0.1 multiply_bitcast_fusion.1
  65.9 0.0 copy-start.1
  65.9 0.0 copy-start.2
  65.9 4.9 %collective-permute-start = (f32[4,16,8,128]{3,2,1,0:T(8,128)S(1)}, f32[4,16,8,128]{3,2,1,0:T(8,128)S(1)}, u32[]{:S(2)}, u32[]{:S(2)}) collective-permute-start(f32[4,16,8,128]{3,2,1,0:T(8,128)S(1)} %get-tuple-element.8), channel_id=1, source_target_pairs={{4,0},{8,4},{12,8},{16,12},{20,16},{24,20},{28,24},{32,28},{36,32}... | collective-permute-start | bytes 786440 | tf_op jit(solution)/shard_map/ppermute | solution.py:19
  70.9 0.0 collective-permute-start.1
  70.9 0.1 pad.1.clone
  71.0 3.6 %collective-permute-done.s_ref = f32[4,16,8,128]{3,2,1,0:T(8,128)S(1)} collective-permute-done((f32[4,16,8,128]{3,2,1,0:T(8,128)S(1)}, f32[4,16,8,128]{3,2,1,0:T(8,128)S(1)}, u32[]{:S(2)}, u32[]{:S(2)}) %collective-permute-start) | collective-permute-done | bytes 262176 | tf_op jit(solution)/shard_map/ppermute | solution.py:19
  74.5 5.2 %collective-permute-done.1.n_ref = f32[4,16,8,128]{3,2,1,0:T(8,128)S(1)} collective-permute-done((f32[4,16,8,128]{3,2,1,0:T(8,128)S(1)}, f32[4,16,8,128]{3,2,1,0:T(8,128)S(1)}, u32[]{:S(2)}, u32[]{:S(2)}) %collective-permute-start.1) | collective-permute-done | bytes 262176 | tf_op jit(solution)/shard_map/ppermute | solution.py:18
  79.8 0.0 copy-done
  79.8 0.0 copy-done.1
  79.8 0.0 copy-done.2
  79.8 0.0 copy-start.6
  79.8 0.7 copy-done.6
  80.5 0.2 pad_maximum_fusion
  80.7 2.4 %fusion.6 = (f32[4,16,80,4]{3,2,1,0:T(8,128)}, f32[4,16,80,4]{3,2,1,0:T(8,128)S(1)}) fusion(f32[4,16,80,128]{3,2,1,0:T(8,128)S(1)} %pad_maximum_fusion), kind=kLoop, calls=%fused_computation.21 | loop fusion | bytes 327680 | tf_op jit(solution)/shard_map/slice | solution.py:23
  83.1 0.0 copy-done.5
  83.1 2.5 %copy.16 = f32[4,16,80,4]{2,1,3,0:T(8,128)S(1)} copy(f32[4,16,80,4]{3,2,1,0:T(8,128)} %get-tuple-element.5) | data formatting | bytes 163840 | tf_op jit(solution)/shard_map/slice | solution.py:23
  85.7 5.1 %collective-permute-start.2 = (f32[4,16,80,4]{2,1,3,0:T(8,128)S(1)}, f32[4,16,80,4]{2,1,3,0:T(8,128)S(1)}, u32[]{:S(2)}, u32[]{:S(2)}) collective-permute-start(f32[4,16,80,4]{2,1,3,0:T(8,128)S(1)} %copy.16), channel_id=1, source_target_pairs={{1,0},{2,1},{3,2},{5,4},{6,5},{7,6},{9,8},{10,9},{11,10},{13,12},{... | collective-permute-start | bytes 245768 | tf_op jit(solution)/shard_map/ppermute | solution.py:23
  90.7 1.5 copy.17
  92.2 4.9 %collective-permute-start.3 = (f32[4,16,80,4]{2,1,3,0:T(8,128)}, f32[4,16,80,4]{2,1,3,0:T(8,128)}, u32[]{:S(2)}, u32[]{:S(2)}) collective-permute-start(f32[4,16,80,4]{2,1,3,0:T(8,128)} %copy.17), channel_id=1, source_target_pairs={{0,1},{1,2},{2,3},{4,5},{5,6},{6,7},{8,9},{9,10},{10,11},{12,13},{... | collective-permute-start | bytes 245768 | tf_op jit(solution)/shard_map/ppermute | solution.py:24
  97.1 2.3 %pad_maximum_fusion.2.ct_ref = f32[2,16,64,128]{3,2,1,0:T(8,128)} fusion(f32[1,16,64,128]{3,2,1,0:T(8,128)} %copy-done.2, f32[1,16,64,128]{3,2,1,0:T(8,128)} %copy-done.1), kind=kLoop, calls=%fused_computation.4 | loop fusion | flops 262144 | bytes 2097152 | tf_op jit(solution)/shard_map/stack | solution.py:187
  99.4 0.0 collective-permute-done.2
  99.5 0.8 copy.18
  100.3 0.0 collective-permute-done.3
  100.3 3.2 %copy.19 = f32[4,16,80,4]{3,2,1,0:T(8,128)} copy(f32[4,16,80,4]{2,1,3,0:T(8,128)} %collective-permute-done.3) | data formatting | bytes 163840 | tf_op jit(solution)/shard_map/ppermute | solution.py:24
  103.5 4.0 %pad_maximum_fusion.1.e_ref = f32[4,16,80,128]{3,2,1,0:T(8,128)} fusion(f32[4,16,80,4]{3,2,1,0:T(8,128)} %copy.19, f32[4,16,80,4]{3,2,1,0:T(8,128)S(1)} %copy.18, f32[128]{0:T(128)S(1)} %pad.1.clone), kind=kLoop, calls=%fused_computation.1 | loop fusion | flops 1310720 | bytes 2785792 | tf_op jit(solution)/shard_map/concatenate | solution.py:26
  107.5 15.9 %shard_map.66.x_ref = f32[2,16,64,128]{3,2,1,0:T(8,128)} custom-call(f32[2,16,64,128]{3,2,1,0:T(8,128)} %copy-done, f32[2,16,64,128]{3,2,1,0:T(8,128)} %pad_maximum_fusion.2.ct_ref, f32[4,16,8,128]{3,2,1,0:T(8,128)} %copy-done.5, f32[4,16,8,128]{3,2,1,0:T(8,128)} %copy-done.6, f32[4,16,80,128]{3,2,1,0:T(8,128)} %pad_maximum_fusion.1.e_ref), custom_call_target="tpu_custom_call" | custom-call | tf_op jit(solution)/shard_map/pallas_call | solution.py:63
  123.4 26.2 %shard_map.67 = f32[2,64,16,128]{3,2,1,0:T(8,128)} custom-call(f32[2,16,64,128]{3,2,1,0:T(8,128)} %shard_map.66.x_ref), custom_call_target="tpu_custom_call" | custom-call | tf_op jit(solution)/shard_map/pallas_call | solution.py:145
  149.7 2.5 %convolution_bitcast_fusion = f32[2,64,16,128]{3,1,2,0:T(8,128)S(1)} fusion(f32[2,64,16,128]{3,2,1,0:T(8,128)} %shard_map.67, f32[2,64,2,64,1]{3,2,1,0,4:T(2,128)S(1)} %bitcast.24), kind=kOutput, calls=%fused_computation.2 | convolution fusion | flops 402653184 | bytes 2162688 | tf_op jit(solution)/shard_map/abcd,cdij->abij/dot_general | solution.py:174
  152.2 0.0 copy-start.3
  152.2 1.6 copy.22.x_ref
  153.8 19.8 %shard_map.68 = f32[2,16,64,128]{3,2,1,0:T(8,128)} custom-call(f32[2,64,16,128]{3,2,1,0:T(8,128)} %copy.22.x_ref), custom_call_target="tpu_custom_call" | custom-call | tf_op jit(solution)/shard_map/pallas_call | solution.py:145
  173.6 2.4 %multiply_multiply_fusion = f32[2,16,64,128]{3,2,1,0:T(8,128)} fusion(f32[2,16,64,128]{3,2,1,0:T(8,128)} %shard_map.68, f32[2,16,64,128]{3,2,1,0:T(8,128)S(1)} %copy-done.3, f32[16,64,128]{2,1,0:T(8,128)S(1)} %convert_element_type.6), kind=kLoop, calls=%fused_computation.9 | loop fusion | flops 524288 | bytes 3670016 | tf_op jit(solution)/shard_map/mul | solution.py:191
  (8 shorter events, 0.1 us)
Async XLA Ops:
  1.1 34.4 %copy-start.9 = (f32[128,128]{1,0:T(8,128)S(1)}, f32[128,128]{1,0:T(8,128)}, u32[]{:S(2)}) copy-start(f32[128,128]{1,0:T(8,128)} %param.11) | copy-start | bytes 196612
  39.9 25.8 %copy-start.4 = (s32[16,64,128]{2,1,0:T(8,128)S(1)}, s32[16,64,128]{2,1,0:T(8,128)}, u32[]{:S(2)}) copy-start(s32[16,64,128]{2,1,0:T(8,128)} %param.10) | copy-start | bytes 1572868
  39.9 25.9 %copy-start.7 = (f32[16,64,128]{2,1,0:T(8,128)S(1)}, f32[16,64,128]{2,1,0:T(8,128)}, u32[]{:S(2)}) copy-start(f32[16,64,128]{2,1,0:T(8,128)} %param.8) | copy-start | bytes 1572868
  39.9 25.9 %copy-start.8 = (f32[16,64,128]{2,1,0:T(8,128)S(1)}, f32[16,64,128]{2,1,0:T(8,128)}, u32[]{:S(2)}) copy-start(f32[16,64,128]{2,1,0:T(8,128)} %param.9) | copy-start | bytes 1572868
  65.7 14.0 %copy-start = (f32[2,16,64,128]{3,2,1,0:T(8,128)}, f32[2,16,64,128]{3,2,1,0:T(8,128)S(1)}, u32[]{:S(2)}) copy-start(f32[2,16,64,128]{3,2,1,0:T(8,128)S(1)} %broadcast_multiply_fusion.x_ref) | copy-start | bytes 3145732
  65.9 13.9 %copy-start.1 = (f32[1,16,64,128]{3,2,1,0:T(8,128)}, f32[1,16,64,128]{3,2,1,0:T(8,128)S(1)}, u32[]{:S(2)}) copy-start(f32[1,16,64,128]{3,2,1,0:T(8,128)S(1)} %get-tuple-element.9) | copy-start | bytes 1572868
  65.9 13.9 %copy-start.2 = (f32[1,16,64,128]{3,2,1,0:T(8,128)}, f32[1,16,64,128]{3,2,1,0:T(8,128)S(1)}, u32[]{:S(2)}) copy-start(f32[1,16,64,128]{3,2,1,0:T(8,128)S(1)} %get-tuple-element.10) | copy-start | bytes 1572868
  65.9 8.6 %collective-permute-start = (f32[4,16,8,128]{3,2,1,0:T(8,128)S(1)}, f32[4,16,8,128]{3,2,1,0:T(8,128)S(1)}, u32[]{:S(2)}, u32[]{:S(2)}) collective-permute-start(f32[4,16,8,128]{3,2,1,0:T(8,128)S(1)} %get-tuple-element.8), channel_id=1, source_target_pairs={{4,0},{8,4},{12,8},{16,12},{20,16},{24,20},{28,24},{32,28},{36,32}... | collective-permute-start | bytes 786440 | tf_op jit(solution)/shard_map/ppermute | solution.py:19
  70.9 8.9 %collective-permute-start.1 = (f32[4,16,8,128]{3,2,1,0:T(8,128)S(1)}, f32[4,16,8,128]{3,2,1,0:T(8,128)S(1)}, u32[]{:S(2)}, u32[]{:S(2)}) collective-permute-start(f32[4,16,8,128]{3,2,1,0:T(8,128)S(1)} %get-tuple-element.7), channel_id=1, source_target_pairs={{0,4},{4,8},{8,12},{12,16},{16,20},{20,24},{24,28},{28,32},{32,36}... | collective-permute-start | bytes 786440 | tf_op jit(solution)/shard_map/ppermute | solution.py:18
  74.5 8.6 %copy-start.5 = (f32[4,16,8,128]{3,2,1,0:T(8,128)}, f32[4,16,8,128]{3,2,1,0:T(8,128)S(1)}, u32[]{:S(2)}) copy-start(f32[4,16,8,128]{3,2,1,0:T(8,128)S(1)} %collective-permute-done.s_ref) | copy-start | bytes 786436
  79.8 0.7 copy-start.6
  85.7 13.8 %collective-permute-start.2 = (f32[4,16,80,4]{2,1,3,0:T(8,128)S(1)}, f32[4,16,80,4]{2,1,3,0:T(8,128)S(1)}, u32[]{:S(2)}, u32[]{:S(2)}) collective-permute-start(f32[4,16,80,4]{2,1,3,0:T(8,128)S(1)} %copy.16), channel_id=1, source_target_pairs={{1,0},{2,1},{3,2},{5,4},{6,5},{7,6},{9,8},{10,9},{11,10},{13,12},{... | collective-permute-start | bytes 245768 | tf_op jit(solution)/shard_map/ppermute | solution.py:23
  92.2 8.1 %collective-permute-start.3 = (f32[4,16,80,4]{2,1,3,0:T(8,128)}, f32[4,16,80,4]{2,1,3,0:T(8,128)}, u32[]{:S(2)}, u32[]{:S(2)}) collective-permute-start(f32[4,16,80,4]{2,1,3,0:T(8,128)} %copy.17), channel_id=1, source_target_pairs={{0,1},{1,2},{2,3},{4,5},{5,6},{6,7},{8,9},{9,10},{10,11},{12,13},{... | collective-permute-start | bytes 245768 | tf_op jit(solution)/shard_map/ppermute | solution.py:24
  152.2 21.4 %copy-start.3 = (f32[2,16,64,128]{3,2,1,0:T(8,128)S(1)}, f32[2,16,64,128]{3,2,1,0:T(8,128)}, u32[]{:S(2)}) copy-start(f32[2,16,64,128]{3,2,1,0:T(8,128)} %param.7) | copy-start | bytes 3145732
